TPU v7x, 768 devices: a whole 4x8x12 slice. The times are simulated.
768 devices in a mesh: elem: 96 (over y, x, z_lo), state: 8 (over z_hi, core).
Axes of the slice: x: 4, y: 8, z: 12 (z_hi: 4, z_lo: 3; z = z_hi * 3 + z_lo), core: 2. Of those that a mesh axis runs over, the one named last changes fastest.
Arguments:
- cell_matrices: bfloat16 [384, 512, 512], P('elem'), may hold values from -0.25 to 0.25
- initial_states: bfloat16 [384, 512, 1024], P('elem', None, 'state'), may hold values from -6 to 6
- face_map: int32 [384, 64], P('elem'), may hold values from 0 to 63, each once within a row
Outputs:
- filtered_states: bfloat16 [384, 512, 1024], P('elem', None, 'state')
- projected_hamiltonian: float32 [1024, 1024], P('state')
- projected_intersection: float32 [1024, 1024], P('state')
Inputs may be any that keep to these rules, and one draw needn't show every extreme that they name: Each row of face_map is a permutation of 0 to 63.
All inputs are finite; a program needn't handle non-finite values.
Results may differ from a plain program's by a relative error of at most 0.013.
Values may be sent and summed in bfloat16 or wider, within the bound.
No kernel may reach another device: no remote copies, remote signals or barrier semaphores. Data moves between devices by JAX's collectives and lax.ppermute only.
A program may use at most 32 MiB of HBM per device.

v0:
```python
import jax
import jax.numpy as jnp
from jax import lax
from jax.sharding import PartitionSpec as P

PASSES = 4


filter_width = 2.5


def extended(cells, sides, width):
    for axis, dim in sides:
        count = lax.axis_size(axis)
        ends = count - 1
        head = lax.slice_in_dim(cells, 0, width, axis=dim)
        tail = lax.slice_in_dim(cells, cells.shape[dim] - width, cells.shape[dim], axis=dim)
        cells = jnp.concatenate(
            [
                lax.ppermute(tail, axis, [(i, (i + 1) % count) for i in range(ends)]),
                cells,
                lax.ppermute(head, axis, [((i + 1) % count, i) for i in range(ends)]),
            ],
            axis=dim,
        )
    return cells


def apply_operator(cell_matrices, values, onehot):
    face = onehot.shape[1]
    products = jnp.einsum("cij,cjo->cio", cell_matrices, values, preferred_element_type=jnp.float32)
    lower_face = products[:, :face]
    upper_face = products[:, -face:]
    middle = products[:, face:-face]
    to_next = jnp.einsum("cfm,cfo->cmo", onehot, upper_face, precision=lax.Precision.HIGHEST)
    rim_faces = jnp.stack([lower_face[0], to_next[-1]])
    haloed = extended(rim_faces, (("elem", 0),), 1)
    lower_next = jnp.concatenate([lower_face[1:], haloed[3:4]], 0)
    from_next = jnp.einsum("cfm,cmo->cfo", onehot, lower_next, precision=lax.Precision.HIGHEST)
    from_low = jnp.concatenate([haloed[0:1], to_next[:-1]], 0)
    return jnp.concatenate([lower_face + from_low, middle, upper_face + from_next], 1)


def local(cell_matrices, initial_states, face_map):
    face = face_map.shape[1]
    cells_dev = cell_matrices.shape[0]
    nodes = cell_matrices.shape[1]
    orb_dev = initial_states.shape[2]
    onehot = (face_map[:, :, None] == jnp.arange(face, dtype=jnp.int32)[None, None, :]).astype(
        jnp.float32
    )
    previous = initial_states.astype(jnp.float32)
    current = previous
    current_b = initial_states
    for degree in range(PASSES):
        image = apply_operator(cell_matrices, current_b, onehot)
        if degree == 0:
            following = image / filter_width
        else:
            following = 2.0 / filter_width * image - previous
        previous = current
        current = following
        current_b = following.astype(jnp.bfloat16)
    image_b = apply_operator(cell_matrices, current_b, onehot).astype(jnp.bfloat16)
    cells_total = cells_dev * lax.axis_size("elem")
    cell_index = lax.axis_index("elem") * cells_dev + jnp.arange(cells_dev, dtype=jnp.int32)
    has_next = cell_index < cells_total - 1
    on_upper = jnp.arange(nodes, dtype=jnp.int32) >= nodes - face
    dropped = has_next[:, None] & on_upper[None, :]
    weighted = jnp.where(dropped[:, :, None], jnp.zeros((), jnp.bfloat16), current_b)
    own_rows = weighted.reshape(cells_dev * nodes, orb_dev)
    stacked = jnp.stack([own_rows, image_b.reshape(cells_dev * nodes, orb_dev)])
    exchanged = lax.all_to_all(stacked, "state", split_axis=1, concat_axis=2, tiled=True)
    left_rows = exchanged[0]
    block = lax.psum_scatter(
        jnp.einsum("ni,knj->ikj", left_rows, exchanged, preferred_element_type=jnp.float32).astype(
            jnp.bfloat16
        ),
        "state",
        scatter_dimension=0,
        tiled=True,
    ).astype(jnp.float32)
    totals = lax.psum(block, "elem")
    inv_points = 1.0 / (cells_total * nodes)
    intersection = totals[:, 0] * inv_points
    hamiltonian = totals[:, 1] * inv_points
    return (current_b, hamiltonian, intersection)


def solution(mesh):
    return jax.shard_map(
        local,
        mesh=mesh,
        in_specs=(P("elem", None, None), P("elem", None, "state"), P("elem", None)),
        out_specs=(P("elem", None, "state"), P("state", None), P("state", None)),
        check_vma=False,
    )
```

profile of v0, /device:TPU:192, one launch (start us, length us, event | category | flops | bytes accessed | tf_op | source)
XLA Modules:
  0.0 824.6 jit_solution(17758113593402069790)
XLA Ops:
  7.2 1.5 copy-done
  8.8 1.7 fusion.65
  10.5 1.3 collective-permute-start.1
  11.8 0.4 fusion.37
  12.2 6.1 collective-permute-start
  18.4 0.1 broadcast_and_fusion
  18.5 0.3 convolution_add_fusion.4
  18.8 1.1 collective-permute-done
  19.9 0.7 convolution_bitcast_fusion.2
  20.7 1.4 collective-permute-start.3
  22.1 0.4 fusion.36
  22.6 6.1 collective-permute-start.2
  28.6 0.3 convolution_add_fusion.3
  28.9 1.3 collective-permute-done.2
  30.2 0.7 convolution_bitcast_fusion.1
  31.0 1.3 collective-permute-start.5
  32.3 0.4 fusion.35
  32.7 0.1 slice.182
  32.7 6.4 collective-permute-start.4
  39.2 0.3 convolution_add_fusion.2
  39.4 1.3 collective-permute-done.4
  40.7 0.7 convolution_bitcast_fusion
  41.5 1.3 collective-permute-start.7
  42.8 0.4 fusion.34
  43.2 7.9 collective-permute-start.6
  51.1 0.3 convolution_add_fusion.1
  51.4 1.3 collective-permute-done.6
  52.7 0.5 broadcast_select_fusion
  53.2 0.8 convolution_bitcast_fusion.3
  54.1 1.3 collective-permute-start.9
  55.4 0.4 fusion.20
  55.9 0.2 slice.231
  56.1 8.0 collective-permute-start.8
  64.2 0.3 fusion
  64.5 1.5 collective-permute-done.8
  66.1 0.3 pad_maximum_fusion.1
  66.4 1.0 copy.62
  67.4 1.1 pad_maximum_fusion
  68.5 8.7 %copy.63 = bf16[2,2048,128]{2,0,1:T(2,128)(2,1)S(1)} copy(bf16[2,2048,128]{2,1,0:T(8,128)(2,1)S(1)} %pad_maximum_fusion) | data formatting | bytes 2097152 | tf_op jit(solution)/shard_map/stack | solution.py:72
  77.2 47.2 %all_to_all.18 = bf16[2,2048,128]{2,0,1:T(2,128)(2,1)S(1)} all-to-all(bf16[2,2048,128]{2,0,1:T(2,128)(2,1)S(1)} %copy.63), channel_id=1, replica_groups=mesh['elem'=96,'state'=8] {'state'}, dimensions={1} | all-to-all | bytes 2097152 | tf_op jit(solution)/shard_map/all_to_all | solution.py:73
  124.5 0.7 copy.83
  125.2 0.8 slice.199
  126.0 1.3 all_to_all.16
  127.2 1.3 copy.65
  128.6 4.4 convolution_convert_fusion
  133.0 102.8 %reduce-scatter.2.cloned.1.call-done = bf16[128,2,1024]{2,0,1:T(8,128)(2,1)} async-done(((bf16[1024,2,1024]{2,0,1:T(8,128)(2,1)}), bf16[128,2,1024]{2,0,1:T(8,128)(2,1)}) %reduce-scatter.2.cloned.1.call-update) | async-done | bytes 524304 | tf_op jit(solution)/shard_map/reduce_scatter | solution.py:75
  235.8 581.0 %all-reduce.1 = f32[128,2,1024]{2,0,1:T(8,128)S(1)} all-reduce(bf16[128,2,1024]{2,0,1:T(8,128)(2,1)} %reduce-scatter.2.cloned.1.call-done), channel_id=1, replica_groups=mesh['elem'=96,'state'=8] {'elem'}, use_global_device_ids=true, to_apply=%region_1.2 | all-reduce | flops 262144 | bytes 1572864 | tf_op jit(solution)/shard_map/psum | solution.py:83
  816.7 1.1 fusion.9
  (44 shorter events, 0.5 us)
Async XLA Ops:
  7.2 1.6 copy-start
  7.2 4.6 copy-start.3
  7.2 228.6 %reduce-scatter.2.cloned.1.call-start = ((), (), s32[]{:S(2)}) async-start(), calls=%async_computation.2 | async-start | bytes 4718592 | tf_op jit(solution)/shard_map/reduce_scatter | solution.py:75
  10.5 8.0 collective-permute-start.1
  12.2 7.7 collective-permute-start
  20.6 9.6 %copy-start.1 = (bf16[4,512,128]{2,1,0:T(8,128)(2,1)S(1)}, bf16[4,512,128]{2,1,0:T(8,128)(2,1)}, u32[]{:S(2)}) copy-start(bf16[4,512,128]{2,1,0:T(8,128)(2,1)} %param.4) | copy-start | bytes 1572868
  20.7 8.0 collective-permute-start.3
  22.6 7.6 collective-permute-start.2
  31.0 8.2 collective-permute-start.5
  32.7 8.0 collective-permute-start.4
  41.5 9.6 %collective-permute-start.7 = (f32[1,64,128]{2,1,0:T(8,128)S(1)}, f32[1,64,128]{2,1,0:T(8,128)S(1)}, u32[]{:S(2)}, u32[]{:S(2)}) collective-permute-start(f32[1,64,128]{2,1,0:T(8,128)S(1)} %slice.191), channel_id=1, source_target_pairs={{8,0},{16,8},{24,16},{32,24},{40,32},{48,40},{56,48},{64,56},{72,6... | collective-permute-start | bytes 98312 | tf_op jit(solution)/shard_map/ppermute | solution.py:22
  43.2 9.4 %collective-permute-start.6 = (f32[1,64,128]{2,1,0:T(8,128)S(1)}, f32[1,64,128]{2,1,0:T(8,128)S(1)}, u32[]{:S(2)}, u32[]{:S(2)}) collective-permute-start(f32[1,64,128]{2,1,0:T(8,128)S(1)} %slice.187), channel_id=1, source_target_pairs={{0,8},{8,16},{16,24},{24,32},{32,40},{40,48},{48,56},{56,64},{64,7... | collective-permute-start | bytes 98312 | tf_op jit(solution)/shard_map/ppermute | solution.py:20
  53.2 2.6 copy-start.2
  54.1 10.0 %collective-permute-start.9 = (f32[1,64,128]{1,2,0:T(8,128)S(1)}, f32[1,64,128]{1,2,0:T(8,128)S(1)}, u32[]{:S(2)}, u32[]{:S(2)}) collective-permute-start(f32[1,64,128]{1,2,0:T(8,128)S(1)} %slice.198), channel_id=1, source_target_pairs={{8,0},{16,8},{24,16},{32,24},{40,32},{48,40},{56,48},{64,56},{72,6... | collective-permute-start | bytes 98312 | tf_op jit(solution)/shard_map/ppermute | solution.py:22
  56.1 9.9 %collective-permute-start.8 = (f32[1,64,128]{1,2,0:T(8,128)S(1)}, f32[1,64,128]{1,2,0:T(8,128)S(1)}, u32[]{:S(2)}, u32[]{:S(2)}) collective-permute-start(f32[1,64,128]{1,2,0:T(8,128)S(1)} %slice.194), channel_id=1, source_target_pairs={{0,8},{8,16},{16,24},{24,32},{32,40},{40,48},{48,56},{56,64},{64,7... | collective-permute-start | bytes 98312 | tf_op jit(solution)/shard_map/ppermute | solution.py:20
Sparse Core Ops, SparseCore 0:
  133.1 102.5 reduce-scatter.1
where the time goes:
time: 825 us
  blocking collectives  628 us (76%)
  waiting for transfers between devices  109 us (13%)
  starting transfers between devices  41.1 us (5%)
  local copies, waits for them, and re-layouts  15.9 us (2%)
  between operations  14.6 us (2%)
  matrix products  12.3 us (1%)
    psum x1, blocking collectives, local(): totals = lax.psum(block, 'elem')  581 us
    reduce_scatter x1, waiting for transfers between devices, local(): lax.psum_scatter(jnp.einsum('ni,knj->ikj', left_rows, exchanged, preferre...  103 us
    all_to_all x1, blocking collectives, local(): lax.all_to_all(stacked, 'state', split_axis=1, concat_axis=2, tiled=True)  47.2 us
    ppermute x5, starting transfers between devices, extended(): lax.ppermute(tail, axis, [(i, (i + 1) % count) for i in range(ends)])  34.5 us
  transfers between devices with their start and end apart: 11, of which 6 were waited for; matrix products, arithmetic and copies ran while one was open for 0% of the time, Pallas kernels for 0%

commit v1 on v0

v1 whole, which is shorter than its diff:
```python
import jax
import jax.numpy as jnp
from jax import lax
from jax.experimental import pallas as pl
from jax.experimental.pallas import tpu as pltpu
from jax.sharding import Mesh
from jax.sharding import PartitionSpec as P

PASSES = 4
ELEM = (("y", 8), ("x", 4), ("zl", 3))
STATE = (("zh", 4), ("core", 2))


filter_width = 2.5

f32 = jnp.float32
bf16 = jnp.bfloat16
elem = tuple(name for name, _ in ELEM)
state = tuple(name for name, _ in STATE)


def dot(a, b, dims=((1,), (0,))):
    return lax.dot_general(a, b, (dims, ((), ())), preferred_element_type=f32)


def shifted(faces, up):
    count = lax.axis_size(elem)
    pairs = [(i, i + 1) if up else (i + 1, i) for i in range(count - 1)]
    return lax.ppermute(faces, elem, pairs)


def reorder_kernel(perm_ref, perm_t_ref, k_ref, out_ref):
    face = perm_t_ref.shape[1]
    nodes = k_ref.shape[1]
    wide = perm_ref.shape[1]
    out_ref[0, :, : nodes - wide] = k_ref[0, :, : nodes - wide]
    out_ref[0, :, nodes - wide :] = dot(k_ref[0, :, nodes - wide :], perm_ref[0]).astype(bf16)
    out_ref[0, nodes - face :, :] = dot(perm_t_ref[0], out_ref[0, nodes - face :, :]).astype(bf16)


def reordered(cell_matrices, onehot):
    cells, nodes = cell_matrices.shape[:2]
    face = onehot.shape[1]
    wide = 2 * face
    eye = jnp.broadcast_to(jnp.eye(face, dtype=bf16), (cells, face, face))
    none = jnp.zeros((cells, face, face), bf16)
    perm = jnp.concatenate(
        [jnp.concatenate([eye, none], 2), jnp.concatenate([none, onehot], 2)], 1
    )
    perm_t = jnp.swapaxes(onehot, 1, 2)
    return pl.pallas_call(
        reorder_kernel,
        grid=(cells,),
        in_specs=[
            pl.BlockSpec((1, wide, wide), lambda c: (c, 0, 0)),
            pl.BlockSpec((1, face, face), lambda c: (c, 0, 0)),
            pl.BlockSpec((1, nodes, nodes), lambda c: (c, 0, 0)),
        ],
        out_specs=pl.BlockSpec((1, nodes, nodes), lambda c: (c, 0, 0)),
        out_shape=jax.ShapeDtypeStruct(cell_matrices.shape, bf16),
        name="reorder",
    )(perm, perm_t, cell_matrices)


def scatter_rows(part, out_ref, block):
    xs, ys, _, rows, cols = out_ref.shape
    for x in range(xs):
        for y in range(ys):
            out_ref[x, y, block] = part[x * rows : (x + 1) * rows, y * cols : (y + 1) * cols].astype(bf16)


def gram_own_kernel(where_ref, k_ref, rows_ref, out_ref, right_ref):
    blocks, total, orb = rows_ref.shape
    nodes = k_ref.shape[1]
    face = total - nodes
    inner = nodes - face
    is_last = where_ref[1] == 1
    for s in range(blocks):
        at = slice(s * orb, (s + 1) * orb)
        right_ref[:, at] = dot(k_ref[0], rows_ref[s, :nodes]).astype(bf16)
        at = slice((blocks + s) * orb, (blocks + s + 1) * orb)
        right_ref[:inner, at] = rows_ref[s, :inner]
        paired = rows_ref[s, nodes:]
        right_ref[inner:, at] = jnp.where(is_last, paired, jnp.zeros_like(paired))
    for s in range(blocks):
        part = dot(rows_ref[s, :inner], right_ref[:inner], ((0,), (0,)))
        part += dot(rows_ref[s, nodes:], right_ref[inner:], ((0,), (0,)))
        scatter_rows(part, out_ref, s)


def gram_other_kernel(rows_ref, right_ref, out_ref):
    blocks, total, _ = rows_ref.shape
    nodes = right_ref.shape[0]
    inner = 2 * nodes - total
    for s in range(blocks):
        part = dot(rows_ref[s, :inner], right_ref[:inner], ((0,), (0,)))
        part += dot(rows_ref[s, nodes:], right_ref[inner:], ((0,), (0,)))
        scatter_rows(part, out_ref, s)


def gram_shapes(blocks, orb):
    xs, ys = lax.axis_size("x"), lax.axis_size("y")
    return jax.ShapeDtypeStruct((xs, ys, blocks, orb // xs, 2 * blocks * orb // ys), bf16)


def gram_own(where, matrices, rows):
    blocks, total, orb = rows.shape
    nodes = matrices.shape[1]
    out = gram_shapes(blocks, orb)
    return pl.pallas_call(
        gram_own_kernel,
        grid_spec=pltpu.PrefetchScalarGridSpec(
            num_scalar_prefetch=1,
            grid=(1,),
            in_specs=[
                pl.BlockSpec((1, nodes, nodes), lambda i, w: (w[0], 0, 0)),
                pl.BlockSpec(rows.shape, lambda i, w: (0, 0, 0)),
            ],
            out_specs=[
                pl.BlockSpec(out.shape, lambda i, w: (0,) * 5),
                pl.BlockSpec((nodes, 2 * blocks * orb), lambda i, w: (0, 0)),
            ],
        ),
        out_shape=[out, jax.ShapeDtypeStruct((nodes, 2 * blocks * orb), bf16)],
        name="gram_own",
    )(where, matrices, rows)


def gram_other(rows, right):
    return pl.pallas_call(
        gram_other_kernel,
        out_shape=gram_shapes(rows.shape[0], rows.shape[2]),
        name="gram_other",
    )(rows, right)


def summed(parts):
    return jnp.sum(parts.astype(f32), 0).astype(bf16)


def swap_sum(part, axis):
    return summed(lax.all_to_all(part, axis, split_axis=0, concat_axis=0, tiled=True))


def local(cell_matrices, initial_states, face_map):
    face = face_map.shape[1]
    cells_dev, nodes = cell_matrices.shape[:2]
    orb_dev = initial_states.shape[2]
    elems = lax.axis_size(elem)
    zhs, cores, zls = lax.axis_size("zh"), lax.axis_size("core"), lax.axis_size("zl")
    xs, ys = lax.axis_size("x"), lax.axis_size("y")
    onehot = (face_map[:, :, None] == jnp.arange(face, dtype=jnp.int32)[None, None, :]).astype(bf16)
    matrices = reordered(cell_matrices, onehot)

    def to_next_order(faces):
        return jnp.einsum("cfm,cfo->cmo", onehot, faces, preferred_element_type=f32)

    def edges(values):
        return (
            dot(matrices[0, :face], values[0]),
            dot(matrices[-1, -face:], values[-1]),
        )

    start_upper = to_next_order(initial_states[:, -face:])
    current_b = jnp.concatenate([initial_states[:, :-face], start_upper.astype(bf16)], 1)
    start = current_b.astype(f32)
    previous = start
    current = start
    next_start = None
    for degree in range(PASSES):
        head, tail = edges(current_b)
        if degree == 0:
            both = shifted(jnp.stack([head, start[0, :face]]), False)
            from_above, next_start = both[0], both[1]
        else:
            from_above = shifted(head, False)
        from_below = shifted(tail, True)
        products = jnp.einsum("cij,cjo->cio", matrices, current_b, preferred_element_type=f32)
        from_next = jnp.concatenate([products[1:, :face], from_above[None]], 0)
        from_low = jnp.concatenate([from_below[None], products[:-1, -face:]], 0)
        image = jnp.concatenate(
            [
                products[:, :face] + from_low,
                products[:, face:-face],
                products[:, -face:] + from_next,
            ],
            1,
        )
        following = image / filter_width if degree == 0 else 2.0 / filter_width * image - previous
        previous = current
        current = following
        current_b = following.astype(bf16)

    place = lax.axis_index(elem) * cells_dev
    cell_index = place + jnp.arange(cells_dev, dtype=jnp.int32)
    is_last = cell_index == cells_dev * elems - 1
    step = start[:, -face:] - jnp.concatenate([start[1:, :face], next_start[None]], 0)
    step = jnp.where(is_last[:, None, None], 0.0, step)
    paired = (current[:, -face:] - step).astype(bf16)

    rows = jnp.concatenate([current_b, paired], 1)
    rows = lax.all_to_all(rows, "zh", split_axis=0, concat_axis=0, tiled=True)
    other = lax.ppermute(rows, "core", [(0, 1), (1, 0)])
    zh = lax.axis_index("zh")
    where = jnp.stack([zh, (place + zh == cells_dev * elems - 1).astype(jnp.int32)])
    own_part, right = gram_own(where, matrices, rows)
    other_part = gram_other(other, right)
    own_part = swap_sum(swap_sum(own_part, "x"), "y")
    other_part = swap_sum(swap_sum(other_part, "x"), "y")
    is_first = lax.axis_index("core") == 0
    by_core = jnp.stack(
        [jnp.where(is_first, own_part, other_part), jnp.where(is_first, other_part, own_part)], 1
    )
    sub, cols = by_core.shape[2:]
    column = jnp.broadcast_to(by_core[None], (zls,) + by_core.shape).reshape(-1, sub, cols)
    column = lax.all_to_all(column, ("zl", "zh", "core"), split_axis=0, concat_axis=0, tiled=True)
    piece = summed(column.reshape(zls * zhs, cores, sub, cols))
    whole = lax.all_gather(piece, ("y", "x"), axis=0, tiled=False)
    whole = whole.reshape(ys, xs, cores, sub, cols).transpose(1, 3, 2, 0, 4)
    whole = whole.reshape(xs, sub, cores, 2, zhs, orb_dev).transpose(3, 0, 1, 4, 2, 5)
    whole = whole.reshape(2, orb_dev, zhs * cores * orb_dev)
    whole = whole.astype(f32) * (1.0 / (cells_dev * elems * nodes))

    upper = jnp.einsum("cfm,cmo->cfo", onehot, current_b[:, -face:], preferred_element_type=f32)
    states = jnp.concatenate([current_b[:, :-face], upper.astype(bf16)], 1)
    return (states, whole[0], whole[1])


def solution(mesh):
    names = elem + state
    fine = Mesh(mesh.devices.reshape([size for _, size in ELEM + STATE]), names)
    return jax.shard_map(
        local,
        mesh=fine,
        in_specs=(P(elem, None, None), P(elem, None, state), P(elem, None)),
        out_specs=(P(elem, None, state), P(state, None), P(state, None)),
        check_vma=False,
    )
```

time: 825 us -> 253 us (0.31)
  the two profiles are of different devices: /device:TPU:192 before, /device:TPU:64 now
where the time goes in v1:
time: 253 us; the launch traced here: 251 us
  starting transfers between devices  85.2 us (34%)
  waiting for transfers between devices  77.8 us (31%)
  blocking collectives  47.4 us (19%)
  Pallas kernels  12.4 us (5%)
  other arithmetic  10.3 us (4%)
  local copies, waits for them, and re-layouts  10.2 us (4%)
  matrix products  7.05 us (3%)
    all_gather x1, blocking collectives, local(): whole = lax.all_gather(piece, ('y', 'x'), axis=0, tiled=False)  47.4 us
    all_to_all x4, waiting for transfers between devices, swap_sum(): lax.all_to_all(part, axis, split_axis=0, concat_axis=0, tiled=True)  35.6 us
    ppermute x8, starting transfers between devices, shifted(): return lax.ppermute(faces, elem, pairs)  29.3 us
    all_to_all x4, starting transfers between devices, swap_sum(): lax.all_to_all(part, axis, split_axis=0, concat_axis=0, tiled=True)  24.1 us
    all_to_all x1, waiting for transfers between devices, local(): rows = lax.all_to_all(rows, 'zh', split_axis=0, concat_axis=0, tiled=True)  20.1 us
    all_to_all x1, starting transfers between devices, local(): rows = lax.all_to_all(rows, 'zh', split_axis=0, concat_axis=0, tiled=True)  19.4 us
    all_to_all x1, waiting for transfers between devices, local(): lax.all_to_all(column, ('zl', 'zh', 'core'), split_axis=0, concat_axis=0,...  12 us
    all_to_all x1, starting transfers between devices, local(): lax.all_to_all(column, ('zl', 'zh', 'core'), split_axis=0, concat_axis=0,...  10.4 us
  transfers between devices with their start and end apart: 15, of which 10 were waited for; matrix products, arithmetic and copies ran while one was open for 3% of the time, Pallas kernels for 1%

profile of v1, /device:TPU:64, one launch (start us, length us, event | category | flops | bytes accessed | tf_op | source)
XLA Modules:
  0.0 251.3 jit_solution(6773382696489086457)
XLA Ops:
  0.6 1.1 slice.134
  1.7 1.1 convolution_convert_fusion.1
  2.9 1.4 fusion.23
  5.1 4.4 %reorder.1.k_ref = bf16[4,512,512]{2,1,0:T(8,128)(2,1)} custom-call(bf16[4,128,128]{2,1,0:T(8,128)(2,1)} %fusion.8.perm_ref, bf16[4,64,64]{2,1,0:T(8,128)(2,1)} %get-tuple-element.31.perm_t_ref, bf16[4,512,512]{2,1,0:T(8,128)(2,1)} %k_ref.1), custom_call_target="tpu_custom_call" | custom-call | tf_op jit(solution)/shard_map/reorder/pallas_call | solution.py:51
  9.5 1.8 fusion.24
  11.2 4.3 %collective-permute-start = (f32[64,128]{1,0:T(8,128)}, f32[64,128]{1,0:T(8,128)S(1)}, u32[]{:S(2)}, u32[]{:S(2)}) collective-permute-start(f32[64,128]{1,0:T(8,128)} %fusion.24), channel_id=1, source_target_pairs={{0,8},{8,16},{16,24},{24,32},{32,40},{40,48},{48,56},{56,64},{64,7... | collective-permute-start | bytes 98312 | tf_op jit(solution)/shard_map/ppermute | solution.py:29
  15.8 0.8 pad_maximum_fusion.4
  16.5 7.6 %collective-permute-start.1 = (f32[2,64,128]{2,1,0:T(8,128)}, f32[2,64,128]{2,1,0:T(8,128)}, u32[]{:S(2)}, u32[]{:S(2)}) collective-permute-start(f32[2,64,128]{2,1,0:T(8,128)} %pad_maximum_fusion.4), channel_id=1, source_target_pairs={{8,0},{16,8},{24,16},{32,24},{40,32},{48,40},{56,48},{64,56},{72,6... | collective-permute-start | bytes 196616 | tf_op jit(solution)/shard_map/ppermute | solution.py:29
  26.5 0.8 fusion.42
  27.3 1.1 slice_add_fusion.7
  28.5 0.7 fusion.43
  29.5 1.9 collective-permute-start.2
  31.5 3.9 %collective-permute-start.3 = (f32[64,128]{1,0:T(8,128)S(1)}, f32[64,128]{1,0:T(8,128)S(1)}, u32[]{:S(2)}, u32[]{:S(2)}) collective-permute-start(f32[64,128]{1,0:T(8,128)S(1)} %fusion.21), channel_id=1, source_target_pairs={{8,0},{16,8},{24,16},{32,24},{40,32},{48,40},{56,48},{64,56},{72,6... | collective-permute-start | bytes 98312 | tf_op jit(solution)/shard_map/ppermute | solution.py:29
  35.5 1.8 collective-permute-done.3
  37.5 0.7 fusion.44
  38.5 2.6 %collective-permute-start.4 = (f32[64,128]{1,0:T(8,128)S(1)}, f32[64,128]{1,0:T(8,128)S(1)}, u32[]{:S(2)}, u32[]{:S(2)}) collective-permute-start(f32[64,128]{1,0:T(8,128)S(1)} %fusion.20), channel_id=1, source_target_pairs={{0,8},{8,16},{16,24},{24,32},{32,40},{40,48},{48,56},{56,64},{64,7... | collective-permute-start | bytes 98312 | tf_op jit(solution)/shard_map/ppermute | solution.py:29
  41.1 3.3 %collective-permute-start.5 = (f32[64,128]{1,0:T(8,128)S(1)}, f32[64,128]{1,0:T(8,128)S(1)}, u32[]{:S(2)}, u32[]{:S(2)}) collective-permute-start(f32[64,128]{1,0:T(8,128)S(1)} %fusion.19), channel_id=1, source_target_pairs={{8,0},{16,8},{24,16},{32,24},{40,32},{48,40},{56,48},{64,56},{72,6... | collective-permute-start | bytes 98312 | tf_op jit(solution)/shard_map/ppermute | solution.py:29
  44.4 2.4 collective-permute-done.5
  48.1 3.9 %collective-permute-start.6 = (f32[64,128]{1,0:T(8,128)S(1)}, f32[64,128]{1,0:T(8,128)S(1)}, u32[]{:S(2)}, u32[]{:S(2)}) collective-permute-start(f32[64,128]{1,0:T(8,128)S(1)} %fusion.18), channel_id=1, source_target_pairs={{0,8},{8,16},{16,24},{24,32},{32,40},{40,48},{48,56},{56,64},{64,7... | collective-permute-start | bytes 98312 | tf_op jit(solution)/shard_map/ppermute | solution.py:29
  52.1 1.9 collective-permute-start.7
  54.1 3.8 %collective-permute-done.7 = f32[64,128]{1,0:T(8,128)S(1)} collective-permute-done((f32[64,128]{1,0:T(8,128)S(1)}, f32[64,128]{1,0:T(8,128)S(1)}, u32[]{:S(2)}, u32[]{:S(2)}) %collective-permute-start.7) | collective-permute-done | bytes 32800 | tf_op jit(solution)/shard_map/ppermute | solution.py:29
  58.8 1.0 fusion.16
  59.8 0.9 pad_maximum_fusion.1
  60.7 19.4 %all-to-all-start = ((bf16[4,576,128]{2,1,0:T(8,128)(2,1)}), bf16[4,576,128]{2,1,0:T(8,128)(2,1)S(1)}, u32[]{:S(2)}, u32[]{:S(2)}) async-start(bf16[4,576,128]{2,1,0:T(8,128)(2,1)} %pad_maximum_fusion.1), calls=%async_computation | async-start | bytes 1179648 | tf_op jit(solution)/shard_map/all_to_all | solution.py:202
  80.7 20.1 %all-to-all-done.rows_ref = bf16[4,576,128]{2,1,0:T(8,128)(2,1)S(1)} async-done(((bf16[4,576,128]{2,1,0:T(8,128)(2,1)}), bf16[4,576,128]{2,1,0:T(8,128)(2,1)S(1)}, u32[]{:S(2)}, u32[]{:S(2)}) %all-to-all-start) | async-done | bytes 589856 | tf_op jit(solution)/shard_map/all_to_all | solution.py:202
  100.8 0.8 copy-done.1
  101.6 4.5 %gram_own.1 = (bf16[4,8,4,32,128]{4,3,2,1,0:T(8,128)(2,1)}, bf16[512,1024]{1,0:T(8,128)(2,1)}) custom-call(s32[2]{0:T(128)} %pad_add_fusion.where_ref, bf16[4,512,512]{2,1,0:T(8,128)(2,1)} %reorder.1.k_ref, bf16[4,576,128]{2,1,0:T(8,128)(2,1)} %copy-done.1), custom_call_target="tpu_custom_call" | custom-call | tf_op jit(solution)/shard_map/gram_own/pallas_call | solution.py:110
  106.1 8.4 %all-to-all-start.1 = ((bf16[4,8,4,32,128]{4,3,2,1,0:T(8,128)(2,1)}), bf16[4,8,4,32,128]{4,3,2,1,0:T(8,128)(2,1)S(1)}, u32[]{:S(2)}, u32[]{:S(2)}) async-start(bf16[4,8,4,32,128]{4,3,2,1,0:T(8,128)(2,1)} %get-tuple-element.5), calls=%async_computation.1 | async-start | bytes 2097152 | tf_op jit(solution)/shard_map/all_to_all | solution.py:142
  114.5 1.9 collective-permute-start.8
  116.4 2.0 collective-permute-done.8.rows_ref
  118.4 0.8 copy-done.5
  119.2 3.4 %gram_other.1 = bf16[4,8,4,32,128]{4,3,2,1,0:T(8,128)(2,1)} custom-call(bf16[4,576,128]{2,1,0:T(8,128)(2,1)} %copy-done.5, bf16[512,1024]{1,0:T(8,128)(2,1)} %get-tuple-element.6.right_ref), custom_call_target="tpu_custom_call" | custom-call | tf_op jit(solution)/shard_map/gram_other/pallas_call | solution.py:130
  122.7 2.7 %all-to-all-done.1 = bf16[4,8,4,32,128]{4,3,2,1,0:T(8,128)(2,1)S(1)} async-done(((bf16[4,8,4,32,128]{4,3,2,1,0:T(8,128)(2,1)}), bf16[4,8,4,32,128]{4,3,2,1,0:T(8,128)(2,1)S(1)}, u32[]{:S(2)}, u32[]{:S(2)}) %all-to-all-start.1) | async-done | bytes 1048608 | tf_op jit(solution)/shard_map/all_to_all | solution.py:142
  125.4 3.5 %all-to-all-start.3 = ((bf16[4,8,4,32,128]{4,3,2,1,0:T(8,128)(2,1)}), bf16[4,8,4,32,128]{4,3,2,1,0:T(8,128)(2,1)S(1)}, u32[]{:S(2)}, u32[]{:S(2)}) async-start(bf16[4,8,4,32,128]{4,3,2,1,0:T(8,128)(2,1)} %gram_other.1), calls=%async_computation.3 | async-start | bytes 2097152 | tf_op jit(solution)/shard_map/all_to_all | solution.py:142
  128.9 0.9 reduce_sum.60
  129.9 13.0 %all-to-all-done.3 = bf16[4,8,4,32,128]{4,3,2,1,0:T(8,128)(2,1)S(1)} async-done(((bf16[4,8,4,32,128]{4,3,2,1,0:T(8,128)(2,1)}), bf16[4,8,4,32,128]{4,3,2,1,0:T(8,128)(2,1)S(1)}, u32[]{:S(2)}, u32[]{:S(2)}) %all-to-all-start.3) | async-done | bytes 1048608 | tf_op jit(solution)/shard_map/all_to_all | solution.py:142
  142.9 8.8 %all-to-all-start.2 = ((bf16[8,4,32,128]{3,2,1,0:T(8,128)(2,1)}), bf16[8,4,32,128]{3,2,1,0:T(8,128)(2,1)S(1)}, u32[]{:S(2)}, u32[]{:S(2)}) async-start(bf16[8,4,32,128]{3,2,1,0:T(8,128)(2,1)} %reduce_sum.60), calls=%async_computation.2 | async-start | bytes 524288 | tf_op jit(solution)/shard_map/all_to_all | solution.py:142
  151.7 0.9 reduce_sum.62
  152.6 9.6 %all-to-all-done.2 = bf16[8,4,32,128]{3,2,1,0:T(8,128)(2,1)S(1)} async-done(((bf16[8,4,32,128]{3,2,1,0:T(8,128)(2,1)}), bf16[8,4,32,128]{3,2,1,0:T(8,128)(2,1)S(1)}, u32[]{:S(2)}, u32[]{:S(2)}) %all-to-all-start.2) | async-done | bytes 262176 | tf_op jit(solution)/shard_map/all_to_all | solution.py:142
  162.1 3.4 %all-to-all-start.4 = ((bf16[8,4,32,128]{3,2,1,0:T(8,128)(2,1)}), bf16[8,4,32,128]{3,2,1,0:T(8,128)(2,1)S(1)}, u32[]{:S(2)}, u32[]{:S(2)}) async-start(bf16[8,4,32,128]{3,2,1,0:T(8,128)(2,1)} %reduce_sum.62), calls=%async_computation.4 | async-start | bytes 524288 | tf_op jit(solution)/shard_map/all_to_all | solution.py:142
  165.6 10.3 %all-to-all-done.4 = bf16[8,4,32,128]{3,2,1,0:T(8,128)(2,1)S(1)} async-done(((bf16[8,4,32,128]{3,2,1,0:T(8,128)(2,1)}), bf16[8,4,32,128]{3,2,1,0:T(8,128)(2,1)S(1)}, u32[]{:S(2)}, u32[]{:S(2)}) %all-to-all-start.4) | async-done | bytes 262176 | tf_op jit(solution)/shard_map/all_to_all | solution.py:142
  176.1 0.7 broadcast_in_dim.56
  176.8 10.4 %all-to-all-start.5 = ((bf16[24,32,128]{2,1,0:T(8,128)(2,1)}), bf16[24,32,128]{2,1,0:T(8,128)(2,1)S(1)}, u32[]{:S(2)}, u32[]{:S(2)}) async-start(bf16[24,32,128]{2,1,0:T(8,128)(2,1)} %bitcast.22), calls=%async_computation.5 | async-start | bytes 393216 | tf_op jit(solution)/shard_map/all_to_all | solution.py:216
  187.4 0.8 pad_maximum_fusion.2
  188.3 12.0 %all-to-all-done.5 = bf16[24,32,128]{2,1,0:T(8,128)(2,1)S(1)} async-done(((bf16[24,32,128]{2,1,0:T(8,128)(2,1)}), bf16[24,32,128]{2,1,0:T(8,128)(2,1)S(1)}, u32[]{:S(2)}, u32[]{:S(2)}) %all-to-all-start.5) | async-done | bytes 196640 | tf_op jit(solution)/shard_map/all_to_all | solution.py:216
  200.4 47.4 %all-gather = bf16[64,32,128]{2,1,0:T(8,128)(2,1)S(1)} all-gather(bf16[2,32,128]{2,1,0:T(8,128)(2,1)S(1)} %reduce_sum.64), channel_id=2, replica_groups=mesh['y'=8,'x'=4,'zl'=3,'zh'=4,'core'=2] {'y','x'}, dimensions={0}, use_global_device_ids=true | all-gather | bytes 540672 | tf_op jit(solution)/shard_map/all_gather | solution.py:218
  248.5 1.2 squeeze.52
  250.1 1.2 squeeze.53
  (65 shorter events, 8.8 us)
Async XLA Ops:
  9.5 6.1 %copy-start = (bf16[4,512,512]{2,1,0:T(8,128)(2,1)S(1)}, bf16[4,512,512]{2,1,0:T(8,128)(2,1)}, u32[]{:S(2)}) copy-start(bf16[4,512,512]{2,1,0:T(8,128)(2,1)} %reorder.1.k_ref) | copy-start | bytes 6291460
  11.2 16.1 %collective-permute-start = (f32[64,128]{1,0:T(8,128)}, f32[64,128]{1,0:T(8,128)S(1)}, u32[]{:S(2)}, u32[]{:S(2)}) collective-permute-start(f32[64,128]{1,0:T(8,128)} %fusion.24), channel_id=1, source_target_pairs={{0,8},{8,16},{16,24},{24,32},{32,40},{40,48},{48,56},{56,64},{64,7... | collective-permute-start | bytes 98312 | tf_op jit(solution)/shard_map/ppermute | solution.py:29
  15.6 10.3 %copy-start.3 = (f32[4,512,128]{2,1,0:T(8,128)}, f32[4,512,128]{2,1,0:T(8,128)S(1)}, u32[]{:S(2)}) copy-start(f32[4,512,128]{2,1,0:T(8,128)S(1)} %fusion.5) | copy-start | bytes 3145732
  16.5 10.0 %collective-permute-start.1 = (f32[2,64,128]{2,1,0:T(8,128)}, f32[2,64,128]{2,1,0:T(8,128)}, u32[]{:S(2)}, u32[]{:S(2)}) collective-permute-start(f32[2,64,128]{2,1,0:T(8,128)} %pad_maximum_fusion.4), channel_id=1, source_target_pairs={{8,0},{16,8},{24,16},{32,24},{40,32},{48,40},{56,48},{64,56},{72,6... | collective-permute-start | bytes 196616 | tf_op jit(solution)/shard_map/ppermute | solution.py:29
  24.8 1.0 copy-start.4
  29.5 5.9 %collective-permute-start.2 = (f32[64,128]{1,0:T(8,128)S(1)}, f32[64,128]{1,0:T(8,128)S(1)}, u32[]{:S(2)}, u32[]{:S(2)}) collective-permute-start(f32[64,128]{1,0:T(8,128)S(1)} %fusion.22), channel_id=1, source_target_pairs={{0,8},{8,16},{16,24},{24,32},{32,40},{40,48},{48,56},{56,64},{64,7... | collective-permute-start | bytes 98312 | tf_op jit(solution)/shard_map/ppermute | solution.py:29
  31.5 5.8 %collective-permute-start.3 = (f32[64,128]{1,0:T(8,128)S(1)}, f32[64,128]{1,0:T(8,128)S(1)}, u32[]{:S(2)}, u32[]{:S(2)}) collective-permute-start(f32[64,128]{1,0:T(8,128)S(1)} %fusion.21), channel_id=1, source_target_pairs={{8,0},{16,8},{24,16},{32,24},{40,32},{48,40},{56,48},{64,56},{72,6... | collective-permute-start | bytes 98312 | tf_op jit(solution)/shard_map/ppermute | solution.py:29
  38.5 5.9 %collective-permute-start.4 = (f32[64,128]{1,0:T(8,128)S(1)}, f32[64,128]{1,0:T(8,128)S(1)}, u32[]{:S(2)}, u32[]{:S(2)}) collective-permute-start(f32[64,128]{1,0:T(8,128)S(1)} %fusion.20), channel_id=1, source_target_pairs={{0,8},{8,16},{16,24},{24,32},{32,40},{40,48},{48,56},{56,64},{64,7... | collective-permute-start | bytes 98312 | tf_op jit(solution)/shard_map/ppermute | solution.py:29
  41.1 5.8 %collective-permute-start.5 = (f32[64,128]{1,0:T(8,128)S(1)}, f32[64,128]{1,0:T(8,128)S(1)}, u32[]{:S(2)}, u32[]{:S(2)}) collective-permute-start(f32[64,128]{1,0:T(8,128)S(1)} %fusion.19), channel_id=1, source_target_pairs={{8,0},{16,8},{24,16},{32,24},{40,32},{48,40},{56,48},{64,56},{72,6... | collective-permute-start | bytes 98312 | tf_op jit(solution)/shard_map/ppermute | solution.py:29
  48.1 6.0 %collective-permute-start.6 = (f32[64,128]{1,0:T(8,128)S(1)}, f32[64,128]{1,0:T(8,128)S(1)}, u32[]{:S(2)}, u32[]{:S(2)}) collective-permute-start(f32[64,128]{1,0:T(8,128)S(1)} %fusion.18), channel_id=1, source_target_pairs={{0,8},{8,16},{16,24},{24,32},{32,40},{40,48},{48,56},{56,64},{64,7... | collective-permute-start | bytes 98312 | tf_op jit(solution)/shard_map/ppermute | solution.py:29
  52.1 5.8 %collective-permute-start.7 = (f32[64,128]{1,0:T(8,128)S(1)}, f32[64,128]{1,0:T(8,128)S(1)}, u32[]{:S(2)}, u32[]{:S(2)}) collective-permute-start(f32[64,128]{1,0:T(8,128)S(1)} %fusion.17), channel_id=1, source_target_pairs={{8,0},{16,8},{24,16},{32,24},{40,32},{48,40},{56,48},{64,56},{72,6... | collective-permute-start | bytes 98312 | tf_op jit(solution)/shard_map/ppermute | solution.py:29
  57.9 0.9 copy-start.6
  60.7 40.1 %all-to-all-start = ((bf16[4,576,128]{2,1,0:T(8,128)(2,1)}), bf16[4,576,128]{2,1,0:T(8,128)(2,1)S(1)}, u32[]{:S(2)}, u32[]{:S(2)}) async-start(bf16[4,576,128]{2,1,0:T(8,128)(2,1)} %pad_maximum_fusion.1), calls=%async_computation | async-start | bytes 1179648 | tf_op jit(solution)/shard_map/all_to_all | solution.py:202
  100.8 0.8 copy-start.1
  106.1 8.4 %copy-start.2 = (bf16[4,576,128]{2,1,0:T(8,128)(2,1)S(1)}, bf16[4,576,128]{2,1,0:T(8,128)(2,1)}, u32[]{:S(2)}) copy-start(bf16[4,576,128]{2,1,0:T(8,128)(2,1)} %copy-done.1) | copy-start | bytes 1769476
  106.1 19.3 %all-to-all-start.1 = ((bf16[4,8,4,32,128]{4,3,2,1,0:T(8,128)(2,1)}), bf16[4,8,4,32,128]{4,3,2,1,0:T(8,128)(2,1)S(1)}, u32[]{:S(2)}, u32[]{:S(2)}) async-start(bf16[4,8,4,32,128]{4,3,2,1,0:T(8,128)(2,1)} %get-tuple-element.5), calls=%async_computation.1 | async-start | bytes 2097152 | tf_op jit(solution)/shard_map/all_to_all | solution.py:142
  114.5 3.9 %collective-permute-start.8 = (bf16[4,576,128]{2,1,0:T(8,128)(2,1)S(1)}, bf16[4,576,128]{2,1,0:T(8,128)(2,1)S(1)}, u32[]{:S(2)}, u32[]{:S(2)}) collective-permute-start(bf16[4,576,128]{2,1,0:T(8,128)(2,1)S(1)} %copy-done.2), channel_id=1, source_target_pairs={{0,1},{1,0},{2,3},{3,2},{4,5},{5,4},{6,7},{7,6},{8,9},{9,8},{10,11... | collective-permute-start | bytes 1769480 | tf_op jit(solution)/shard_map/ppermute | solution.py:203
  118.4 0.8 copy-start.5
  125.4 17.5 %all-to-all-start.3 = ((bf16[4,8,4,32,128]{4,3,2,1,0:T(8,128)(2,1)}), bf16[4,8,4,32,128]{4,3,2,1,0:T(8,128)(2,1)S(1)}, u32[]{:S(2)}, u32[]{:S(2)}) async-start(bf16[4,8,4,32,128]{4,3,2,1,0:T(8,128)(2,1)} %gram_other.1), calls=%async_computation.3 | async-start | bytes 2097152 | tf_op jit(solution)/shard_map/all_to_all | solution.py:142
  142.9 19.3 %all-to-all-start.2 = ((bf16[8,4,32,128]{3,2,1,0:T(8,128)(2,1)}), bf16[8,4,32,128]{3,2,1,0:T(8,128)(2,1)S(1)}, u32[]{:S(2)}, u32[]{:S(2)}) async-start(bf16[8,4,32,128]{3,2,1,0:T(8,128)(2,1)} %reduce_sum.60), calls=%async_computation.2 | async-start | bytes 524288 | tf_op jit(solution)/shard_map/all_to_all | solution.py:142
  151.7 35.6 %copy-start.7 = (s32[4,64]{1,0:T(4,128)S(1)}, s32[4,64]{1,0:T(4,128)}, u32[]{:S(2)}) copy-start(s32[4,64]{1,0:T(4,128)} %param.5) | copy-start | bytes 3076
  162.1 13.8 %all-to-all-start.4 = ((bf16[8,4,32,128]{3,2,1,0:T(8,128)(2,1)}), bf16[8,4,32,128]{3,2,1,0:T(8,128)(2,1)S(1)}, u32[]{:S(2)}, u32[]{:S(2)}) async-start(bf16[8,4,32,128]{3,2,1,0:T(8,128)(2,1)} %reduce_sum.62), calls=%async_computation.4 | async-start | bytes 524288 | tf_op jit(solution)/shard_map/all_to_all | solution.py:142
  176.8 23.6 %all-to-all-start.5 = ((bf16[24,32,128]{2,1,0:T(8,128)(2,1)}), bf16[24,32,128]{2,1,0:T(8,128)(2,1)S(1)}, u32[]{:S(2)}, u32[]{:S(2)}) async-start(bf16[24,32,128]{2,1,0:T(8,128)(2,1)} %bitcast.22), calls=%async_computation.5 | async-start | bytes 393216 | tf_op jit(solution)/shard_map/all_to_all | solution.py:216

commit v2 on v1

v2 whole, which is shorter than its diff:
```python
import jax
import jax.numpy as jnp
from jax import lax
from jax.experimental import pallas as pl
from jax.experimental.pallas import tpu as pltpu
from jax.sharding import Mesh
from jax.sharding import PartitionSpec as P

PASSES = 4
ELEM = (("y", 8), ("x", 4), ("zl", 3))
STATE = (("zh", 4), ("core", 2))


filter_width = 2.5

f32 = jnp.float32
bf16 = jnp.bfloat16
elem = tuple(name for name, _ in ELEM)
state = tuple(name for name, _ in STATE)


def dot(a, b, dims=((1,), (0,))):
    return lax.dot_general(a, b, (dims, ((), ())), preferred_element_type=f32)


def shifted(faces, up):
    count = lax.axis_size(elem)
    pairs = [(i, i + 1) if up else (i + 1, i) for i in range(count - 1)]
    return lax.ppermute(faces, elem, pairs)


def vmem():
    return pl.BlockSpec(memory_space=pltpu.VMEM)


def smem():
    return pl.BlockSpec(memory_space=pltpu.SMEM)


SMALL = pltpu.CompilerParams(vmem_limit_bytes=20 * 1024 * 1024)


def selection(map_row):
    face = map_row.shape[1]
    rows = lax.broadcasted_iota(jnp.int32, (face, face), 0)
    return jnp.where(rows == map_row, 1.0, 0.0).astype(bf16)


def first_edges_kernel(map_ref, low_ref, up_ref, first_ref, last_ref, head_ref, tail_ref):
    face = low_ref.shape[1]
    head_ref[0] = dot(low_ref[0], first_ref[0])
    head_ref[1] = first_ref[0, :face].astype(f32)
    cells = map_ref.shape[0]
    up = dot(selection(map_ref[cells - 1 :, :]), up_ref[0]).astype(bf16)
    tail_ref[...] = dot(up, last_ref[0])


def first_edges(cell_matrices, states, face_map):
    cells, nodes, orb = states.shape
    face = face_map.shape[1]
    return pl.pallas_call(
        first_edges_kernel,
        grid=(1,),
        in_specs=[
            pl.BlockSpec((cells, face), lambda i: (0, 0)),
            pl.BlockSpec((1, face, nodes), lambda i: (0, 0, 0)),
            pl.BlockSpec((1, face, nodes), lambda i: (cells - 1, nodes // face - 1, 0)),
            pl.BlockSpec((1, nodes, orb), lambda i: (0, 0, 0)),
            pl.BlockSpec((1, nodes, orb), lambda i: (cells - 1, 0, 0)),
        ],
        out_specs=[
            pl.BlockSpec((2, face, orb), lambda i: (0, 0, 0)),
            pl.BlockSpec((face, orb), lambda i: (0, 0)),
        ],
        out_shape=[
            jax.ShapeDtypeStruct((2, face, orb), f32),
            jax.ShapeDtypeStruct((face, orb), f32),
        ],
        compiler_params=SMALL,
        name="first_edges",
    )(face_map, cell_matrices, cell_matrices, states, states)


def reorder_kernel(map_ref, k_ref, x_ref, out_ref, start_ref):
    face = map_ref.shape[2]
    nodes = k_ref.shape[1]
    inner = nodes - face
    select = selection(map_ref[0])
    wide = 2 * face
    eye = lax.broadcasted_iota(jnp.int32, (wide, wide), 0) == lax.broadcasted_iota(jnp.int32, (wide, wide), 1)
    both = jnp.concatenate([jnp.zeros((face, face), bf16), select], 1)
    both = jnp.concatenate([jnp.where(eye[:face], 1.0, 0.0).astype(bf16), both], 0)
    out_ref[0, :, : nodes - wide] = k_ref[0, :, : nodes - wide]
    out_ref[0, :, nodes - wide :] = dot(k_ref[0, :, nodes - wide :], both, ((1,), (1,))).astype(bf16)
    out_ref[0, inner:, :] = dot(select, out_ref[0, inner:, :]).astype(bf16)
    start_ref[0, :inner] = x_ref[0, :inner]
    start_ref[0, inner:] = dot(select, x_ref[0, inner:]).astype(bf16)


def reordered(cell_matrices, states, face_map):
    cells, nodes = cell_matrices.shape[:2]
    orb = states.shape[2]
    face = face_map.shape[1]
    per_cell = lambda *shape: pl.BlockSpec((1,) + shape, lambda c: (c, 0, 0))
    return pl.pallas_call(
        reorder_kernel,
        grid=(cells,),
        in_specs=[per_cell(1, face), per_cell(nodes, nodes), per_cell(nodes, orb)],
        out_specs=[per_cell(nodes, nodes), per_cell(nodes, orb)],
        out_shape=[
            jax.ShapeDtypeStruct(cell_matrices.shape, bf16),
            jax.ShapeDtypeStruct(states.shape, bf16),
        ],
        compiler_params=SMALL,
        name="reorder",
    )(face_map[:, None, :], cell_matrices, states)


def scatter_rows(part, out_ref, block, core):
    xs, ys, _, _, rows, cols = out_ref.shape
    for x in range(xs):
        for y in range(ys):
            tile = part[x * rows : (x + 1) * rows, y * cols : (y + 1) * cols].astype(bf16)
            out_ref[x, y, block, core] = tile


def right_kernel(where_ref, k_ref, rows_ref, right_ref):
    blocks, total, orb = rows_ref.shape
    nodes = k_ref.shape[1]
    inner = 2 * nodes - total
    is_last = where_ref[1] == 1
    matrix = k_ref[where_ref[0]]
    for s in range(blocks):
        at = slice(s * orb, (s + 1) * orb)
        right_ref[:, at] = dot(matrix, rows_ref[s, :nodes]).astype(bf16)
        at = slice((blocks + s) * orb, (blocks + s + 1) * orb)
        right_ref[:inner, at] = rows_ref[s, :inner]
        paired = rows_ref[s, nodes:]
        right_ref[inner:, at] = jnp.where(is_last, paired, jnp.zeros_like(paired))


def gram_kernel(where_ref, own_ref, other_ref, right_ref, out_ref, left_ref):
    blocks, total, _ = own_ref.shape
    nodes = right_ref.shape[0]
    inner = 2 * nodes - total
    for ref, core in ((own_ref, where_ref[2]), (other_ref, 1 - where_ref[2])):
        for s in range(blocks):
            left_ref[:inner] = ref[s, :inner]
            left_ref[inner:] = ref[s, nodes:]
            part = dot(left_ref[...], right_ref[...], ((0,), (0,)))
            scatter_rows(part, out_ref, s, core)


def right_of(where, matrices, rows):
    blocks, _, orb = rows.shape
    nodes = matrices.shape[1]
    return pl.pallas_call(
        right_kernel,
        in_specs=[smem(), vmem(), vmem()],
        out_specs=vmem(),
        out_shape=jax.ShapeDtypeStruct((nodes, 2 * blocks * orb), bf16),
        compiler_params=SMALL,
        name="right",
    )(where, matrices, rows)


def gram(where, own, other, right):
    blocks, _, orb = own.shape
    xs, ys, cores = lax.axis_size("x"), lax.axis_size("y"), lax.axis_size("core")
    shape = (xs, ys, blocks, cores, orb // xs, 2 * blocks * orb // ys)
    return pl.pallas_call(
        gram_kernel,
        in_specs=[smem(), vmem(), vmem(), vmem()],
        out_specs=vmem(),
        out_shape=jax.ShapeDtypeStruct(shape, bf16),
        scratch_shapes=[pltpu.VMEM((right.shape[0], orb), bf16)],
        compiler_params=SMALL,
        name="gram",
    )(where, own, other, right)


def assemble_kernel(scale, pieces_ref, ham_ref, inter_ref):
    ys, xs, cores, sub, cols = pieces_ref.shape
    orb = sub * xs
    for out_ref, half in ((ham_ref, 0), (inter_ref, 1)):
        for y in range(ys // 2):
            for k in range(cols // orb):
                zh = y * cols // orb + k
                for c in range(cores):
                    for x in range(xs):
                        tile = pieces_ref[half * ys // 2 + y, x, c, :, k * orb : (k + 1) * orb]
                        at = (zh * cores + c) * orb
                        out_ref[x * sub : (x + 1) * sub, at : at + orb] = tile.astype(f32) * scale


def assemble(pieces, scale):
    ys, xs, cores, sub, cols = pieces.shape
    out = jax.ShapeDtypeStruct((sub * xs, ys * cores * cols // 2), f32)
    return pl.pallas_call(
        lambda *refs: assemble_kernel(scale, *refs),
        in_specs=[vmem()],
        out_specs=[vmem(), vmem()],
        out_shape=[out, out],
        compiler_params=SMALL,
        name="assemble",
    )(pieces)


def summed(parts):
    return jnp.sum(parts.astype(f32), 0).astype(bf16)


def swap_sum(part, axis):
    return summed(lax.all_to_all(part, axis, split_axis=0, concat_axis=0, tiled=True))


def local(cell_matrices, initial_states, face_map):
    face = face_map.shape[1]
    cells_dev, nodes = cell_matrices.shape[:2]
    orb_dev = initial_states.shape[2]
    elems = lax.axis_size(elem)
    zhs, cores, zls = lax.axis_size("zh"), lax.axis_size("core"), lax.axis_size("zl")
    xs, ys = lax.axis_size("x"), lax.axis_size("y")
    head, tail = first_edges(cell_matrices, initial_states, face_map)
    cell_matrices, initial_states, head, tail = lax.optimization_barrier(
        (cell_matrices, initial_states, head, tail)
    )
    both = shifted(head, False)
    from_below = shifted(tail, True)
    matrices, current_b = reordered(cell_matrices, initial_states, face_map)

    def edges(values):
        return (
            dot(matrices[0, :face], values[0]),
            dot(matrices[-1, -face:], values[-1]),
        )

    start = current_b.astype(f32)
    previous = start
    current = start
    from_above, next_start = both[0], both[1]
    for degree in range(PASSES):
        if degree > 0:
            head, tail = edges(current_b)
            from_above = shifted(head, False)
            from_below = shifted(tail, True)
        products = jnp.einsum("cij,cjo->cio", matrices, current_b, preferred_element_type=f32)
        from_next = jnp.concatenate([products[1:, :face], from_above[None]], 0)
        from_low = jnp.concatenate([from_below[None], products[:-1, -face:]], 0)
        image = jnp.concatenate(
            [
                products[:, :face] + from_low,
                products[:, face:-face],
                products[:, -face:] + from_next,
            ],
            1,
        )
        following = image / filter_width if degree == 0 else 2.0 / filter_width * image - previous
        previous = current
        current = following
        current_b = following.astype(bf16)

    place = lax.axis_index(elem) * cells_dev
    cell_index = place + jnp.arange(cells_dev, dtype=jnp.int32)
    is_last = cell_index == cells_dev * elems - 1
    step = start[:, -face:] - jnp.concatenate([start[1:, :face], next_start[None]], 0)
    step = jnp.where(is_last[:, None, None], 0.0, step)
    paired = (current[:, -face:] - step).astype(bf16)

    rows = jnp.concatenate([current_b, paired], 1)
    rows = lax.all_to_all(rows, "zh", split_axis=0, concat_axis=0, tiled=True)
    other = lax.ppermute(rows, "core", [(0, 1), (1, 0)])
    zh = lax.axis_index("zh")
    at_end = (place + zh == cells_dev * elems - 1).astype(jnp.int32)
    where = jnp.stack([zh, at_end, lax.axis_index("core")])
    right = right_of(where, matrices, rows)
    part = gram(where, rows, other, right)
    part = swap_sum(part, "x")
    part = swap_sum(part, "y")
    sub, cols = part.shape[2:]
    column = jnp.broadcast_to(part[None], (zls,) + part.shape).reshape(-1, sub, cols)
    column = lax.all_to_all(column, ("zl", "zh", "core"), split_axis=0, concat_axis=0, tiled=True)
    piece = summed(column.reshape(zls * zhs, cores, sub, cols))
    pieces = jnp.broadcast_to(piece[None], (ys * xs,) + piece.shape)
    pieces = lax.all_to_all(pieces, ("y", "x"), split_axis=0, concat_axis=0, tiled=True)
    scale = 1.0 / (cells_dev * elems * nodes)
    hamiltonian, intersection = assemble(pieces.reshape(ys, xs, cores, sub, cols), scale)

    onehot = (face_map[:, :, None] == jnp.arange(face, dtype=jnp.int32)[None, None, :]).astype(bf16)
    upper = jnp.einsum("cfm,cmo->cfo", onehot, current_b[:, -face:], preferred_element_type=f32)
    states = jnp.concatenate([current_b[:, :-face], upper.astype(bf16)], 1)
    return (states, hamiltonian, intersection)


def solution(mesh):
    names = elem + state
    fine = Mesh(mesh.devices.reshape([size for _, size in ELEM + STATE]), names)
    return jax.shard_map(
        local,
        mesh=fine,
        in_specs=(P(elem, None, None), P(elem, None, state), P(elem, None)),
        out_specs=(P(elem, None, state), P(state, None), P(state, None)),
        check_vma=False,
    )
```

time: 253 us -> 210 us (0.83)
  the two profiles are of different devices: /device:TPU:64 before, /device:TPU:1 now
where the time goes in v2:
time: 210 us; the launch traced here: 209 us
  blocking collectives  115 us (55%)
  starting transfers between devices  39 us (19%)
  waiting for transfers between devices  28.4 us (14%)
  local copies, waits for them, and re-layouts  9.35 us (4%)
  Pallas kernels  6.04 us (3%)
  other arithmetic  5.47 us (3%)
  matrix products  5.01 us (2%)
    all_to_all x2, blocking collectives, swap_sum(): lax.all_to_all(part, axis, split_axis=0, concat_axis=0, tiled=True)  59.6 us
    all_to_all x1, blocking collectives, local(): rows = lax.all_to_all(rows, 'zh', split_axis=0, concat_axis=0, tiled=True)  35.2 us
    ppermute x8, starting transfers between devices, shifted(): return lax.ppermute(faces, elem, pairs)  21.7 us
    all_to_all x1, blocking collectives, local(): lax.all_to_all(column, ('zl', 'zh', 'core'), split_axis=0, concat_axis=0,...  20.1 us
    all_to_all x1, waiting for transfers between devices, local(): lax.all_to_all(pieces, ('y', 'x'), split_axis=0, concat_axis=0, tiled=True)  16.2 us
    ppermute x1, starting transfers between devices, local(): other = lax.ppermute(rows, 'core', [(0, 1), (1, 0)])  13.5 us
    ppermute x8, waiting for transfers between devices, shifted(): return lax.ppermute(faces, elem, pairs)  12 us
  transfers between devices with their start and end apart: 10, of which 5 were waited for; matrix products, arithmetic and copies ran while one was open for 4% of the time, Pallas kernels for 1%

profile of v2, /device:TPU:1, one launch (start us, length us, event | category | flops | bytes accessed | tf_op | source)
XLA Modules:
  0.0 209.2 jit_solution(5898741492082262776)
XLA Ops:
  0.6 1.6 copy-done
  2.2 1.0 copy-done.1
  3.3 0.7 copy-done.2
  3.9 0.3 first_edges.1
  4.2 4.8 %collective-permute-start = (f32[64,128]{1,0:T(8,128)S(1)}, f32[64,128]{1,0:T(8,128)S(1)}, u32[]{:S(2)}, u32[]{:S(2)}) collective-permute-start(f32[64,128]{1,0:T(8,128)S(1)} %get-tuple-element.19), channel_id=1, source_target_pairs={{0,8},{8,16},{16,24},{24,32},{32,40},{40,48},{48,56},{56,64},{64,7... | collective-permute-start | bytes 98312 | tf_op jit(solution)/shard_map/ppermute | solution.py:29
  9.1 1.3 collective-permute-start.1
  10.4 1.5 reorder.1
  11.9 1.7 fusion.36
  13.6 1.6 fusion.34
  15.2 1.2 slice.146
  16.4 1.0 convert_element_type.30
  17.5 0.6 slice.175
  18.1 0.8 fusion.35
  18.9 1.1 slice_add_fusion.7
  20.2 0.7 fusion.37
  21.0 0.2 fusion.13
  21.2 4.6 %collective-permute-start.2 = (f32[64,128]{1,0:T(8,128)S(1)}, f32[64,128]{1,0:T(8,128)S(1)}, u32[]{:S(2)}, u32[]{:S(2)}) collective-permute-start(f32[64,128]{1,0:T(8,128)S(1)} %fusion.14), channel_id=1, source_target_pairs={{0,8},{8,16},{16,24},{24,32},{32,40},{40,48},{48,56},{56,64},{64,7... | collective-permute-start | bytes 98312 | tf_op jit(solution)/shard_map/ppermute | solution.py:29
  25.8 1.3 collective-permute-start.3
  27.2 3.3 %collective-permute-done.3 = f32[64,128]{1,0:T(8,128)S(1)} collective-permute-done((f32[64,128]{1,0:T(8,128)S(1)}, f32[64,128]{1,0:T(8,128)S(1)}, u32[]{:S(2)}, u32[]{:S(2)}) %collective-permute-start.3) | collective-permute-done | bytes 32800 | tf_op jit(solution)/shard_map/ppermute | solution.py:29
  30.7 0.7 fusion.38
  31.5 0.2 fusion.11
  31.7 3.7 %collective-permute-start.4 = (f32[64,128]{1,0:T(8,128)S(1)}, f32[64,128]{1,0:T(8,128)S(1)}, u32[]{:S(2)}, u32[]{:S(2)}) collective-permute-start(f32[64,128]{1,0:T(8,128)S(1)} %fusion.12), channel_id=1, source_target_pairs={{0,8},{8,16},{16,24},{24,32},{32,40},{40,48},{48,56},{56,64},{64,7... | collective-permute-start | bytes 98312 | tf_op jit(solution)/shard_map/ppermute | solution.py:29
  35.4 1.3 collective-permute-start.5
  36.8 5.1 %collective-permute-done.5 = f32[64,128]{1,0:T(8,128)S(1)} collective-permute-done((f32[64,128]{1,0:T(8,128)S(1)}, f32[64,128]{1,0:T(8,128)S(1)}, u32[]{:S(2)}, u32[]{:S(2)}) %collective-permute-start.5) | collective-permute-done | bytes 32800 | tf_op jit(solution)/shard_map/ppermute | solution.py:29
  41.9 0.2 fusion.2
  42.1 0.7 fusion.39
  43.0 0.2 fusion.9
  43.1 3.4 %collective-permute-start.6 = (f32[64,128]{1,0:T(8,128)S(1)}, f32[64,128]{1,0:T(8,128)S(1)}, u32[]{:S(2)}, u32[]{:S(2)}) collective-permute-start(f32[64,128]{1,0:T(8,128)S(1)} %fusion.10), channel_id=1, source_target_pairs={{0,8},{8,16},{16,24},{24,32},{32,40},{40,48},{48,56},{56,64},{64,7... | collective-permute-start | bytes 98312 | tf_op jit(solution)/shard_map/ppermute | solution.py:29
  46.5 1.3 collective-permute-start.7
  47.9 3.7 %collective-permute-done.7 = f32[64,128]{1,0:T(8,128)S(1)} collective-permute-done((f32[64,128]{1,0:T(8,128)S(1)}, f32[64,128]{1,0:T(8,128)S(1)}, u32[]{:S(2)}, u32[]{:S(2)}) %collective-permute-start.7) | collective-permute-done | bytes 32800 | tf_op jit(solution)/shard_map/ppermute | solution.py:29
  51.6 0.3 fusion.29
  51.9 0.6 copy-done.6
  52.5 1.0 fusion.8
  53.5 35.2 %all_to_all.25.rows_ref.own_ref = bf16[4,576,128]{2,1,0:T(8,128)(2,1)S(1)} all-to-all(bf16[4,576,128]{2,1,0:T(8,128)(2,1)S(1)} %pad_maximum_fusion), channel_id=1, replica_groups=mesh['y'=8,'x'=4,'zl'=3,'zh'=4,'core'=2] {'zh'}, dimensions={0} | all-to-all | bytes 1179648 | tf_op jit(solution)/shard_map/all_to_all | solution.py:271
  88.7 13.5 %collective-permute-start.8 = (bf16[4,576,128]{2,1,0:T(8,128)(2,1)S(1)}, bf16[4,576,128]{2,1,0:T(8,128)(2,1)S(1)}, u32[]{:S(2)}, u32[]{:S(2)}) collective-permute-start(bf16[4,576,128]{2,1,0:T(8,128)(2,1)S(1)} %all_to_all.25.rows_ref.own_ref), channel_id=1, source_target_pairs={{0,1},{1,0},{2,3},{3,2},{4,5},{5,4},{6,7},{7,6},{8,9},{9,8},{10,11... | collective-permute-start | bytes 1769480 | tf_op jit(solution)/shard_map/ppermute | solution.py:272
  102.3 1.3 right.1.right_ref
  103.6 0.2 collective-permute-done.8.other_ref
  103.8 1.9 gram.1
  105.7 35.9 %all_to_all.26 = bf16[4,8,4,2,32,128]{5,4,3,2,1,0:T(8,128)(2,1)S(1)} all-to-all(bf16[4,8,4,2,32,128]{5,4,3,2,1,0:T(8,128)(2,1)S(1)} %gram.1), channel_id=1, replica_groups=mesh['y'=8,'x'=4,'zl'=3,'zh'=4,'core'=2] {'x'}, dimensions={0} | all-to-all | bytes 4194304 | tf_op jit(solution)/shard_map/all_to_all | solution.py:214
  141.6 0.4 reduce_sum.36
  142.0 23.7 %all_to_all.27 = bf16[8,4,2,32,128]{4,3,2,1,0:T(8,128)(2,1)S(1)} all-to-all(bf16[8,4,2,32,128]{4,3,2,1,0:T(8,128)(2,1)S(1)} %reduce_sum.36), channel_id=1, replica_groups=mesh['y'=8,'x'=4,'zl'=3,'zh'=4,'core'=2] {'y'}, dimensions={0} | all-to-all | bytes 1048576 | tf_op jit(solution)/shard_map/all_to_all | solution.py:214
  165.9 20.1 %all_to_all.28 = bf16[24,32,128]{2,1,0:T(8,128)(2,1)S(1)} all-to-all(bf16[24,32,128]{2,1,0:T(8,128)(2,1)S(1)} %bitcast.57), channel_id=1, replica_groups=mesh['y'=8,'x'=4,'zl'=3,'zh'=4,'core'=2] {'zl','zh','core'}, dimensions={0} | all-to-all | bytes 393216 | tf_op jit(solution)/shard_map/all_to_all | solution.py:282
  186.0 0.9 broadcast_in_dim.62
  187.0 3.9 %all-to-all-start.4 = ((bf16[32,2,32,128]{3,2,1,0:T(8,128)(2,1)}), bf16[32,2,32,128]{3,2,1,0:T(8,128)(2,1)S(1)}, u32[]{:S(2)}, u32[]{:S(2)}) async-start(bf16[32,2,32,128]{3,2,1,0:T(8,128)(2,1)} %broadcast_in_dim.62), calls=%async_computation.4 | async-start | bytes 1048576 | tf_op jit(solution)/shard_map/all_to_all | solution.py:285
  190.9 0.2 convolution_convert_fusion
  191.1 0.8 pad_maximum_fusion.1
  192.0 16.2 %all-to-all-done.4 = bf16[32,2,32,128]{3,2,1,0:T(8,128)(2,1)S(1)} async-done(((bf16[32,2,32,128]{3,2,1,0:T(8,128)(2,1)}), bf16[32,2,32,128]{3,2,1,0:T(8,128)(2,1)S(1)}, u32[]{:S(2)}, u32[]{:S(2)}) %all-to-all-start.4) | async-done | bytes 524320 | tf_op jit(solution)/shard_map/all_to_all | solution.py:285
  208.1 1.0 assemble.1
  (36 shorter events, 1.4 us)
Async XLA Ops:
  0.6 1.6 copy-start
  2.2 1.0 copy-start.1
  3.3 0.7 copy-start.2
  4.2 14.7 %collective-permute-start = (f32[64,128]{1,0:T(8,128)S(1)}, f32[64,128]{1,0:T(8,128)S(1)}, u32[]{:S(2)}, u32[]{:S(2)}) collective-permute-start(f32[64,128]{1,0:T(8,128)S(1)} %get-tuple-element.19), channel_id=1, source_target_pairs={{0,8},{8,16},{16,24},{24,32},{32,40},{40,48},{48,56},{56,64},{64,7... | collective-permute-start | bytes 98312 | tf_op jit(solution)/shard_map/ppermute | solution.py:29
  9.1 9.1 %collective-permute-start.1 = (f32[2,64,128]{2,1,0:T(8,128)S(1)}, f32[2,64,128]{2,1,0:T(8,128)}, u32[]{:S(2)}, u32[]{:S(2)}) collective-permute-start(f32[2,64,128]{2,1,0:T(8,128)S(1)} %get-tuple-element.20), channel_id=1, source_target_pairs={{8,0},{16,8},{24,16},{32,24},{40,32},{48,40},{56,48},{64,56},{72,6... | collective-permute-start | bytes 196616 | tf_op jit(solution)/shard_map/ppermute | solution.py:29
  21.2 6.0 %collective-permute-start.2 = (f32[64,128]{1,0:T(8,128)S(1)}, f32[64,128]{1,0:T(8,128)S(1)}, u32[]{:S(2)}, u32[]{:S(2)}) collective-permute-start(f32[64,128]{1,0:T(8,128)S(1)} %fusion.14), channel_id=1, source_target_pairs={{0,8},{8,16},{16,24},{24,32},{32,40},{40,48},{48,56},{56,64},{64,7... | collective-permute-start | bytes 98312 | tf_op jit(solution)/shard_map/ppermute | solution.py:29
  25.8 4.7 %collective-permute-start.3 = (f32[64,128]{1,0:T(8,128)S(1)}, f32[64,128]{1,0:T(8,128)S(1)}, u32[]{:S(2)}, u32[]{:S(2)}) collective-permute-start(f32[64,128]{1,0:T(8,128)S(1)} %fusion.13), channel_id=1, source_target_pairs={{8,0},{16,8},{24,16},{32,24},{40,32},{48,40},{56,48},{64,56},{72,6... | collective-permute-start | bytes 98312 | tf_op jit(solution)/shard_map/ppermute | solution.py:29
  31.7 5.1 %collective-permute-start.4 = (f32[64,128]{1,0:T(8,128)S(1)}, f32[64,128]{1,0:T(8,128)S(1)}, u32[]{:S(2)}, u32[]{:S(2)}) collective-permute-start(f32[64,128]{1,0:T(8,128)S(1)} %fusion.12), channel_id=1, source_target_pairs={{0,8},{8,16},{16,24},{24,32},{32,40},{40,48},{48,56},{56,64},{64,7... | collective-permute-start | bytes 98312 | tf_op jit(solution)/shard_map/ppermute | solution.py:29
  35.4 6.5 %collective-permute-start.5 = (f32[64,128]{1,0:T(8,128)S(1)}, f32[64,128]{1,0:T(8,128)S(1)}, u32[]{:S(2)}, u32[]{:S(2)}) collective-permute-start(f32[64,128]{1,0:T(8,128)S(1)} %fusion.11), channel_id=1, source_target_pairs={{8,0},{16,8},{24,16},{32,24},{40,32},{48,40},{56,48},{64,56},{72,6... | collective-permute-start | bytes 98312 | tf_op jit(solution)/shard_map/ppermute | solution.py:29
  43.1 4.8 %collective-permute-start.6 = (f32[64,128]{1,0:T(8,128)S(1)}, f32[64,128]{1,0:T(8,128)S(1)}, u32[]{:S(2)}, u32[]{:S(2)}) collective-permute-start(f32[64,128]{1,0:T(8,128)S(1)} %fusion.10), channel_id=1, source_target_pairs={{0,8},{8,16},{16,24},{24,32},{32,40},{40,48},{48,56},{56,64},{64,7... | collective-permute-start | bytes 98312 | tf_op jit(solution)/shard_map/ppermute | solution.py:29
  46.5 5.0 %collective-permute-start.7 = (f32[64,128]{1,0:T(8,128)S(1)}, f32[64,128]{1,0:T(8,128)S(1)}, u32[]{:S(2)}, u32[]{:S(2)}) collective-permute-start(f32[64,128]{1,0:T(8,128)S(1)} %fusion.9), channel_id=1, source_target_pairs={{8,0},{16,8},{24,16},{32,24},{40,32},{48,40},{56,48},{64,56},{72,6... | collective-permute-start | bytes 98312 | tf_op jit(solution)/shard_map/ppermute | solution.py:29
  51.6 0.9 copy-start.6
  51.9 1.7 copy-start.4
  88.7 15.1 %collective-permute-start.8 = (bf16[4,576,128]{2,1,0:T(8,128)(2,1)S(1)}, bf16[4,576,128]{2,1,0:T(8,128)(2,1)S(1)}, u32[]{:S(2)}, u32[]{:S(2)}) collective-permute-start(bf16[4,576,128]{2,1,0:T(8,128)(2,1)S(1)} %all_to_all.25.rows_ref.own_ref), channel_id=1, source_target_pairs={{0,1},{1,0},{2,3},{3,2},{4,5},{5,4},{6,7},{7,6},{8,9},{9,8},{10,11... | collective-permute-start | bytes 1769480 | tf_op jit(solution)/shard_map/ppermute | solution.py:272
  142.0 48.8 %copy-start.5 = (bf16[4,512,128]{2,1,0:T(8,128)(2,1)S(1)}, bf16[4,512,128]{2,1,0:T(8,128)(2,1)}, u32[]{:S(2)}) copy-start(bf16[4,512,128]{2,1,0:T(8,128)(2,1)} %copy-done.4) | copy-start | bytes 1572868
  165.8 25.1 %copy-start.3 = (s32[4,64]{1,0:T(4,128)S(1)}, s32[4,64]{1,0:T(4,128)}, u32[]{:S(2)}) copy-start(s32[4,64]{1,0:T(4,128)} %map_ref.1) | copy-start | bytes 3076
  187.0 21.2 %all-to-all-start.4 = ((bf16[32,2,32,128]{3,2,1,0:T(8,128)(2,1)}), bf16[32,2,32,128]{3,2,1,0:T(8,128)(2,1)S(1)}, u32[]{:S(2)}, u32[]{:S(2)}) async-start(bf16[32,2,32,128]{3,2,1,0:T(8,128)(2,1)} %broadcast_in_dim.62), calls=%async_computation.4 | async-start | bytes 1048576 | tf_op jit(solution)/shard_map/all_to_all | solution.py:285

commit v3 on v2

--- a/solution.py
+++ b/solution.py
@@ -81,47 +81,118 @@
     )(face_map, cell_matrices, cell_matrices, states, states)
 
 
-def reorder_kernel(map_ref, k_ref, x_ref, out_ref, start_ref):
-    face = map_ref.shape[2]
-    nodes = k_ref.shape[1]
+def reorder_kernel(map_ref, k_ref, x_ref, out_ref, start_ref, wide_ref, product_ref):
+    cells, nodes, _ = k_ref.shape
+    face = map_ref.shape[1]
     inner = nodes - face
-    select = selection(map_ref[0])
     wide = 2 * face
     eye = lax.broadcasted_iota(jnp.int32, (wide, wide), 0) == lax.broadcasted_iota(jnp.int32, (wide, wide), 1)
-    both = jnp.concatenate([jnp.zeros((face, face), bf16), select], 1)
-    both = jnp.concatenate([jnp.where(eye[:face], 1.0, 0.0).astype(bf16), both], 0)
-    out_ref[0, :, : nodes - wide] = k_ref[0, :, : nodes - wide]
-    out_ref[0, :, nodes - wide :] = dot(k_ref[0, :, nodes - wide :], both, ((1,), (1,))).astype(bf16)
-    out_ref[0, inner:, :] = dot(select, out_ref[0, inner:, :]).astype(bf16)
-    start_ref[0, :inner] = x_ref[0, :inner]
-    start_ref[0, inner:] = dot(select, x_ref[0, inner:]).astype(bf16)
+    eye = jnp.where(eye[:face], 1.0, 0.0).astype(bf16)
+    for c in range(cells):
+        select = selection(map_ref[c : c + 1, :])
+        both = jnp.concatenate([jnp.zeros((face, face), bf16), select], 1)
+        both = jnp.concatenate([eye, both], 0)
+        out_ref[c, :, : nodes - wide] = k_ref[c, :, : nodes - wide]
+        out_ref[c, :, nodes - wide :] = dot(k_ref[c, :, nodes - wide :], both, ((1,), (1,))).astype(bf16)
+        out_ref[c, inner:, :] = dot(select, out_ref[c, inner:, :]).astype(bf16)
+        start_ref[c, :inner] = x_ref[c, :inner]
+        start_ref[c, inner:] = dot(select, x_ref[c, inner:]).astype(bf16)
+        wide_ref[c] = start_ref[c].astype(f32)
+        product_ref[c] = dot(out_ref[c], start_ref[c])
 
 
 def reordered(cell_matrices, states, face_map):
-    cells, nodes = cell_matrices.shape[:2]
-    orb = states.shape[2]
-    face = face_map.shape[1]
-    per_cell = lambda *shape: pl.BlockSpec((1,) + shape, lambda c: (c, 0, 0))
     return pl.pallas_call(
         reorder_kernel,
-        grid=(cells,),
-        in_specs=[per_cell(1, face), per_cell(nodes, nodes), per_cell(nodes, orb)],
-        out_specs=[per_cell(nodes, nodes), per_cell(nodes, orb)],
+        in_specs=[vmem()] * 3,
+        out_specs=[vmem()] * 4,
         out_shape=[
             jax.ShapeDtypeStruct(cell_matrices.shape, bf16),
             jax.ShapeDtypeStruct(states.shape, bf16),
+            jax.ShapeDtypeStruct(states.shape, f32),
+            jax.ShapeDtypeStruct(states.shape, f32),
         ],
         compiler_params=SMALL,
         name="reorder",
-    )(face_map[:, None, :], cell_matrices, states)
-
-
-def scatter_rows(part, out_ref, block, core):
-    xs, ys, _, _, rows, cols = out_ref.shape
-    for x in range(xs):
-        for y in range(ys):
+    )(face_map, cell_matrices, states)
+
+
+def scatter_rows(part, out_ref, block, core, place):
+    half = out_ref.shape[1]
+    rows, cols = out_ref.shape[-2:]
+    for x in range(part.shape[0] // rows):
+        away = lax.rem(x - place + 4, 4)
+        slots = (
+            jnp.where(away == 0, 4, jnp.where(away == 1, 6, jnp.where(away == 2, 0, 3))),
+            jnp.where(away == 0, 5, jnp.where(away == 1, 1, jnp.where(away == 2, 2, 7))),
+        )
+        for y in range(2 * half):
             tile = part[x * rows : (x + 1) * rows, y * cols : (y + 1) * cols].astype(bf16)
-            out_ref[x, y, block, core] = tile
+            out_ref[slots[y // half], y % half, block, core] = tile
+
+
+def pack_kernel(where_ref, now_ref, start_ref, next_ref, own_ref, up_ref, down_ref):
+    cells, nodes, _ = now_ref.shape
+    face = next_ref.shape[0]
+    total = nodes + face
+    inner = nodes - face
+    half = total // 2
+    last_cell = where_ref[3]
+
+    def rows_of(away):
+        c = lax.rem(where_ref[0] + away, cells)
+        now = now_ref[c]
+        after = jnp.where(c == cells - 1, next_ref[...], start_ref[lax.rem(c + 1, cells), :face])
+        step = jnp.where(c == last_cell, 0.0, start_ref[c, inner:] - after)
+        paired = (now[inner:] - step).astype(bf16)
+        return now.astype(bf16), paired
+
+    for away, ref in ((0, own_ref), (1, up_ref), (3, down_ref)):
+        now, paired = rows_of(away)
+        ref[:nodes] = now
+        ref[nodes:total] = paired
+    now, paired = rows_of(2)
+    up_ref[total:] = now[:half]
+    down_ref[total : total + nodes - half] = now[half:]
+    down_ref[total + nodes - half :] = paired
+
+
+def pack(where, now, start, after):
+    cells, nodes, orb = now.shape
+    total = nodes + after.shape[0]
+    sent = jax.ShapeDtypeStruct((total + total // 2, orb), bf16)
+    return pl.pallas_call(
+        pack_kernel,
+        in_specs=[smem()] + [vmem()] * 3,
+        out_specs=[vmem()] * 3,
+        out_shape=[jax.ShapeDtypeStruct((total, orb), bf16), sent, sent],
+        compiler_params=SMALL,
+        name="pack",
+    )(where, now, start, after)
+
+
+def collect_kernel(where_ref, own_ref, below_ref, above_ref, low_half_ref, high_half_ref, rows_ref):
+    cells, total, _ = rows_ref.shape
+    half = total // 2
+    place = where_ref[0]
+    rows_ref[place] = own_ref[...]
+    rows_ref[lax.rem(place + 3, cells)] = below_ref[:total]
+    rows_ref[lax.rem(place + 1, cells)] = above_ref[:total]
+    far = lax.rem(place + 2, cells)
+    rows_ref[far, :half] = low_half_ref[...]
+    rows_ref[far, half:] = high_half_ref[...]
+
+
+def collect(where, own, below, above, low_half, high_half):
+    total, orb = own.shape
+    return pl.pallas_call(
+        collect_kernel,
+        in_specs=[smem()] + [vmem()] * 5,
+        out_specs=vmem(),
+        out_shape=jax.ShapeDtypeStruct((4, total, orb), bf16),
+        compiler_params=SMALL,
+        name="collect",
+    )(where, own, below, above, low_half, high_half)
 
 
 def right_kernel(where_ref, k_ref, rows_ref, right_ref):
@@ -148,7 +219,7 @@
             left_ref[:inner] = ref[s, :inner]
             left_ref[inner:] = ref[s, nodes:]
             part = dot(left_ref[...], right_ref[...], ((0,), (0,)))
-            scatter_rows(part, out_ref, s, core)
+            scatter_rows(part, out_ref, s, core, where_ref[4])
 
 
 def right_of(where, matrices, rows):
@@ -167,7 +238,7 @@
 def gram(where, own, other, right):
     blocks, _, orb = own.shape
     xs, ys, cores = lax.axis_size("x"), lax.axis_size("y"), lax.axis_size("core")
-    shape = (xs, ys, blocks, cores, orb // xs, 2 * blocks * orb // ys)
+    shape = (2 * xs, ys // 2, blocks, cores, orb // xs, 2 * blocks * orb // ys)
     return pl.pallas_call(
         gram_kernel,
         in_specs=[smem(), vmem(), vmem(), vmem()],
@@ -208,6 +279,23 @@
 
 def summed(parts):
     return jnp.sum(parts.astype(f32), 0).astype(bf16)
+
+
+def ring(part, axis, step):
+    count = lax.axis_size(axis)
+    return lax.ppermute(part, axis, [(i, (i + step) % count) for i in range(count)])
+
+
+def added(*parts):
+    return sum(part.astype(f32) for part in parts).astype(bf16)
+
+
+def x_sum(part):
+    below = ring(part[0:2], "x", 1)
+    above = ring(part[2:4], "x", -1)
+    below_2 = ring(added(below[0], part[6]), "x", 1)
+    above_2 = ring(added(above[0], part[7]), "x", -1)
+    return jnp.concatenate([added(part[4], above[1], below_2), added(part[5], below[1], above_2)], 0)
 
 
 def swap_sum(part, axis):
@@ -227,7 +315,7 @@
     )
     both = shifted(head, False)
     from_below = shifted(tail, True)
-    matrices, current_b = reordered(cell_matrices, initial_states, face_map)
+    matrices, current_b, start, products = reordered(cell_matrices, initial_states, face_map)
 
     def edges(values):
         return (
@@ -235,7 +323,6 @@
             dot(matrices[-1, -face:], values[-1]),
         )
 
-    start = current_b.astype(f32)
     previous = start
     current = start
     from_above, next_start = both[0], both[1]
@@ -244,7 +331,8 @@
             head, tail = edges(current_b)
             from_above = shifted(head, False)
             from_below = shifted(tail, True)
-        products = jnp.einsum("cij,cjo->cio", matrices, current_b, preferred_element_type=f32)
+            current_b, head, tail = lax.optimization_barrier((current_b, head, tail))
+            products = jnp.einsum("cij,cjo->cio", matrices, current_b, preferred_element_type=f32)
         from_next = jnp.concatenate([products[1:, :face], from_above[None]], 0)
         from_low = jnp.concatenate([from_below[None], products[:-1, -face:]], 0)
         image = jnp.concatenate(
@@ -261,21 +349,23 @@
         current_b = following.astype(bf16)
 
     place = lax.axis_index(elem) * cells_dev
-    cell_index = place + jnp.arange(cells_dev, dtype=jnp.int32)
-    is_last = cell_index == cells_dev * elems - 1
-    step = start[:, -face:] - jnp.concatenate([start[1:, :face], next_start[None]], 0)
-    step = jnp.where(is_last[:, None, None], 0.0, step)
-    paired = (current[:, -face:] - step).astype(bf16)
-
-    rows = jnp.concatenate([current_b, paired], 1)
-    rows = lax.all_to_all(rows, "zh", split_axis=0, concat_axis=0, tiled=True)
-    other = lax.ppermute(rows, "core", [(0, 1), (1, 0)])
     zh = lax.axis_index("zh")
-    at_end = (place + zh == cells_dev * elems - 1).astype(jnp.int32)
-    where = jnp.stack([zh, at_end, lax.axis_index("core")])
+    last_cell = cells_dev * elems - 1 - place
+    where = jnp.stack(
+        [zh, (zh == last_cell).astype(jnp.int32), lax.axis_index("core"), last_cell, lax.axis_index("x")]
+    )
+
+    own, up, down = pack(where, current, start, next_start)
+    total = own.shape[0]
+    below = ring(up, "zh", 1)
+    above = ring(down, "zh", -1)
+    low_half = ring(below[total:], "zh", 1)
+    high_half = ring(above[total:], "zh", -1)
+    rows = collect(where, own, below, above, low_half, high_half)
+    other = ring(rows, "core", 1)
     right = right_of(where, matrices, rows)
     part = gram(where, rows, other, right)
-    part = swap_sum(part, "x")
+    part = x_sum(part)
     part = swap_sum(part, "y")
     sub, cols = part.shape[2:]
     column = jnp.broadcast_to(part[None], (zls,) + part.shape).reshape(-1, sub, cols)

time: 210 us -> 217 us (1.033)
  blocking collectives: 115 us -> 57.4 us
  starting transfers between devices: 39 us -> 84.3 us
  waiting for transfers between devices: 28.4 us -> 50.1 us
  local copies, waits for them, and re-layouts: 9.35 us -> 6.6 us
    ppermute x1 -> x9, starting transfers between devices: 13.5 us -> 57.8 us  [ring(): lax.ppermute(part, axis, [(i, (i + step) % count) for i in range(count)])]
    all_to_all x1 -> x0, blocking collectives: 35.2 us -> none  [local(): rows = lax.all_to_all(rows, 'zh', split_axis=0, concat_axis=0, tiled=True)]
    all_to_all x2 -> x1, blocking collectives: 59.6 us -> 27.9 us  [swap_sum(): lax.all_to_all(part, axis, split_axis=0, concat_axis=0, tiled=True)]
    ppermute x1 -> x9, waiting for transfers between devices: 0.23 us -> 24.1 us  [ring(): lax.ppermute(part, axis, [(i, (i + step) % count) for i in range(count)])]
    all_to_all x1, blocking collectives: 20.1 us -> 29.5 us  [local(): lax.all_to_all(column, ('zl', 'zh', 'core'), split_axis=0, concat_axis=0,...]
  transfers between devices with their start and end apart: 10 -> 18, of which waited for: 5 -> 13; matrix products, arithmetic and copies ran while one was open for 4% -> 2% of each run, Pallas kernels for 1% -> 2%
where the time goes in v3:
time: 217 us; the launch traced here: 216 us
  starting transfers between devices  84.3 us (39%)
  blocking collectives  57.4 us (26%)
  waiting for transfers between devices  50.1 us (23%)
  Pallas kernels  7.88 us (4%)
  local copies, waits for them, and re-layouts  6.6 us (3%)
  other arithmetic  5.17 us (2%)
  matrix products  3.28 us (2%)
    ppermute x9, starting transfers between devices, ring(): lax.ppermute(part, axis, [(i, (i + step) % count) for i in range(count)])  57.8 us
    all_to_all x1, blocking collectives, local(): lax.all_to_all(column, ('zl', 'zh', 'core'), split_axis=0, concat_axis=0,...  29.5 us
    all_to_all x1, blocking collectives, swap_sum(): lax.all_to_all(part, axis, split_axis=0, concat_axis=0, tiled=True)  27.9 us
    ppermute x9, waiting for transfers between devices, ring(): lax.ppermute(part, axis, [(i, (i + step) % count) for i in range(count)])  24.1 us
    ppermute x8, starting transfers between devices, shifted(): return lax.ppermute(faces, elem, pairs)  21.5 us
    all_to_all x1, waiting for transfers between devices, local(): lax.all_to_all(pieces, ('y', 'x'), split_axis=0, concat_axis=0, tiled=True)  15.9 us
    ppermute x8, waiting for transfers between devices, shifted(): return lax.ppermute(faces, elem, pairs)  10.1 us
    all_to_all x1, starting transfers between devices, local(): lax.all_to_all(pieces, ('y', 'x'), split_axis=0, concat_axis=0, tiled=True)  4.98 us
  transfers between devices with their start and end apart: 18, of which 13 were waited for; matrix products, arithmetic and copies ran while one was open for 2% of the time, Pallas kernels for 2%

profile of v3, /device:TPU:1, one launch (start us, length us, event | category | flops | bytes accessed | tf_op | source)
XLA Modules:
  0.0 215.7 jit_solution(3434608456372185233)
XLA Ops:
  0.6 1.6 copy-done
  2.2 1.0 copy-done.1
  3.3 0.7 copy-done.3
  4.2 4.8 %collective-permute-start = (f32[64,128]{1,0:T(8,128)S(1)}, f32[64,128]{1,0:T(8,128)S(1)}, u32[]{:S(2)}, u32[]{:S(2)}) collective-permute-start(f32[64,128]{1,0:T(8,128)S(1)} %get-tuple-element.26), channel_id=1, source_target_pairs={{0,8},{8,16},{16,24},{24,32},{32,40},{40,48},{48,56},{56,64},{64,7... | collective-permute-start | bytes 98312 | tf_op jit(solution)/shard_map/ppermute | solution.py:29
  9.1 1.3 collective-permute-start.1
  10.4 2.1 reorder.1
  12.5 1.0 copy-done.2
  13.5 0.9 slice.138
  14.7 1.0 maximum_add_fusion
  15.8 1.2 fusion.4
  17.3 4.4 %collective-permute-start.2 = (f32[64,128]{1,0:T(8,128)S(1)}, f32[64,128]{1,0:T(8,128)S(1)}, u32[]{:S(2)}, u32[]{:S(2)}) collective-permute-start(f32[64,128]{1,0:T(8,128)S(1)} %fusion.13), channel_id=1, source_target_pairs={{0,8},{8,16},{16,24},{24,32},{32,40},{40,48},{48,56},{56,64},{64,7... | collective-permute-start | bytes 98312 | tf_op jit(solution)/shard_map/ppermute | solution.py:29
  21.7 1.3 collective-permute-start.3
  23.0 0.7 fusion.37
  23.9 2.6 %collective-permute-done.3 = f32[64,128]{1,0:T(8,128)S(1)} collective-permute-done((f32[64,128]{1,0:T(8,128)S(1)}, f32[64,128]{1,0:T(8,128)S(1)}, u32[]{:S(2)}, u32[]{:S(2)}) %collective-permute-start.3) | collective-permute-done | bytes 32800 | tf_op jit(solution)/shard_map/ppermute | solution.py:29
  26.9 3.7 %collective-permute-start.4 = (f32[64,128]{1,0:T(8,128)S(1)}, f32[64,128]{1,0:T(8,128)S(1)}, u32[]{:S(2)}, u32[]{:S(2)}) collective-permute-start(f32[64,128]{1,0:T(8,128)S(1)} %fusion.11), channel_id=1, source_target_pairs={{0,8},{8,16},{16,24},{24,32},{32,40},{40,48},{48,56},{56,64},{64,7... | collective-permute-start | bytes 98312 | tf_op jit(solution)/shard_map/ppermute | solution.py:29
  30.6 1.3 collective-permute-start.5
  31.9 0.7 fusion.38
  32.8 4.3 %collective-permute-done.5 = f32[64,128]{1,0:T(8,128)S(1)} collective-permute-done((f32[64,128]{1,0:T(8,128)S(1)}, f32[64,128]{1,0:T(8,128)S(1)}, u32[]{:S(2)}, u32[]{:S(2)}) %collective-permute-start.5) | collective-permute-done | bytes 32800 | tf_op jit(solution)/shard_map/ppermute | solution.py:29
  37.6 3.4 %collective-permute-start.6 = (f32[64,128]{1,0:T(8,128)S(1)}, f32[64,128]{1,0:T(8,128)S(1)}, u32[]{:S(2)}, u32[]{:S(2)}) collective-permute-start(f32[64,128]{1,0:T(8,128)S(1)} %fusion.9), channel_id=1, source_target_pairs={{0,8},{8,16},{16,24},{24,32},{32,40},{40,48},{48,56},{56,64},{64,7... | collective-permute-start | bytes 98312 | tf_op jit(solution)/shard_map/ppermute | solution.py:29
  41.0 1.3 collective-permute-start.7
  42.3 0.7 fusion.39
  43.1 2.9 %collective-permute-done.7 = f32[64,128]{1,0:T(8,128)S(1)} collective-permute-done((f32[64,128]{1,0:T(8,128)S(1)}, f32[64,128]{1,0:T(8,128)S(1)}, u32[]{:S(2)}, u32[]{:S(2)}) %collective-permute-start.7) | collective-permute-done | bytes 32800 | tf_op jit(solution)/shard_map/ppermute | solution.py:29
  46.1 1.0 fusion.30
  47.1 0.6 pack.1
  47.8 12.4 %collective-permute-start.8 = (bf16[864,128]{1,0:T(8,128)(2,1)S(1)}, bf16[864,128]{1,0:T(8,128)(2,1)S(1)}, u32[]{:S(2)}, u32[]{:S(2)}) collective-permute-start(bf16[864,128]{1,0:T(8,128)(2,1)S(1)} %get-tuple-element.33), channel_id=1, source_target_pairs={{0,2},{2,4},{4,6},{6,0},{1,3},{3,5},{5,7},{7,1},{8,10},{10,12},{12... | collective-permute-start | bytes 663560 | tf_op jit(solution)/shard_map/ppermute | solution.py:286
  60.2 3.1 %collective-permute-start.9 = (bf16[864,128]{1,0:T(8,128)(2,1)S(1)}, bf16[864,128]{1,0:T(8,128)(2,1)S(1)}, u32[]{:S(2)}, u32[]{:S(2)}) collective-permute-start(bf16[864,128]{1,0:T(8,128)(2,1)S(1)} %get-tuple-element.34), channel_id=1, source_target_pairs={{0,6},{2,0},{4,2},{6,4},{1,7},{3,1},{5,3},{7,5},{8,14},{10,8},{12,... | collective-permute-start | bytes 663560 | tf_op jit(solution)/shard_map/ppermute | solution.py:286
  63.3 1.6 collective-permute-done.8.below_ref
  64.9 9.5 %collective-permute-start.10 = (bf16[288,128]{1,0:T(8,128)(2,1)S(1)}, bf16[288,128]{1,0:T(8,128)(2,1)S(1)}, u32[]{:S(2)}, u32[]{:S(2)}) collective-permute-start(bf16[288,128]{1,0:T(8,128)(2,1)S(1)} %slice.205), channel_id=1, source_target_pairs={{0,2},{2,4},{4,6},{6,0},{1,3},{3,5},{5,7},{7,1},{8,10},{10,12},{12... | collective-permute-start | bytes 221192 | tf_op jit(solution)/shard_map/ppermute | solution.py:286
  74.4 3.1 %collective-permute-start.11 = (bf16[288,128]{1,0:T(8,128)(2,1)S(1)}, bf16[288,128]{1,0:T(8,128)(2,1)S(1)}, u32[]{:S(2)}, u32[]{:S(2)}) collective-permute-start(bf16[288,128]{1,0:T(8,128)(2,1)S(1)} %slice.206), channel_id=1, source_target_pairs={{0,6},{2,0},{4,2},{6,4},{1,7},{3,1},{5,3},{7,5},{8,14},{10,8},{12,... | collective-permute-start | bytes 221192 | tf_op jit(solution)/shard_map/ppermute | solution.py:286
  77.8 6.6 %collective-permute-done.11.high_half_ref = bf16[288,128]{1,0:T(8,128)(2,1)S(1)} collective-permute-done((bf16[288,128]{1,0:T(8,128)(2,1)S(1)}, bf16[288,128]{1,0:T(8,128)(2,1)S(1)}, u32[]{:S(2)}, u32[]{:S(2)}) %collective-permute-start.11) | collective-permute-done | bytes 73760 | tf_op jit(solution)/shard_map/ppermute | solution.py:286
  85.0 11.1 %collective-permute-start.12 = (bf16[4,576,128]{2,1,0:T(8,128)(2,1)S(1)}, bf16[4,576,128]{2,1,0:T(8,128)(2,1)S(1)}, u32[]{:S(2)}, u32[]{:S(2)}) collective-permute-start(bf16[4,576,128]{2,1,0:T(8,128)(2,1)S(1)} %collect.1.rows_ref.own_ref), channel_id=1, source_target_pairs={{0,1},{1,0},{2,3},{3,2},{4,5},{5,4},{6,7},{7,6},{8,9},{9,8},{10,11... | collective-permute-start | bytes 1769480 | tf_op jit(solution)/shard_map/ppermute | solution.py:286
  96.1 1.3 right.1.right_ref
  97.7 1.9 gram.1
  99.7 3.0 %collective-permute-start.14 = (bf16[2,4,4,2,32,128]{5,4,3,2,1,0:T(8,128)(2,1)S(1)}, bf16[2,4,4,2,32,128]{5,4,3,2,1,0:T(8,128)(2,1)S(1)}, u32[]{:S(2)}, u32[]{:S(2)}) collective-permute-start(bf16[2,4,4,2,32,128]{5,4,3,2,1,0:T(8,128)(2,1)S(1)} %get-tuple-element.43), channel_id=1, source_target_pairs={{0,24},{24,48},{48,72},{72,0},{1,25},{25,49},{49,73},{73,1},{2,26}... | collective-permute-start | bytes 1572872 | tf_op jit(solution)/shard_map/ppermute | solution.py:286
  102.7 8.3 %collective-permute-start.13 = (bf16[2,4,4,2,32,128]{5,4,3,2,1,0:T(8,128)(2,1)S(1)}, bf16[2,4,4,2,32,128]{5,4,3,2,1,0:T(8,128)(2,1)S(1)}, u32[]{:S(2)}, u32[]{:S(2)}) collective-permute-start(bf16[2,4,4,2,32,128]{5,4,3,2,1,0:T(8,128)(2,1)S(1)} %get-tuple-element.44), channel_id=1, source_target_pairs={{0,72},{24,0},{48,24},{72,48},{1,73},{25,1},{49,25},{73,49},{2,74}... | collective-permute-start | bytes 1572872 | tf_op jit(solution)/shard_map/ppermute | solution.py:286
  111.1 10.0 %collective-permute-done.14 = bf16[2,4,4,2,32,128]{5,4,3,2,1,0:T(8,128)(2,1)S(1)} collective-permute-done((bf16[2,4,4,2,32,128]{5,4,3,2,1,0:T(8,128)(2,1)S(1)}, bf16[2,4,4,2,32,128]{5,4,3,2,1,0:T(8,128)(2,1)S(1)}, u32[]{:S(2)}, u32[]{:S(2)}) %collective-permute-start.14) | collective-permute-done | bytes 524320 | tf_op jit(solution)/shard_map/ppermute | solution.py:286
  121.1 0.9 collective-permute-done.13
  122.1 3.5 %collective-permute-start.15 = (bf16[4,4,2,32,128]{4,3,2,1,0:T(8,128)(2,1)S(1)}, bf16[4,4,2,32,128]{4,3,2,1,0:T(8,128)(2,1)S(1)}, u32[]{:S(2)}, u32[]{:S(2)}) collective-permute-start(bf16[4,4,2,32,128]{4,3,2,1,0:T(8,128)(2,1)S(1)} %get-tuple-element.41), channel_id=1, source_target_pairs={{0,24},{24,48},{48,72},{72,0},{1,25},{25,49},{49,73},{73,1},{2,26}... | collective-permute-start | bytes 786440 | tf_op jit(solution)/shard_map/ppermute | solution.py:286
  125.7 3.7 %collective-permute-start.16 = (bf16[4,4,2,32,128]{4,3,2,1,0:T(8,128)(2,1)S(1)}, bf16[4,4,2,32,128]{4,3,2,1,0:T(8,128)(2,1)S(1)}, u32[]{:S(2)}, u32[]{:S(2)}) collective-permute-start(bf16[4,4,2,32,128]{4,3,2,1,0:T(8,128)(2,1)S(1)} %get-tuple-element.42), channel_id=1, source_target_pairs={{0,72},{24,0},{48,24},{72,48},{1,73},{25,1},{49,25},{73,49},{2,74}... | collective-permute-start | bytes 786440 | tf_op jit(solution)/shard_map/ppermute | solution.py:286
  129.4 3.5 %collective-permute-done.15 = bf16[4,4,2,32,128]{4,3,2,1,0:T(8,128)(2,1)S(1)} collective-permute-done((bf16[4,4,2,32,128]{4,3,2,1,0:T(8,128)(2,1)S(1)}, bf16[4,4,2,32,128]{4,3,2,1,0:T(8,128)(2,1)S(1)}, u32[]{:S(2)}, u32[]{:S(2)}) %collective-permute-start.15) | collective-permute-done | bytes 262176 | tf_op jit(solution)/shard_map/ppermute | solution.py:286
  132.9 1.0 collective-permute-done.16
  134.2 27.9 %all_to_all.15 = bf16[8,4,2,32,128]{4,3,2,1,0:T(8,128)(2,1)S(1)} all-to-all(bf16[8,4,2,32,128]{4,3,2,1,0:T(8,128)(2,1)S(1)} %pad_maximum_fusion.1), channel_id=1, replica_groups=mesh['y'=8,'x'=4,'zl'=3,'zh'=4,'core'=2] {'y'}, dimensions={0} | all-to-all | bytes 1048576 | tf_op jit(solution)/shard_map/all_to_all | solution.py:302
  162.2 29.5 %all_to_all.16 = bf16[24,32,128]{2,1,0:T(8,128)(2,1)S(1)} all-to-all(bf16[24,32,128]{2,1,0:T(8,128)(2,1)S(1)} %bitcast.69), channel_id=1, replica_groups=mesh['y'=8,'x'=4,'zl'=3,'zh'=4,'core'=2] {'zl','zh','core'}, dimensions={0} | all-to-all | bytes 393216 | tf_op jit(solution)/shard_map/all_to_all | solution.py:372
  191.8 0.9 broadcast_in_dim.43
  192.7 5.0 %all-to-all-start.2 = ((bf16[32,2,32,128]{3,2,1,0:T(8,128)(2,1)}), bf16[32,2,32,128]{3,2,1,0:T(8,128)(2,1)S(1)}, u32[]{:S(2)}, u32[]{:S(2)}) async-start(bf16[32,2,32,128]{3,2,1,0:T(8,128)(2,1)} %broadcast_in_dim.43), calls=%async_computation.2 | async-start | bytes 1048576 | tf_op jit(solution)/shard_map/all_to_all | solution.py:375
  197.9 0.8 pad_maximum_fusion
  198.8 15.9 %all-to-all-done.2 = bf16[32,2,32,128]{3,2,1,0:T(8,128)(2,1)S(1)} async-done(((bf16[32,2,32,128]{3,2,1,0:T(8,128)(2,1)}), bf16[32,2,32,128]{3,2,1,0:T(8,128)(2,1)S(1)}, u32[]{:S(2)}, u32[]{:S(2)}) %all-to-all-start.2) | async-done | bytes 524320 | tf_op jit(solution)/shard_map/all_to_all | solution.py:375
  214.7 1.0 assemble.1
  (51 shorter events, 4.4 us)
Async XLA Ops:
  0.6 1.6 copy-start
  2.2 1.0 copy-start.1
  3.3 0.7 copy-start.3
  3.9 6.4 %copy-start.4 = (s32[4,64]{1,0:T(4,128)S(1)}, s32[4,64]{1,0:T(4,128)}, u32[]{:S(2)}) copy-start(s32[4,64]{1,0:T(4,128)} %map_ref.3) | copy-start | bytes 3076
  4.2 10.5 %collective-permute-start = (f32[64,128]{1,0:T(8,128)S(1)}, f32[64,128]{1,0:T(8,128)S(1)}, u32[]{:S(2)}, u32[]{:S(2)}) collective-permute-start(f32[64,128]{1,0:T(8,128)S(1)} %get-tuple-element.26), channel_id=1, source_target_pairs={{0,8},{8,16},{16,24},{24,32},{32,40},{40,48},{48,56},{56,64},{64,7... | collective-permute-start | bytes 98312 | tf_op jit(solution)/shard_map/ppermute | solution.py:29
  9.1 5.7 %collective-permute-start.1 = (f32[2,64,128]{2,1,0:T(8,128)S(1)}, f32[2,64,128]{2,1,0:T(8,128)S(1)}, u32[]{:S(2)}, u32[]{:S(2)}) collective-permute-start(f32[2,64,128]{2,1,0:T(8,128)S(1)} %get-tuple-element.27), channel_id=1, source_target_pairs={{8,0},{16,8},{24,16},{32,24},{40,32},{48,40},{56,48},{64,56},{72,6... | collective-permute-start | bytes 196616 | tf_op jit(solution)/shard_map/ppermute | solution.py:29
  12.5 1.0 copy-start.2
  17.3 6.5 %collective-permute-start.2 = (f32[64,128]{1,0:T(8,128)S(1)}, f32[64,128]{1,0:T(8,128)S(1)}, u32[]{:S(2)}, u32[]{:S(2)}) collective-permute-start(f32[64,128]{1,0:T(8,128)S(1)} %fusion.13), channel_id=1, source_target_pairs={{0,8},{8,16},{16,24},{24,32},{32,40},{40,48},{48,56},{56,64},{64,7... | collective-permute-start | bytes 98312 | tf_op jit(solution)/shard_map/ppermute | solution.py:29
  21.7 4.7 %collective-permute-start.3 = (f32[64,128]{1,0:T(8,128)S(1)}, f32[64,128]{1,0:T(8,128)S(1)}, u32[]{:S(2)}, u32[]{:S(2)}) collective-permute-start(f32[64,128]{1,0:T(8,128)S(1)} %fusion.14), channel_id=1, source_target_pairs={{8,0},{16,8},{24,16},{32,24},{40,32},{48,40},{56,48},{64,56},{72,6... | collective-permute-start | bytes 98312 | tf_op jit(solution)/shard_map/ppermute | solution.py:29
  26.9 5.8 %collective-permute-start.4 = (f32[64,128]{1,0:T(8,128)S(1)}, f32[64,128]{1,0:T(8,128)S(1)}, u32[]{:S(2)}, u32[]{:S(2)}) collective-permute-start(f32[64,128]{1,0:T(8,128)S(1)} %fusion.11), channel_id=1, source_target_pairs={{0,8},{8,16},{16,24},{24,32},{32,40},{40,48},{48,56},{56,64},{64,7... | collective-permute-start | bytes 98312 | tf_op jit(solution)/shard_map/ppermute | solution.py:29
  30.6 6.5 %collective-permute-start.5 = (f32[64,128]{1,0:T(8,128)S(1)}, f32[64,128]{1,0:T(8,128)S(1)}, u32[]{:S(2)}, u32[]{:S(2)}) collective-permute-start(f32[64,128]{1,0:T(8,128)S(1)} %fusion.12), channel_id=1, source_target_pairs={{8,0},{16,8},{24,16},{32,24},{40,32},{48,40},{56,48},{64,56},{72,6... | collective-permute-start | bytes 98312 | tf_op jit(solution)/shard_map/ppermute | solution.py:29
  32.6 4.5 %copy-start.5 = (f32[4,384,128]{2,1,0:T(8,128)S(1)}, f32[4,384,128]{2,1,0:T(8,128)}, u32[]{:S(2)}) copy-start(f32[4,384,128]{2,1,0:T(8,128)} %slice.138) | copy-start | bytes 2359300
  37.6 5.5 %collective-permute-start.6 = (f32[64,128]{1,0:T(8,128)S(1)}, f32[64,128]{1,0:T(8,128)S(1)}, u32[]{:S(2)}, u32[]{:S(2)}) collective-permute-start(f32[64,128]{1,0:T(8,128)S(1)} %fusion.9), channel_id=1, source_target_pairs={{0,8},{8,16},{16,24},{24,32},{32,40},{40,48},{48,56},{56,64},{64,7... | collective-permute-start | bytes 98312 | tf_op jit(solution)/shard_map/ppermute | solution.py:29
  41.0 5.1 %collective-permute-start.7 = (f32[64,128]{1,0:T(8,128)S(1)}, f32[64,128]{1,0:T(8,128)S(1)}, u32[]{:S(2)}, u32[]{:S(2)}) collective-permute-start(f32[64,128]{1,0:T(8,128)S(1)} %fusion.10), channel_id=1, source_target_pairs={{8,0},{16,8},{24,16},{32,24},{40,32},{48,40},{56,48},{64,56},{72,6... | collective-permute-start | bytes 98312 | tf_op jit(solution)/shard_map/ppermute | solution.py:29
  47.8 17.1 %collective-permute-start.8 = (bf16[864,128]{1,0:T(8,128)(2,1)S(1)}, bf16[864,128]{1,0:T(8,128)(2,1)S(1)}, u32[]{:S(2)}, u32[]{:S(2)}) collective-permute-start(bf16[864,128]{1,0:T(8,128)(2,1)S(1)} %get-tuple-element.33), channel_id=1, source_target_pairs={{0,2},{2,4},{4,6},{6,0},{1,3},{3,5},{5,7},{7,1},{8,10},{10,12},{12... | collective-permute-start | bytes 663560 | tf_op jit(solution)/shard_map/ppermute | solution.py:286
  60.2 14.2 %collective-permute-start.9 = (bf16[864,128]{1,0:T(8,128)(2,1)S(1)}, bf16[864,128]{1,0:T(8,128)(2,1)S(1)}, u32[]{:S(2)}, u32[]{:S(2)}) collective-permute-start(bf16[864,128]{1,0:T(8,128)(2,1)S(1)} %get-tuple-element.34), channel_id=1, source_target_pairs={{0,6},{2,0},{4,2},{6,4},{1,7},{3,1},{5,3},{7,5},{8,14},{10,8},{12,... | collective-permute-start | bytes 663560 | tf_op jit(solution)/shard_map/ppermute | solution.py:286
  64.9 12.9 %collective-permute-start.10 = (bf16[288,128]{1,0:T(8,128)(2,1)S(1)}, bf16[288,128]{1,0:T(8,128)(2,1)S(1)}, u32[]{:S(2)}, u32[]{:S(2)}) collective-permute-start(bf16[288,128]{1,0:T(8,128)(2,1)S(1)} %slice.205), channel_id=1, source_target_pairs={{0,2},{2,4},{4,6},{6,0},{1,3},{3,5},{5,7},{7,1},{8,10},{10,12},{12... | collective-permute-start | bytes 221192 | tf_op jit(solution)/shard_map/ppermute | solution.py:286
  74.4 10.0 %collective-permute-start.11 = (bf16[288,128]{1,0:T(8,128)(2,1)S(1)}, bf16[288,128]{1,0:T(8,128)(2,1)S(1)}, u32[]{:S(2)}, u32[]{:S(2)}) collective-permute-start(bf16[288,128]{1,0:T(8,128)(2,1)S(1)} %slice.206), channel_id=1, source_target_pairs={{0,6},{2,0},{4,2},{6,4},{1,7},{3,1},{5,3},{7,5},{8,14},{10,8},{12,... | collective-permute-start | bytes 221192 | tf_op jit(solution)/shard_map/ppermute | solution.py:286
  85.0 12.7 %collective-permute-start.12 = (bf16[4,576,128]{2,1,0:T(8,128)(2,1)S(1)}, bf16[4,576,128]{2,1,0:T(8,128)(2,1)S(1)}, u32[]{:S(2)}, u32[]{:S(2)}) collective-permute-start(bf16[4,576,128]{2,1,0:T(8,128)(2,1)S(1)} %collect.1.rows_ref.own_ref), channel_id=1, source_target_pairs={{0,1},{1,0},{2,3},{3,2},{4,5},{5,4},{6,7},{7,6},{8,9},{9,8},{10,11... | collective-permute-start | bytes 1769480 | tf_op jit(solution)/shard_map/ppermute | solution.py:286
  99.7 21.4 %collective-permute-start.14 = (bf16[2,4,4,2,32,128]{5,4,3,2,1,0:T(8,128)(2,1)S(1)}, bf16[2,4,4,2,32,128]{5,4,3,2,1,0:T(8,128)(2,1)S(1)}, u32[]{:S(2)}, u32[]{:S(2)}) collective-permute-start(bf16[2,4,4,2,32,128]{5,4,3,2,1,0:T(8,128)(2,1)S(1)} %get-tuple-element.43), channel_id=1, source_target_pairs={{0,24},{24,48},{48,72},{72,0},{1,25},{25,49},{49,73},{73,1},{2,26}... | collective-permute-start | bytes 1572872 | tf_op jit(solution)/shard_map/ppermute | solution.py:286
  102.7 19.2 %collective-permute-start.13 = (bf16[2,4,4,2,32,128]{5,4,3,2,1,0:T(8,128)(2,1)S(1)}, bf16[2,4,4,2,32,128]{5,4,3,2,1,0:T(8,128)(2,1)S(1)}, u32[]{:S(2)}, u32[]{:S(2)}) collective-permute-start(bf16[2,4,4,2,32,128]{5,4,3,2,1,0:T(8,128)(2,1)S(1)} %get-tuple-element.44), channel_id=1, source_target_pairs={{0,72},{24,0},{48,24},{72,48},{1,73},{25,1},{49,25},{73,49},{2,74}... | collective-permute-start | bytes 1572872 | tf_op jit(solution)/shard_map/ppermute | solution.py:286
  122.1 10.8 %collective-permute-start.15 = (bf16[4,4,2,32,128]{4,3,2,1,0:T(8,128)(2,1)S(1)}, bf16[4,4,2,32,128]{4,3,2,1,0:T(8,128)(2,1)S(1)}, u32[]{:S(2)}, u32[]{:S(2)}) collective-permute-start(bf16[4,4,2,32,128]{4,3,2,1,0:T(8,128)(2,1)S(1)} %get-tuple-element.41), channel_id=1, source_target_pairs={{0,24},{24,48},{48,72},{72,0},{1,25},{25,49},{49,73},{73,1},{2,26}... | collective-permute-start | bytes 786440 | tf_op jit(solution)/shard_map/ppermute | solution.py:286
  125.7 8.2 %collective-permute-start.16 = (bf16[4,4,2,32,128]{4,3,2,1,0:T(8,128)(2,1)S(1)}, bf16[4,4,2,32,128]{4,3,2,1,0:T(8,128)(2,1)S(1)}, u32[]{:S(2)}, u32[]{:S(2)}) collective-permute-start(bf16[4,4,2,32,128]{4,3,2,1,0:T(8,128)(2,1)S(1)} %get-tuple-element.42), channel_id=1, source_target_pairs={{0,72},{24,0},{48,24},{72,48},{1,73},{25,1},{49,25},{73,49},{2,74}... | collective-permute-start | bytes 786440 | tf_op jit(solution)/shard_map/ppermute | solution.py:286
  134.2 63.5 %copy-start.6 = (bf16[4,512,128]{2,1,0:T(8,128)(2,1)S(1)}, bf16[4,512,128]{2,1,0:T(8,128)(2,1)}, u32[]{:S(2)}) copy-start(bf16[4,512,128]{2,1,0:T(8,128)(2,1)} %get-tuple-element.37) | copy-start | bytes 1572868
  192.7 22.0 %all-to-all-start.2 = ((bf16[32,2,32,128]{3,2,1,0:T(8,128)(2,1)}), bf16[32,2,32,128]{3,2,1,0:T(8,128)(2,1)S(1)}, u32[]{:S(2)}, u32[]{:S(2)}) async-start(bf16[32,2,32,128]{3,2,1,0:T(8,128)(2,1)} %broadcast_in_dim.43), calls=%async_computation.2 | async-start | bytes 1048576 | tf_op jit(solution)/shard_map/all_to_all | solution.py:375

commit v4 on v3

--- a/solution.py
+++ b/solution.py
@@ -23,10 +23,14 @@
     return lax.dot_general(a, b, (dims, ((), ())), preferred_element_type=f32)
 
 
-def shifted(faces, up):
+def neighbours(head, tail):
     count = lax.axis_size(elem)
-    pairs = [(i, i + 1) if up else (i + 1, i) for i in range(count - 1)]
-    return lax.ppermute(faces, elem, pairs)
+    even = lax.axis_index(elem) % 2 == 0
+    swaps = []
+    for first, sent in ((1, jnp.where(even, head, tail)), (0, jnp.where(even, tail, head))):
+        pairs = [(i, i + 1) for i in range(first, count - 1, 2)]
+        swaps.append(lax.ppermute(sent, elem, pairs + [(j, i) for i, j in pairs]))
+    return jnp.where(even, swaps[1], swaps[0]), jnp.where(even, swaps[0], swaps[1])
 
 
 def vmem():
@@ -52,7 +56,8 @@
     head_ref[1] = first_ref[0, :face].astype(f32)
     cells = map_ref.shape[0]
     up = dot(selection(map_ref[cells - 1 :, :]), up_ref[0]).astype(bf16)
-    tail_ref[...] = dot(up, last_ref[0])
+    tail_ref[0] = dot(up, last_ref[0])
+    tail_ref[1] = jnp.zeros_like(tail_ref[1])
 
 
 def first_edges(cell_matrices, states, face_map):
@@ -70,11 +75,11 @@
         ],
         out_specs=[
             pl.BlockSpec((2, face, orb), lambda i: (0, 0, 0)),
-            pl.BlockSpec((face, orb), lambda i: (0, 0)),
+            pl.BlockSpec((2, face, orb), lambda i: (0, 0, 0)),
         ],
         out_shape=[
             jax.ShapeDtypeStruct((2, face, orb), f32),
-            jax.ShapeDtypeStruct((face, orb), f32),
+            jax.ShapeDtypeStruct((2, face, orb), f32),
         ],
         compiler_params=SMALL,
         name="first_edges",
@@ -117,18 +122,23 @@
     )(face_map, cell_matrices, states)
 
 
-def scatter_rows(part, out_ref, block, core, place):
-    half = out_ref.shape[1]
-    rows, cols = out_ref.shape[-2:]
-    for x in range(part.shape[0] // rows):
+def scatter_rows(part, outs, block, core, place):
+    half = outs[0].shape[1]
+    rows, cols = outs[0].shape[-2:]
+    fine = part.shape[1] // (len(outs) * cols)
+    over = 2 * half // fine
+    for x in range(part.shape[0] // (rows * over)):
         away = lax.rem(x - place + 4, 4)
         slots = (
             jnp.where(away == 0, 4, jnp.where(away == 1, 6, jnp.where(away == 2, 0, 3))),
             jnp.where(away == 0, 5, jnp.where(away == 1, 1, jnp.where(away == 2, 2, 7))),
         )
-        for y in range(2 * half):
-            tile = part[x * rows : (x + 1) * rows, y * cols : (y + 1) * cols].astype(bf16)
-            out_ref[slots[y // half], y % half, block, core] = tile
+        for m, out_ref in enumerate(outs):
+            for y in range(2 * half):
+                low = (x * over + y % over) * rows
+                left = (m * fine + y // over) * cols
+                tile = part[low : low + rows, left : left + cols].astype(bf16)
+                out_ref[slots[y // half], y % half, block, core] = tile
 
 
 def pack_kernel(where_ref, now_ref, start_ref, next_ref, own_ref, up_ref, down_ref):
@@ -210,7 +220,7 @@
         right_ref[inner:, at] = jnp.where(is_last, paired, jnp.zeros_like(paired))
 
 
-def gram_kernel(where_ref, own_ref, other_ref, right_ref, out_ref, left_ref):
+def gram_kernel(where_ref, own_ref, other_ref, right_ref, ham_ref, inter_ref, left_ref):
     blocks, total, _ = own_ref.shape
     nodes = right_ref.shape[0]
     inner = 2 * nodes - total
@@ -219,7 +229,7 @@
             left_ref[:inner] = ref[s, :inner]
             left_ref[inner:] = ref[s, nodes:]
             part = dot(left_ref[...], right_ref[...], ((0,), (0,)))
-            scatter_rows(part, out_ref, s, core, where_ref[4])
+            scatter_rows(part, (ham_ref, inter_ref), s, core, where_ref[4])
 
 
 def right_of(where, matrices, rows):
@@ -238,12 +248,13 @@
 def gram(where, own, other, right):
     blocks, _, orb = own.shape
     xs, ys, cores = lax.axis_size("x"), lax.axis_size("y"), lax.axis_size("core")
-    shape = (2 * xs, ys // 2, blocks, cores, orb // xs, 2 * blocks * orb // ys)
+    over = max(1, ys // blocks)
+    shape = (2 * xs, ys // 2, blocks, cores, orb // (xs * over), over * blocks * orb // ys)
     return pl.pallas_call(
         gram_kernel,
         in_specs=[smem(), vmem(), vmem(), vmem()],
-        out_specs=vmem(),
-        out_shape=jax.ShapeDtypeStruct(shape, bf16),
+        out_specs=[vmem(), vmem()],
+        out_shape=[jax.ShapeDtypeStruct(shape, bf16)] * 2,
         scratch_shapes=[pltpu.VMEM((right.shape[0], orb), bf16)],
         compiler_params=SMALL,
         name="gram",
@@ -251,22 +262,22 @@
 
 
 def assemble_kernel(scale, pieces_ref, ham_ref, inter_ref):
-    ys, xs, cores, sub, cols = pieces_ref.shape
-    orb = sub * xs
-    for out_ref, half in ((ham_ref, 0), (inter_ref, 1)):
-        for y in range(ys // 2):
-            for k in range(cols // orb):
-                zh = y * cols // orb + k
-                for c in range(cores):
-                    for x in range(xs):
-                        tile = pieces_ref[half * ys // 2 + y, x, c, :, k * orb : (k + 1) * orb]
-                        at = (zh * cores + c) * orb
-                        out_ref[x * sub : (x + 1) * sub, at : at + orb] = tile.astype(f32) * scale
-
-
-def assemble(pieces, scale):
-    ys, xs, cores, sub, cols = pieces.shape
-    out = jax.ShapeDtypeStruct((sub * xs, ys * cores * cols // 2), f32)
+    ys, xs, cores, _, sub, cols = pieces_ref.shape
+    over = ham_ref.shape[0] // (sub * xs)
+    for m, out_ref in enumerate((ham_ref, inter_ref)):
+        for y in range(ys):
+            for c in range(cores):
+                for x in range(xs):
+                    for k in range(cols // 128):
+                        tile = pieces_ref[y, x, c, m, :, k * 128 : (k + 1) * 128]
+                        low = (x * over + y % over) * sub
+                        left = ((y // over * cols // 128 + k) * cores + c) * 128
+                        out_ref[low : low + sub, left : left + 128] = tile.astype(f32) * scale
+
+
+def assemble(pieces, scale, orb):
+    ys, xs, cores, _, sub, cols = pieces.shape
+    out = jax.ShapeDtypeStruct((orb, ys * xs * cores * sub * cols // orb), f32)
     return pl.pallas_call(
         lambda *refs: assemble_kernel(scale, *refs),
         in_specs=[vmem()],
@@ -313,8 +324,7 @@
     cell_matrices, initial_states, head, tail = lax.optimization_barrier(
         (cell_matrices, initial_states, head, tail)
     )
-    both = shifted(head, False)
-    from_below = shifted(tail, True)
+    above, from_below = neighbours(head, tail)
     matrices, current_b, start, products = reordered(cell_matrices, initial_states, face_map)
 
     def edges(values):
@@ -325,12 +335,11 @@
 
     previous = start
     current = start
-    from_above, next_start = both[0], both[1]
+    from_above, next_start, from_below = above[0], above[1], from_below[0]
     for degree in range(PASSES):
         if degree > 0:
             head, tail = edges(current_b)
-            from_above = shifted(head, False)
-            from_below = shifted(tail, True)
+            from_above, from_below = neighbours(head, tail)
             current_b, head, tail = lax.optimization_barrier((current_b, head, tail))
             products = jnp.einsum("cij,cjo->cio", matrices, current_b, preferred_element_type=f32)
         from_next = jnp.concatenate([products[1:, :face], from_above[None]], 0)
@@ -364,17 +373,16 @@
     rows = collect(where, own, below, above, low_half, high_half)
     other = ring(rows, "core", 1)
     right = right_of(where, matrices, rows)
-    part = gram(where, rows, other, right)
-    part = x_sum(part)
-    part = swap_sum(part, "y")
-    sub, cols = part.shape[2:]
-    column = jnp.broadcast_to(part[None], (zls,) + part.shape).reshape(-1, sub, cols)
+    parts = gram(where, rows, other, right)
+    parts = [swap_sum(x_sum(part), "y") for part in parts]
+    part = jnp.stack(parts, 2)
+    column = jnp.broadcast_to(part[None], (zls,) + part.shape).reshape((-1,) + part.shape[2:])
     column = lax.all_to_all(column, ("zl", "zh", "core"), split_axis=0, concat_axis=0, tiled=True)
-    piece = summed(column.reshape(zls * zhs, cores, sub, cols))
+    piece = summed(column.reshape((zls * zhs, cores) + part.shape[2:]))
     pieces = jnp.broadcast_to(piece[None], (ys * xs,) + piece.shape)
     pieces = lax.all_to_all(pieces, ("y", "x"), split_axis=0, concat_axis=0, tiled=True)
     scale = 1.0 / (cells_dev * elems * nodes)
-    hamiltonian, intersection = assemble(pieces.reshape(ys, xs, cores, sub, cols), scale)
+    hamiltonian, intersection = assemble(pieces.reshape((ys, xs) + piece.shape), scale, orb_dev)
 
     onehot = (face_map[:, :, None] == jnp.arange(face, dtype=jnp.int32)[None, None, :]).astype(bf16)
     upper = jnp.einsum("cfm,cmo->cfo", onehot, current_b[:, -face:], preferred_element_type=f32)

time: 217 us -> 213 us (0.982)
  blocking collectives: 57.4 us -> 27.4 us
  starting transfers between devices: 84.3 us -> 111 us
  waiting for transfers between devices: 50.1 us -> 45.8 us
    all_to_all x1 -> x0, blocking collectives: 27.9 us -> none  [swap_sum(): lax.all_to_all(part, axis, split_axis=0, concat_axis=0, tiled=True)]
    all_to_all x0 -> x2, waiting for transfers between devices: none -> 17.7 us  [swap_sum(): lax.all_to_all(part, axis, split_axis=0, concat_axis=0, tiled=True)]
    ppermute x9 -> x13, waiting for transfers between devices: 24.1 us -> 10.5 us  [ring(): lax.ppermute(part, axis, [(i, (i + step) % count) for i in range(count)])]
    all_to_all x0 -> x2, starting transfers between devices: none -> 11.1 us  [swap_sum(): lax.all_to_all(part, axis, split_axis=0, concat_axis=0, tiled=True)]
    ppermute x9 -> x13, starting transfers between devices: 57.8 us -> 68.3 us  [ring(): lax.ppermute(part, axis, [(i, (i + step) % count) for i in range(count)])]
    ppermute x8, waiting for transfers between devices: 10.1 us -> 1.45 us  [neighbours(): swaps.append(lax.ppermute(sent, elem, pairs + [(j, i) for i, j in pairs]))]
    ppermute x8, starting transfers between devices: 21.5 us -> 27.8 us  [neighbours(): swaps.append(lax.ppermute(sent, elem, pairs + [(j, i) for i, j in pairs]))]
  transfers between devices with their start and end apart: 18 -> 24, of which waited for: 13 -> 9; matrix products, arithmetic and copies ran while one was open for 2% -> 4% of each run, Pallas kernels for 2% -> 2%
where the time goes in v4:
time: 213 us; the launch traced here: 212 us
  starting transfers between devices  111 us (52%)
  waiting for transfers between devices  45.8 us (22%)
  blocking collectives  27.4 us (13%)
  local copies, waits for them, and re-layouts  8.25 us (4%)
  Pallas kernels  7.81 us (4%)
  other arithmetic  7.25 us (3%)
  matrix products  3.29 us (2%)
    ppermute x13, starting transfers between devices, ring(): lax.ppermute(part, axis, [(i, (i + step) % count) for i in range(count)])  68.3 us
    ppermute x8, starting transfers between devices, neighbours(): swaps.append(lax.ppermute(sent, elem, pairs + [(j, i) for i, j in pairs]))  27.8 us
    all_to_all x1, blocking collectives, local(): lax.all_to_all(column, ('zl', 'zh', 'core'), split_axis=0, concat_axis=0,...  27.4 us
    all_to_all x2, waiting for transfers between devices, swap_sum(): lax.all_to_all(part, axis, split_axis=0, concat_axis=0, tiled=True)  17.7 us
    all_to_all x1, waiting for transfers between devices, local(): lax.all_to_all(pieces, ('y', 'x'), split_axis=0, concat_axis=0, tiled=True)  16.2 us
    all_to_all x2, starting transfers between devices, swap_sum(): lax.all_to_all(part, axis, split_axis=0, concat_axis=0, tiled=True)  11.1 us
    ppermute x13, waiting for transfers between devices, ring(): lax.ppermute(part, axis, [(i, (i + step) % count) for i in range(count)])  10.5 us
    unnamed x14, local copies, waits for them, and re-layouts  4.82 us
  transfers between devices with their start and end apart: 24, of which 9 were waited for; matrix products, arithmetic and copies ran while one was open for 4% of the time, Pallas kernels for 2%

profile of v4, /device:TPU:1, one launch (start us, length us, event | category | flops | bytes accessed | tf_op | source)
XLA Modules:
  0.0 212.2 jit_solution(6713100570878035553)
XLA Ops:
  0.7 1.6 copy-done
  2.3 1.0 copy-done.1
  3.3 0.7 copy-done.3
  5.6 8.2 %collective-permute-start.1 = (f32[2,64,128]{2,1,0:T(8,128)S(1)}, f32[2,64,128]{2,1,0:T(8,128)S(1)}, u32[]{:S(2)}, u32[]{:S(2)}) collective-permute-start(f32[2,64,128]{2,1,0:T(8,128)S(1)} %get-tuple-element.72), channel_id=1, source_target_pairs={{0,8},{16,24},{32,40},{48,56},{64,72},{80,88},{96,104},{112,120},{... | collective-permute-start | bytes 196616 | tf_op jit(solution)/shard_map/ppermute | solution.py:32
  13.8 2.1 reorder.1
  15.9 1.0 copy-done.2
  16.9 2.1 slice.172
  19.1 1.0 maximum_add_fusion
  20.1 1.3 fusion.4
  21.7 0.7 collective-permute-start.2
  22.3 4.6 %collective-permute-start.3 = (f32[64,128]{1,0:T(8,128)S(1)}, f32[64,128]{1,0:T(8,128)S(1)}, u32[]{:S(2)}, u32[]{:S(2)}) collective-permute-start(f32[64,128]{1,0:T(8,128)S(1)} %get-tuple-element.86), channel_id=1, source_target_pairs={{0,8},{16,24},{32,40},{48,56},{64,72},{80,88},{96,104},{112,120},{... | collective-permute-start | bytes 98312 | tf_op jit(solution)/shard_map/ppermute | solution.py:32
  27.0 0.7 fusion.42
  28.8 0.7 collective-permute-start.4
  29.4 6.4 %collective-permute-start.5 = (f32[64,128]{1,0:T(8,128)S(1)}, f32[64,128]{1,0:T(8,128)S(1)}, u32[]{:S(2)}, u32[]{:S(2)}) collective-permute-start(f32[64,128]{1,0:T(8,128)S(1)} %get-tuple-element.82), channel_id=1, source_target_pairs={{0,8},{16,24},{32,40},{48,56},{64,72},{80,88},{96,104},{112,120},{... | collective-permute-start | bytes 98312 | tf_op jit(solution)/shard_map/ppermute | solution.py:32
  35.9 0.7 fusion.43
  38.2 0.7 collective-permute-start.6
  38.9 5.9 %collective-permute-start.7 = (f32[64,128]{1,0:T(8,128)S(1)}, f32[64,128]{1,0:T(8,128)S(1)}, u32[]{:S(2)}, u32[]{:S(2)}) collective-permute-start(f32[64,128]{1,0:T(8,128)S(1)} %get-tuple-element.78), channel_id=1, source_target_pairs={{0,8},{16,24},{32,40},{48,56},{64,72},{80,88},{96,104},{112,120},{... | collective-permute-start | bytes 98312 | tf_op jit(solution)/shard_map/ppermute | solution.py:32
  44.8 0.7 fusion.44
  46.2 1.1 fusion.34
  47.9 12.6 %collective-permute-start.8 = (bf16[864,128]{1,0:T(8,128)(2,1)S(1)}, bf16[864,128]{1,0:T(8,128)(2,1)S(1)}, u32[]{:S(2)}, u32[]{:S(2)}) collective-permute-start(bf16[864,128]{1,0:T(8,128)(2,1)S(1)} %get-tuple-element.35), channel_id=1, source_target_pairs={{0,2},{2,4},{4,6},{6,0},{1,3},{3,5},{5,7},{7,1},{8,10},{10,12},{12... | collective-permute-start | bytes 663560 | tf_op jit(solution)/shard_map/ppermute | solution.py:297
  60.4 3.1 %collective-permute-start.9 = (bf16[864,128]{1,0:T(8,128)(2,1)S(1)}, bf16[864,128]{1,0:T(8,128)(2,1)S(1)}, u32[]{:S(2)}, u32[]{:S(2)}) collective-permute-start(bf16[864,128]{1,0:T(8,128)(2,1)S(1)} %get-tuple-element.36), channel_id=1, source_target_pairs={{0,6},{2,0},{4,2},{6,4},{1,7},{3,1},{5,3},{7,5},{8,14},{10,8},{12,... | collective-permute-start | bytes 663560 | tf_op jit(solution)/shard_map/ppermute | solution.py:297
  63.5 1.6 collective-permute-done.8.below_ref
  65.1 14.5 %collective-permute-start.10 = (bf16[288,128]{1,0:T(8,128)(2,1)S(1)}, bf16[288,128]{1,0:T(8,128)(2,1)S(1)}, u32[]{:S(2)}, u32[]{:S(2)}) collective-permute-start(bf16[288,128]{1,0:T(8,128)(2,1)S(1)} %slice.251), channel_id=1, source_target_pairs={{0,2},{2,4},{4,6},{6,0},{1,3},{3,5},{5,7},{7,1},{8,10},{10,12},{12... | collective-permute-start | bytes 221192 | tf_op jit(solution)/shard_map/ppermute | solution.py:297
  79.6 1.9 collective-permute-start.11
  81.6 8.5 %collective-permute-done.11.high_half_ref = bf16[288,128]{1,0:T(8,128)(2,1)S(1)} collective-permute-done((bf16[288,128]{1,0:T(8,128)(2,1)S(1)}, bf16[288,128]{1,0:T(8,128)(2,1)S(1)}, u32[]{:S(2)}, u32[]{:S(2)}) %collective-permute-start.11) | collective-permute-done | bytes 73760 | tf_op jit(solution)/shard_map/ppermute | solution.py:297
  90.7 6.1 %collective-permute-start.12 = (bf16[4,576,128]{2,1,0:T(8,128)(2,1)S(1)}, bf16[4,576,128]{2,1,0:T(8,128)(2,1)S(1)}, u32[]{:S(2)}, u32[]{:S(2)}) collective-permute-start(bf16[4,576,128]{2,1,0:T(8,128)(2,1)S(1)} %collect.1.rows_ref.own_ref), channel_id=1, source_target_pairs={{0,1},{1,0},{2,3},{3,2},{4,5},{5,4},{6,7},{7,6},{8,9},{9,8},{10,11... | collective-permute-start | bytes 1769480 | tf_op jit(solution)/shard_map/ppermute | solution.py:297
  96.8 1.3 right.1.right_ref
  98.4 1.9 gram.1
  100.4 3.2 %collective-permute-start.14 = (bf16[2,4,4,2,16,128]{5,4,3,2,1,0:T(8,128)(2,1)S(1)}, bf16[2,4,4,2,16,128]{5,4,3,2,1,0:T(8,128)(2,1)S(1)}, u32[]{:S(2)}, u32[]{:S(2)}) collective-permute-start(bf16[2,4,4,2,16,128]{5,4,3,2,1,0:T(8,128)(2,1)S(1)} %get-tuple-element.47), channel_id=1, source_target_pairs={{0,24},{24,48},{48,72},{72,0},{1,25},{25,49},{49,73},{73,1},{2,26}... | collective-permute-start | bytes 786440 | tf_op jit(solution)/shard_map/ppermute | solution.py:297
  103.6 7.5 %collective-permute-start.13 = (bf16[2,4,4,2,16,128]{5,4,3,2,1,0:T(8,128)(2,1)S(1)}, bf16[2,4,4,2,16,128]{5,4,3,2,1,0:T(8,128)(2,1)S(1)}, u32[]{:S(2)}, u32[]{:S(2)}) collective-permute-start(bf16[2,4,4,2,16,128]{5,4,3,2,1,0:T(8,128)(2,1)S(1)} %get-tuple-element.48), channel_id=1, source_target_pairs={{0,72},{24,0},{48,24},{72,48},{1,73},{25,1},{49,25},{73,49},{2,74}... | collective-permute-start | bytes 786440 | tf_op jit(solution)/shard_map/ppermute | solution.py:297
  111.1 1.9 collective-permute-start.18
  113.0 4.6 %collective-permute-start.17 = (bf16[2,4,4,2,16,128]{5,4,3,2,1,0:T(8,128)(2,1)S(1)}, bf16[2,4,4,2,16,128]{5,4,3,2,1,0:T(8,128)(2,1)S(1)}, u32[]{:S(2)}, u32[]{:S(2)}) collective-permute-start(bf16[2,4,4,2,16,128]{5,4,3,2,1,0:T(8,128)(2,1)S(1)} %get-tuple-element.54), channel_id=1, source_target_pairs={{0,72},{24,0},{48,24},{72,48},{1,73},{25,1},{49,25},{73,49},{2,74}... | collective-permute-start | bytes 786440 | tf_op jit(solution)/shard_map/ppermute | solution.py:297
  117.7 2.2 %collective-permute-start.15 = (bf16[4,4,2,16,128]{4,3,2,1,0:T(8,128)(2,1)S(1)}, bf16[4,4,2,16,128]{4,3,2,1,0:T(8,128)(2,1)S(1)}, u32[]{:S(2)}, u32[]{:S(2)}) collective-permute-start(bf16[4,4,2,16,128]{4,3,2,1,0:T(8,128)(2,1)S(1)} %get-tuple-element.45), channel_id=1, source_target_pairs={{0,24},{24,48},{48,72},{72,0},{1,25},{25,49},{49,73},{73,1},{2,26}... | collective-permute-start | bytes 393224 | tf_op jit(solution)/shard_map/ppermute | solution.py:297
  119.9 4.3 %collective-permute-start.16 = (bf16[4,4,2,16,128]{4,3,2,1,0:T(8,128)(2,1)S(1)}, bf16[4,4,2,16,128]{4,3,2,1,0:T(8,128)(2,1)S(1)}, u32[]{:S(2)}, u32[]{:S(2)}) collective-permute-start(bf16[4,4,2,16,128]{4,3,2,1,0:T(8,128)(2,1)S(1)} %get-tuple-element.46), channel_id=1, source_target_pairs={{0,72},{24,0},{48,24},{72,48},{1,73},{25,1},{49,25},{73,49},{2,74}... | collective-permute-start | bytes 393224 | tf_op jit(solution)/shard_map/ppermute | solution.py:297
  124.3 1.9 collective-permute-start.19
  126.3 4.6 %collective-permute-start.20 = (bf16[4,4,2,16,128]{4,3,2,1,0:T(8,128)(2,1)S(1)}, bf16[4,4,2,16,128]{4,3,2,1,0:T(8,128)(2,1)S(1)}, u32[]{:S(2)}, u32[]{:S(2)}) collective-permute-start(bf16[4,4,2,16,128]{4,3,2,1,0:T(8,128)(2,1)S(1)} %get-tuple-element.52), channel_id=1, source_target_pairs={{0,72},{24,0},{48,24},{72,48},{1,73},{25,1},{49,25},{73,49},{2,74}... | collective-permute-start | bytes 393224 | tf_op jit(solution)/shard_map/ppermute | solution.py:297
  131.0 0.7 pad_maximum_fusion.1
  131.7 7.7 %all-to-all-start = ((bf16[8,4,2,16,128]{4,3,2,1,0:T(8,128)(2,1)}), bf16[8,4,2,16,128]{4,3,2,1,0:T(8,128)(2,1)S(1)}, u32[]{:S(2)}, u32[]{:S(2)}) async-start(bf16[8,4,2,16,128]{4,3,2,1,0:T(8,128)(2,1)} %pad_maximum_fusion.1), calls=%async_computation | async-start | bytes 524288 | tf_op jit(solution)/shard_map/all_to_all | solution.py:313
  139.5 0.7 pad_maximum_fusion.2
  140.3 8.5 %all-to-all-done = bf16[8,4,2,16,128]{4,3,2,1,0:T(8,128)(2,1)S(1)} async-done(((bf16[8,4,2,16,128]{4,3,2,1,0:T(8,128)(2,1)}), bf16[8,4,2,16,128]{4,3,2,1,0:T(8,128)(2,1)S(1)}, u32[]{:S(2)}, u32[]{:S(2)}) %all-to-all-start) | async-done | bytes 262176 | tf_op jit(solution)/shard_map/all_to_all | solution.py:313
  148.8 3.4 %all-to-all-start.1 = ((bf16[8,4,2,16,128]{4,3,2,1,0:T(8,128)(2,1)}), bf16[8,4,2,16,128]{4,3,2,1,0:T(8,128)(2,1)S(1)}, u32[]{:S(2)}, u32[]{:S(2)}) async-start(bf16[8,4,2,16,128]{4,3,2,1,0:T(8,128)(2,1)} %pad_maximum_fusion.2), calls=%async_computation.1 | async-start | bytes 524288 | tf_op jit(solution)/shard_map/all_to_all | solution.py:313
  152.2 9.2 %all-to-all-done.1 = bf16[8,4,2,16,128]{4,3,2,1,0:T(8,128)(2,1)S(1)} async-done(((bf16[8,4,2,16,128]{4,3,2,1,0:T(8,128)(2,1)}), bf16[8,4,2,16,128]{4,3,2,1,0:T(8,128)(2,1)S(1)}, u32[]{:S(2)}, u32[]{:S(2)}) %all-to-all-start.1) | async-done | bytes 262176 | tf_op jit(solution)/shard_map/all_to_all | solution.py:313
  161.6 27.4 %all_to_all.20 = bf16[24,2,16,128]{3,2,1,0:T(8,128)(2,1)S(1)} all-to-all(bf16[24,2,16,128]{3,2,1,0:T(8,128)(2,1)S(1)} %bitcast.100), channel_id=1, replica_groups=mesh['y'=8,'x'=4,'zl'=3,'zh'=4,'core'=2] {'zl','zh','core'}, dimensions={0} | all-to-all | bytes 393216 | tf_op jit(solution)/shard_map/all_to_all | solution.py:380
  189.0 0.9 broadcast_in_dim.39
  189.9 3.9 %all-to-all-start.3 = ((bf16[32,2,2,16,128]{4,3,2,1,0:T(8,128)(2,1)}), bf16[32,2,2,16,128]{4,3,2,1,0:T(8,128)(2,1)S(1)}, u32[]{:S(2)}, u32[]{:S(2)}) async-start(bf16[32,2,2,16,128]{4,3,2,1,0:T(8,128)(2,1)} %broadcast_in_dim.39), calls=%async_computation.3 | async-start | bytes 1048576 | tf_op jit(solution)/shard_map/all_to_all | solution.py:383
  194.1 0.8 pad_maximum_fusion
  194.9 16.2 %all-to-all-done.3 = bf16[32,2,2,16,128]{4,3,2,1,0:T(8,128)(2,1)S(1)} async-done(((bf16[32,2,2,16,128]{4,3,2,1,0:T(8,128)(2,1)}), bf16[32,2,2,16,128]{4,3,2,1,0:T(8,128)(2,1)S(1)}, u32[]{:S(2)}, u32[]{:S(2)}) %all-to-all-start.3) | async-done | bytes 524320 | tf_op jit(solution)/shard_map/all_to_all | solution.py:383
  211.1 1.0 assemble.1
  (73 shorter events, 7.7 us)
Async XLA Ops:
  0.7 1.6 copy-start
  2.2 1.0 copy-start.1
  3.3 0.7 copy-start.3
  4.0 9.8 %copy-start.4 = (s32[4,64]{1,0:T(4,128)S(1)}, s32[4,64]{1,0:T(4,128)}, u32[]{:S(2)}) copy-start(s32[4,64]{1,0:T(4,128)} %map_ref.3) | copy-start | bytes 3076
  4.9 14.1 %collective-permute-start = (f32[2,64,128]{2,1,0:T(8,128)}, f32[2,64,128]{2,1,0:T(8,128)S(1)}, u32[]{:S(2)}, u32[]{:S(2)}) collective-permute-start(f32[2,64,128]{2,1,0:T(8,128)} %get-tuple-element.71), channel_id=1, source_target_pairs={{8,16},{24,32},{40,48},{56,64},{72,80},{88,96},{104,112},{120,128}... | collective-permute-start | bytes 196616 | tf_op jit(solution)/shard_map/ppermute | solution.py:32
  5.6 13.5 %collective-permute-start.1 = (f32[2,64,128]{2,1,0:T(8,128)S(1)}, f32[2,64,128]{2,1,0:T(8,128)S(1)}, u32[]{:S(2)}, u32[]{:S(2)}) collective-permute-start(f32[2,64,128]{2,1,0:T(8,128)S(1)} %get-tuple-element.72), channel_id=1, source_target_pairs={{0,8},{16,24},{32,40},{48,56},{64,72},{80,88},{96,104},{112,120},{... | collective-permute-start | bytes 196616 | tf_op jit(solution)/shard_map/ppermute | solution.py:32
  15.9 1.0 copy-start.2
  21.7 6.1 %collective-permute-start.2 = (f32[64,128]{1,0:T(8,128)S(1)}, f32[64,128]{1,0:T(8,128)S(1)}, u32[]{:S(2)}, u32[]{:S(2)}) collective-permute-start(f32[64,128]{1,0:T(8,128)S(1)} %get-tuple-element.85), channel_id=1, source_target_pairs={{8,16},{24,32},{40,48},{56,64},{72,80},{88,96},{104,112},{120,128}... | collective-permute-start | bytes 98312 | tf_op jit(solution)/shard_map/ppermute | solution.py:32
  22.3 5.9 %collective-permute-start.3 = (f32[64,128]{1,0:T(8,128)S(1)}, f32[64,128]{1,0:T(8,128)S(1)}, u32[]{:S(2)}, u32[]{:S(2)}) collective-permute-start(f32[64,128]{1,0:T(8,128)S(1)} %get-tuple-element.86), channel_id=1, source_target_pairs={{0,8},{16,24},{32,40},{48,56},{64,72},{80,88},{96,104},{112,120},{... | collective-permute-start | bytes 98312 | tf_op jit(solution)/shard_map/ppermute | solution.py:32
  28.8 7.9 %collective-permute-start.4 = (f32[64,128]{1,0:T(8,128)S(1)}, f32[64,128]{1,0:T(8,128)S(1)}, u32[]{:S(2)}, u32[]{:S(2)}) collective-permute-start(f32[64,128]{1,0:T(8,128)S(1)} %get-tuple-element.81), channel_id=1, source_target_pairs={{8,16},{24,32},{40,48},{56,64},{72,80},{88,96},{104,112},{120,128}... | collective-permute-start | bytes 98312 | tf_op jit(solution)/shard_map/ppermute | solution.py:32
  29.4 7.7 %collective-permute-start.5 = (f32[64,128]{1,0:T(8,128)S(1)}, f32[64,128]{1,0:T(8,128)S(1)}, u32[]{:S(2)}, u32[]{:S(2)}) collective-permute-start(f32[64,128]{1,0:T(8,128)S(1)} %get-tuple-element.82), channel_id=1, source_target_pairs={{0,8},{16,24},{32,40},{48,56},{64,72},{80,88},{96,104},{112,120},{... | collective-permute-start | bytes 98312 | tf_op jit(solution)/shard_map/ppermute | solution.py:32
  36.6 1.1 copy-start.5
  38.2 7.4 %collective-permute-start.6 = (f32[64,128]{1,0:T(8,128)S(1)}, f32[64,128]{1,0:T(8,128)S(1)}, u32[]{:S(2)}, u32[]{:S(2)}) collective-permute-start(f32[64,128]{1,0:T(8,128)S(1)} %get-tuple-element.77), channel_id=1, source_target_pairs={{8,16},{24,32},{40,48},{56,64},{72,80},{88,96},{104,112},{120,128}... | collective-permute-start | bytes 98312 | tf_op jit(solution)/shard_map/ppermute | solution.py:32
  38.9 7.2 %collective-permute-start.7 = (f32[64,128]{1,0:T(8,128)S(1)}, f32[64,128]{1,0:T(8,128)S(1)}, u32[]{:S(2)}, u32[]{:S(2)}) collective-permute-start(f32[64,128]{1,0:T(8,128)S(1)} %get-tuple-element.78), channel_id=1, source_target_pairs={{0,8},{16,24},{32,40},{48,56},{64,72},{80,88},{96,104},{112,120},{... | collective-permute-start | bytes 98312 | tf_op jit(solution)/shard_map/ppermute | solution.py:32
  47.9 17.2 %collective-permute-start.8 = (bf16[864,128]{1,0:T(8,128)(2,1)S(1)}, bf16[864,128]{1,0:T(8,128)(2,1)S(1)}, u32[]{:S(2)}, u32[]{:S(2)}) collective-permute-start(bf16[864,128]{1,0:T(8,128)(2,1)S(1)} %get-tuple-element.35), channel_id=1, source_target_pairs={{0,2},{2,4},{4,6},{6,0},{1,3},{3,5},{5,7},{7,1},{8,10},{10,12},{12... | collective-permute-start | bytes 663560 | tf_op jit(solution)/shard_map/ppermute | solution.py:297
  60.4 19.2 %collective-permute-start.9 = (bf16[864,128]{1,0:T(8,128)(2,1)S(1)}, bf16[864,128]{1,0:T(8,128)(2,1)S(1)}, u32[]{:S(2)}, u32[]{:S(2)}) collective-permute-start(bf16[864,128]{1,0:T(8,128)(2,1)S(1)} %get-tuple-element.36), channel_id=1, source_target_pairs={{0,6},{2,0},{4,2},{6,4},{1,7},{3,1},{5,3},{7,5},{8,14},{10,8},{12,... | collective-permute-start | bytes 663560 | tf_op jit(solution)/shard_map/ppermute | solution.py:297
  65.1 16.5 %collective-permute-start.10 = (bf16[288,128]{1,0:T(8,128)(2,1)S(1)}, bf16[288,128]{1,0:T(8,128)(2,1)S(1)}, u32[]{:S(2)}, u32[]{:S(2)}) collective-permute-start(bf16[288,128]{1,0:T(8,128)(2,1)S(1)} %slice.251), channel_id=1, source_target_pairs={{0,2},{2,4},{4,6},{6,0},{1,3},{3,5},{5,7},{7,1},{8,10},{10,12},{12... | collective-permute-start | bytes 221192 | tf_op jit(solution)/shard_map/ppermute | solution.py:297
  79.6 10.5 %collective-permute-start.11 = (bf16[288,128]{1,0:T(8,128)(2,1)S(1)}, bf16[288,128]{1,0:T(8,128)(2,1)S(1)}, u32[]{:S(2)}, u32[]{:S(2)}) collective-permute-start(bf16[288,128]{1,0:T(8,128)(2,1)S(1)} %slice.252), channel_id=1, source_target_pairs={{0,6},{2,0},{4,2},{6,4},{1,7},{3,1},{5,3},{7,5},{8,14},{10,8},{12,... | collective-permute-start | bytes 221192 | tf_op jit(solution)/shard_map/ppermute | solution.py:297
  90.7 7.8 %collective-permute-start.12 = (bf16[4,576,128]{2,1,0:T(8,128)(2,1)S(1)}, bf16[4,576,128]{2,1,0:T(8,128)(2,1)S(1)}, u32[]{:S(2)}, u32[]{:S(2)}) collective-permute-start(bf16[4,576,128]{2,1,0:T(8,128)(2,1)S(1)} %collect.1.rows_ref.own_ref), channel_id=1, source_target_pairs={{0,1},{1,0},{2,3},{3,2},{4,5},{5,4},{6,7},{7,6},{8,9},{9,8},{10,11... | collective-permute-start | bytes 1769480 | tf_op jit(solution)/shard_map/ppermute | solution.py:297
  100.4 17.2 %collective-permute-start.14 = (bf16[2,4,4,2,16,128]{5,4,3,2,1,0:T(8,128)(2,1)S(1)}, bf16[2,4,4,2,16,128]{5,4,3,2,1,0:T(8,128)(2,1)S(1)}, u32[]{:S(2)}, u32[]{:S(2)}) collective-permute-start(bf16[2,4,4,2,16,128]{5,4,3,2,1,0:T(8,128)(2,1)S(1)} %get-tuple-element.47), channel_id=1, source_target_pairs={{0,24},{24,48},{48,72},{72,0},{1,25},{25,49},{49,73},{73,1},{2,26}... | collective-permute-start | bytes 786440 | tf_op jit(solution)/shard_map/ppermute | solution.py:297
  103.6 14.0 %collective-permute-start.13 = (bf16[2,4,4,2,16,128]{5,4,3,2,1,0:T(8,128)(2,1)S(1)}, bf16[2,4,4,2,16,128]{5,4,3,2,1,0:T(8,128)(2,1)S(1)}, u32[]{:S(2)}, u32[]{:S(2)}) collective-permute-start(bf16[2,4,4,2,16,128]{5,4,3,2,1,0:T(8,128)(2,1)S(1)} %get-tuple-element.48), channel_id=1, source_target_pairs={{0,72},{24,0},{48,24},{72,48},{1,73},{25,1},{49,25},{73,49},{2,74}... | collective-permute-start | bytes 786440 | tf_op jit(solution)/shard_map/ppermute | solution.py:297
  111.1 13.1 %collective-permute-start.18 = (bf16[2,4,4,2,16,128]{5,4,3,2,1,0:T(8,128)(2,1)S(1)}, bf16[2,4,4,2,16,128]{5,4,3,2,1,0:T(8,128)(2,1)S(1)}, u32[]{:S(2)}, u32[]{:S(2)}) collective-permute-start(bf16[2,4,4,2,16,128]{5,4,3,2,1,0:T(8,128)(2,1)S(1)} %get-tuple-element.53), channel_id=1, source_target_pairs={{0,24},{24,48},{48,72},{72,0},{1,25},{25,49},{49,73},{73,1},{2,26}... | collective-permute-start | bytes 786440 | tf_op jit(solution)/shard_map/ppermute | solution.py:297
  113.0 11.2 %collective-permute-start.17 = (bf16[2,4,4,2,16,128]{5,4,3,2,1,0:T(8,128)(2,1)S(1)}, bf16[2,4,4,2,16,128]{5,4,3,2,1,0:T(8,128)(2,1)S(1)}, u32[]{:S(2)}, u32[]{:S(2)}) collective-permute-start(bf16[2,4,4,2,16,128]{5,4,3,2,1,0:T(8,128)(2,1)S(1)} %get-tuple-element.54), channel_id=1, source_target_pairs={{0,72},{24,0},{48,24},{72,48},{1,73},{25,1},{49,25},{73,49},{2,74}... | collective-permute-start | bytes 786440 | tf_op jit(solution)/shard_map/ppermute | solution.py:297
  117.7 13.1 %collective-permute-start.15 = (bf16[4,4,2,16,128]{4,3,2,1,0:T(8,128)(2,1)S(1)}, bf16[4,4,2,16,128]{4,3,2,1,0:T(8,128)(2,1)S(1)}, u32[]{:S(2)}, u32[]{:S(2)}) collective-permute-start(bf16[4,4,2,16,128]{4,3,2,1,0:T(8,128)(2,1)S(1)} %get-tuple-element.45), channel_id=1, source_target_pairs={{0,24},{24,48},{48,72},{72,0},{1,25},{25,49},{49,73},{73,1},{2,26}... | collective-permute-start | bytes 393224 | tf_op jit(solution)/shard_map/ppermute | solution.py:297
  119.9 10.9 %collective-permute-start.16 = (bf16[4,4,2,16,128]{4,3,2,1,0:T(8,128)(2,1)S(1)}, bf16[4,4,2,16,128]{4,3,2,1,0:T(8,128)(2,1)S(1)}, u32[]{:S(2)}, u32[]{:S(2)}) collective-permute-start(bf16[4,4,2,16,128]{4,3,2,1,0:T(8,128)(2,1)S(1)} %get-tuple-element.46), channel_id=1, source_target_pairs={{0,72},{24,0},{48,24},{72,48},{1,73},{25,1},{49,25},{73,49},{2,74}... | collective-permute-start | bytes 393224 | tf_op jit(solution)/shard_map/ppermute | solution.py:297
  124.3 15.1 %collective-permute-start.19 = (bf16[4,4,2,16,128]{4,3,2,1,0:T(8,128)(2,1)S(1)}, bf16[4,4,2,16,128]{4,3,2,1,0:T(8,128)(2,1)S(1)}, u32[]{:S(2)}, u32[]{:S(2)}) collective-permute-start(bf16[4,4,2,16,128]{4,3,2,1,0:T(8,128)(2,1)S(1)} %get-tuple-element.51), channel_id=1, source_target_pairs={{0,24},{24,48},{48,72},{72,0},{1,25},{25,49},{49,73},{73,1},{2,26}... | collective-permute-start | bytes 393224 | tf_op jit(solution)/shard_map/ppermute | solution.py:297
  126.3 13.1 %collective-permute-start.20 = (bf16[4,4,2,16,128]{4,3,2,1,0:T(8,128)(2,1)S(1)}, bf16[4,4,2,16,128]{4,3,2,1,0:T(8,128)(2,1)S(1)}, u32[]{:S(2)}, u32[]{:S(2)}) collective-permute-start(bf16[4,4,2,16,128]{4,3,2,1,0:T(8,128)(2,1)S(1)} %get-tuple-element.52), channel_id=1, source_target_pairs={{0,72},{24,0},{48,24},{72,48},{1,73},{25,1},{49,25},{73,49},{2,74}... | collective-permute-start | bytes 393224 | tf_op jit(solution)/shard_map/ppermute | solution.py:297
  131.7 17.1 %all-to-all-start = ((bf16[8,4,2,16,128]{4,3,2,1,0:T(8,128)(2,1)}), bf16[8,4,2,16,128]{4,3,2,1,0:T(8,128)(2,1)S(1)}, u32[]{:S(2)}, u32[]{:S(2)}) async-start(bf16[8,4,2,16,128]{4,3,2,1,0:T(8,128)(2,1)} %pad_maximum_fusion.1), calls=%async_computation | async-start | bytes 524288 | tf_op jit(solution)/shard_map/all_to_all | solution.py:313
  139.5 54.3 %copy-start.6 = (bf16[4,512,128]{2,1,0:T(8,128)(2,1)S(1)}, bf16[4,512,128]{2,1,0:T(8,128)(2,1)}, u32[]{:S(2)}) copy-start(bf16[4,512,128]{2,1,0:T(8,128)(2,1)} %get-tuple-element.41) | copy-start | bytes 1572868
  148.8 12.7 %all-to-all-start.1 = ((bf16[8,4,2,16,128]{4,3,2,1,0:T(8,128)(2,1)}), bf16[8,4,2,16,128]{4,3,2,1,0:T(8,128)(2,1)S(1)}, u32[]{:S(2)}, u32[]{:S(2)}) async-start(bf16[8,4,2,16,128]{4,3,2,1,0:T(8,128)(2,1)} %pad_maximum_fusion.2), calls=%async_computation.1 | async-start | bytes 524288 | tf_op jit(solution)/shard_map/all_to_all | solution.py:313
  189.9 21.2 %all-to-all-start.3 = ((bf16[32,2,2,16,128]{4,3,2,1,0:T(8,128)(2,1)}), bf16[32,2,2,16,128]{4,3,2,1,0:T(8,128)(2,1)S(1)}, u32[]{:S(2)}, u32[]{:S(2)}) async-start(bf16[32,2,2,16,128]{4,3,2,1,0:T(8,128)(2,1)} %broadcast_in_dim.39), calls=%async_computation.3 | async-start | bytes 1048576 | tf_op jit(solution)/shard_map/all_to_all | solution.py:383

commit v5 on v2

--- a/solution.py
+++ b/solution.py
@@ -23,10 +23,19 @@
     return lax.dot_general(a, b, (dims, ((), ())), preferred_element_type=f32)
 
 
-def shifted(faces, up):
+def swapped(odd, even):
     count = lax.axis_size(elem)
-    pairs = [(i, i + 1) if up else (i + 1, i) for i in range(count - 1)]
-    return lax.ppermute(faces, elem, pairs)
+    swaps = []
+    for first, sent in ((1, odd), (0, even)):
+        pairs = [(i, i + 1) for i in range(first, count - 1, 2)]
+        swaps.append(lax.ppermute(sent, elem, pairs + [(j, i) for i, j in pairs]))
+    return swaps
+
+
+def neighbours(head, tail):
+    even = lax.axis_index(elem) % 2 == 0
+    first, second = swapped(jnp.where(even, head, tail), jnp.where(even, tail, head))
+    return jnp.where(even, second, first), jnp.where(even, first, second)
 
 
 def vmem():
@@ -46,74 +55,112 @@
     return jnp.where(rows == map_row, 1.0, 0.0).astype(bf16)
 
 
-def first_edges_kernel(map_ref, low_ref, up_ref, first_ref, last_ref, head_ref, tail_ref):
+def first_edges_kernel(even_ref, map_ref, low_ref, up_ref, first_ref, last_ref, odd_out_ref, even_out_ref):
     face = low_ref.shape[1]
-    head_ref[0] = dot(low_ref[0], first_ref[0])
-    head_ref[1] = first_ref[0, :face].astype(f32)
     cells = map_ref.shape[0]
+    is_even = even_ref[0] == 1
+    head = dot(low_ref[0], first_ref[0])
     up = dot(selection(map_ref[cells - 1 :, :]), up_ref[0]).astype(bf16)
-    tail_ref[...] = dot(up, last_ref[0])
-
-
-def first_edges(cell_matrices, states, face_map):
+    tail = dot(up, last_ref[0])
+    odd_out_ref[0] = jnp.where(is_even, head, tail)
+    even_out_ref[0] = jnp.where(is_even, tail, head)
+    states = first_ref[0, :face].astype(f32)
+    odd_out_ref[1] = states
+    even_out_ref[1] = states
+
+
+def first_edges(is_even, cell_matrices, states, face_map):
     cells, nodes, orb = states.shape
     face = face_map.shape[1]
+    out = jax.ShapeDtypeStruct((2, face, orb), f32)
     return pl.pallas_call(
         first_edges_kernel,
         grid=(1,),
         in_specs=[
+            smem(),
             pl.BlockSpec((cells, face), lambda i: (0, 0)),
             pl.BlockSpec((1, face, nodes), lambda i: (0, 0, 0)),
             pl.BlockSpec((1, face, nodes), lambda i: (cells - 1, nodes // face - 1, 0)),
             pl.BlockSpec((1, nodes, orb), lambda i: (0, 0, 0)),
             pl.BlockSpec((1, nodes, orb), lambda i: (cells - 1, 0, 0)),
         ],
-        out_specs=[
-            pl.BlockSpec((2, face, orb), lambda i: (0, 0, 0)),
-            pl.BlockSpec((face, orb), lambda i: (0, 0)),
-        ],
-        out_shape=[
-            jax.ShapeDtypeStruct((2, face, orb), f32),
-            jax.ShapeDtypeStruct((face, orb), f32),
-        ],
+        out_specs=[pl.BlockSpec((2, face, orb), lambda i: (0, 0, 0))] * 2,
+        out_shape=[out, out],
         compiler_params=SMALL,
         name="first_edges",
-    )(face_map, cell_matrices, cell_matrices, states, states)
-
-
-def reorder_kernel(map_ref, k_ref, x_ref, out_ref, start_ref):
-    face = map_ref.shape[2]
-    nodes = k_ref.shape[1]
+    )(is_even, face_map, cell_matrices, cell_matrices, states, states)
+
+
+def first_step_kernel(even_ref, first_ref, second_ref, product_ref, k_ref, wide_ref, now_ref, head_ref, tail_ref, next_ref):
+    cells, nodes, _ = product_ref.shape
+    face = head_ref.shape[0]
     inner = nodes - face
-    select = selection(map_ref[0])
+    is_even = even_ref[0] == 1
+    for c in (0, cells - 1, *range(1, cells - 1)):
+        if c == 0:
+            below = jnp.where(is_even, first_ref[0], second_ref[0])
+        else:
+            below = product_ref[c - 1, inner:]
+        if c == cells - 1:
+            above = jnp.where(is_even, second_ref[0], first_ref[0])
+        else:
+            above = product_ref[c + 1, :face]
+        wide_ref[c, :face] = (product_ref[c, :face] + below) / filter_width
+        wide_ref[c, face:inner] = product_ref[c, face:inner] / filter_width
+        wide_ref[c, inner:] = (product_ref[c, inner:] + above) / filter_width
+        now_ref[c] = wide_ref[c].astype(bf16)
+    head_ref[...] = dot(k_ref[0, :face], now_ref[0])
+    tail_ref[...] = dot(k_ref[cells - 1, inner:], now_ref[cells - 1])
+    next_ref[...] = jnp.where(is_even, second_ref[1], first_ref[1])
+
+
+def first_step(is_even, first, second, products, matrices):
+    face = first.shape[1]
+    edge = jax.ShapeDtypeStruct((face, products.shape[2]), f32)
+    return pl.pallas_call(
+        first_step_kernel,
+        in_specs=[smem()] + [vmem()] * 4,
+        out_specs=[vmem()] * 5,
+        out_shape=[products, jax.ShapeDtypeStruct(products.shape, bf16), edge, edge, edge],
+        compiler_params=SMALL,
+        name="first_step",
+    )(is_even, first, second, products, matrices)
+
+
+def reorder_kernel(map_ref, k_ref, x_ref, out_ref, start_ref, wide_ref, product_ref):
+    cells, nodes, _ = k_ref.shape
+    face = map_ref.shape[1]
+    inner = nodes - face
     wide = 2 * face
     eye = lax.broadcasted_iota(jnp.int32, (wide, wide), 0) == lax.broadcasted_iota(jnp.int32, (wide, wide), 1)
-    both = jnp.concatenate([jnp.zeros((face, face), bf16), select], 1)
-    both = jnp.concatenate([jnp.where(eye[:face], 1.0, 0.0).astype(bf16), both], 0)
-    out_ref[0, :, : nodes - wide] = k_ref[0, :, : nodes - wide]
-    out_ref[0, :, nodes - wide :] = dot(k_ref[0, :, nodes - wide :], both, ((1,), (1,))).astype(bf16)
-    out_ref[0, inner:, :] = dot(select, out_ref[0, inner:, :]).astype(bf16)
-    start_ref[0, :inner] = x_ref[0, :inner]
-    start_ref[0, inner:] = dot(select, x_ref[0, inner:]).astype(bf16)
+    eye = jnp.where(eye[:face], 1.0, 0.0).astype(bf16)
+    for c in range(cells):
+        select = selection(map_ref[c : c + 1, :])
+        both = jnp.concatenate([jnp.zeros((face, face), bf16), select], 1)
+        both = jnp.concatenate([eye, both], 0)
+        out_ref[c, :, : nodes - wide] = k_ref[c, :, : nodes - wide]
+        out_ref[c, :, nodes - wide :] = dot(k_ref[c, :, nodes - wide :], both, ((1,), (1,))).astype(bf16)
+        out_ref[c, inner:, :] = dot(select, out_ref[c, inner:, :]).astype(bf16)
+        start_ref[c, :inner] = x_ref[c, :inner]
+        start_ref[c, inner:] = dot(select, x_ref[c, inner:]).astype(bf16)
+        wide_ref[c] = start_ref[c].astype(f32)
+        product_ref[c] = dot(out_ref[c], start_ref[c])
 
 
 def reordered(cell_matrices, states, face_map):
-    cells, nodes = cell_matrices.shape[:2]
-    orb = states.shape[2]
-    face = face_map.shape[1]
-    per_cell = lambda *shape: pl.BlockSpec((1,) + shape, lambda c: (c, 0, 0))
     return pl.pallas_call(
         reorder_kernel,
-        grid=(cells,),
-        in_specs=[per_cell(1, face), per_cell(nodes, nodes), per_cell(nodes, orb)],
-        out_specs=[per_cell(nodes, nodes), per_cell(nodes, orb)],
+        in_specs=[vmem()] * 3,
+        out_specs=[vmem()] * 4,
         out_shape=[
             jax.ShapeDtypeStruct(cell_matrices.shape, bf16),
             jax.ShapeDtypeStruct(states.shape, bf16),
+            jax.ShapeDtypeStruct(states.shape, f32),
+            jax.ShapeDtypeStruct(states.shape, f32),
         ],
         compiler_params=SMALL,
         name="reorder",
-    )(face_map[:, None, :], cell_matrices, states)
+    )(face_map, cell_matrices, states)
 
 
 def scatter_rows(part, out_ref, block, core):
@@ -122,6 +169,29 @@
         for y in range(ys):
             tile = part[x * rows : (x + 1) * rows, y * cols : (y + 1) * cols].astype(bf16)
             out_ref[x, y, block, core] = tile
+
+
+def pack_kernel(last_ref, now_ref, start_ref, next_ref, rows_ref):
+    cells, nodes, _ = now_ref.shape
+    face = next_ref.shape[0]
+    inner = nodes - face
+    for c in range(cells):
+        after = next_ref[...] if c == cells - 1 else start_ref[c + 1, :face]
+        step = jnp.where(last_ref[0] == c, 0.0, start_ref[c, inner:] - after)
+        rows_ref[c, :nodes] = now_ref[c].astype(bf16)
+        rows_ref[c, nodes:] = (now_ref[c, inner:] - step).astype(bf16)
+
+
+def pack(last_cell, now, start, after):
+    cells, nodes, orb = now.shape
+    return pl.pallas_call(
+        pack_kernel,
+        in_specs=[smem()] + [vmem()] * 3,
+        out_specs=vmem(),
+        out_shape=jax.ShapeDtypeStruct((cells, nodes + after.shape[0], orb), bf16),
+        compiler_params=SMALL,
+        name="pack",
+    )(last_cell, now, start, after)
 
 
 def right_kernel(where_ref, k_ref, rows_ref, right_ref):
@@ -210,6 +280,11 @@
     return jnp.sum(parts.astype(f32), 0).astype(bf16)
 
 
+def ring(part, axis, step):
+    count = lax.axis_size(axis)
+    return lax.ppermute(part, axis, [(i, (i + step) % count) for i in range(count)])
+
+
 def swap_sum(part, axis):
     return summed(lax.all_to_all(part, axis, split_axis=0, concat_axis=0, tiled=True))
 
@@ -221,29 +296,21 @@
     elems = lax.axis_size(elem)
     zhs, cores, zls = lax.axis_size("zh"), lax.axis_size("core"), lax.axis_size("zl")
     xs, ys = lax.axis_size("x"), lax.axis_size("y")
-    head, tail = first_edges(cell_matrices, initial_states, face_map)
-    cell_matrices, initial_states, head, tail = lax.optimization_barrier(
-        (cell_matrices, initial_states, head, tail)
+    is_even = (1 - lax.axis_index(elem) % 2).reshape(1)
+    sent = first_edges(is_even, cell_matrices, initial_states, face_map)
+    cell_matrices, initial_states, *sent = lax.optimization_barrier(
+        (cell_matrices, initial_states, *sent)
     )
-    both = shifted(head, False)
-    from_below = shifted(tail, True)
-    matrices, current_b = reordered(cell_matrices, initial_states, face_map)
-
-    def edges(values):
-        return (
-            dot(matrices[0, :face], values[0]),
-            dot(matrices[-1, -face:], values[-1]),
-        )
-
-    start = current_b.astype(f32)
+    first, second = swapped(*sent)
+    matrices, current_b, start, products = reordered(cell_matrices, initial_states, face_map)
     previous = start
-    current = start
-    from_above, next_start = both[0], both[1]
-    for degree in range(PASSES):
-        if degree > 0:
-            head, tail = edges(current_b)
-            from_above = shifted(head, False)
-            from_below = shifted(tail, True)
+    current, current_b, head, tail, next_start = first_step(is_even, first, second, products, matrices)
+    for degree in range(1, PASSES):
+        if degree > 1:
+            head = dot(matrices[0, :face], current_b[0])
+            tail = dot(matrices[-1, -face:], current_b[-1])
+        from_above, from_below = neighbours(head, tail)
+        current_b, head, tail = lax.optimization_barrier((current_b, head, tail))
         products = jnp.einsum("cij,cjo->cio", matrices, current_b, preferred_element_type=f32)
         from_next = jnp.concatenate([products[1:, :face], from_above[None]], 0)
         from_low = jnp.concatenate([from_below[None], products[:-1, -face:]], 0)
@@ -255,24 +322,19 @@
             ],
             1,
         )
-        following = image / filter_width if degree == 0 else 2.0 / filter_width * image - previous
+        following = 2.0 / filter_width * image - previous
         previous = current
         current = following
         current_b = following.astype(bf16)
 
     place = lax.axis_index(elem) * cells_dev
-    cell_index = place + jnp.arange(cells_dev, dtype=jnp.int32)
-    is_last = cell_index == cells_dev * elems - 1
-    step = start[:, -face:] - jnp.concatenate([start[1:, :face], next_start[None]], 0)
-    step = jnp.where(is_last[:, None, None], 0.0, step)
-    paired = (current[:, -face:] - step).astype(bf16)
-
-    rows = jnp.concatenate([current_b, paired], 1)
+    zh = lax.axis_index("zh")
+    last_cell = cells_dev * elems - 1 - place
+    where = jnp.stack([zh, (zh == last_cell).astype(jnp.int32), lax.axis_index("core")])
+
+    rows = pack(last_cell.reshape(1), current, start, next_start)
     rows = lax.all_to_all(rows, "zh", split_axis=0, concat_axis=0, tiled=True)
-    other = lax.ppermute(rows, "core", [(0, 1), (1, 0)])
-    zh = lax.axis_index("zh")
-    at_end = (place + zh == cells_dev * elems - 1).astype(jnp.int32)
-    where = jnp.stack([zh, at_end, lax.axis_index("core")])
+    other = ring(rows, "core", 1)
     right = right_of(where, matrices, rows)
     part = gram(where, rows, other, right)
     part = swap_sum(part, "x")

time: 210 us -> 195 us (0.929)
  waiting for transfers between devices: 28.4 us -> 17.9 us
  starting transfers between devices: 39 us -> 44.6 us
  blocking collectives: 115 us -> 111 us
  local copies, waits for them, and re-layouts: 9.35 us -> 6.08 us
  other arithmetic: 5.47 us -> 2.96 us
    ppermute x9, waiting for transfers between devices: 12.2 us -> 1.69 us  [the longest x8 1.46 us: swapped(): swaps.append(lax.ppermute(sent, elem, pairs + [(j, i) for i, j in pairs]))]
    ppermute x9, starting transfers between devices: 35.1 us -> 40.7 us  [the longest x8 28.3 us: swapped(): swaps.append(lax.ppermute(sent, elem, pairs + [(j, i) for i, j in pairs]))]
    all_to_all x2, blocking collectives: 59.6 us -> 55.9 us  [swap_sum(): lax.all_to_all(part, axis, split_axis=0, concat_axis=0, tiled=True)]
  transfers between devices with their start and end apart: 10 -> 10, of which waited for: 5 -> 5; matrix products, arithmetic and copies ran while one was open for 4% -> 2% of each run, Pallas kernels for 1% -> 2%
where the time goes in v5:
time: 195 us; the launch traced here: 194 us
  blocking collectives  111 us (57%)
  starting transfers between devices  44.6 us (23%)
  waiting for transfers between devices  17.9 us (9%)
  Pallas kernels  7 us (4%)
  local copies, waits for them, and re-layouts  6.08 us (3%)
  matrix products  2.97 us (2%)
  other arithmetic  2.96 us (2%)
    all_to_all x2, blocking collectives, swap_sum(): lax.all_to_all(part, axis, split_axis=0, concat_axis=0, tiled=True)  55.9 us
    all_to_all x1, blocking collectives, local(): rows = lax.all_to_all(rows, 'zh', split_axis=0, concat_axis=0, tiled=True)  35.6 us
    ppermute x8, starting transfers between devices, swapped(): swaps.append(lax.ppermute(sent, elem, pairs + [(j, i) for i, j in pairs]))  28.3 us
    all_to_all x1, blocking collectives, local(): lax.all_to_all(column, ('zl', 'zh', 'core'), split_axis=0, concat_axis=0,...  19.9 us
    all_to_all x1, waiting for transfers between devices, local(): lax.all_to_all(pieces, ('y', 'x'), split_axis=0, concat_axis=0, tiled=True)  16.2 us
    ppermute x1, starting transfers between devices, ring(): lax.ppermute(part, axis, [(i, (i + step) % count) for i in range(count)])  12.4 us
    unnamed x14, local copies, waits for them, and re-layouts  4.91 us
  transfers between devices with their start and end apart: 10, of which 5 were waited for; matrix products, arithmetic and copies ran while one was open for 2% of the time, Pallas kernels for 2%

profile of v5, /device:TPU:1, one launch (start us, length us, event | category | flops | bytes accessed | tf_op | source)
XLA Modules:
  0.0 193.9 jit_solution(1941780655823544281)
XLA Ops:
  0.7 1.6 copy-done
  2.3 1.0 copy-done.2
  3.3 0.7 copy-done.4
  4.0 0.3 first_edges.1
  4.3 0.7 collective-permute-start
  4.9 8.2 %collective-permute-start.1 = (f32[2,64,128]{2,1,0:T(8,128)S(1)}, f32[2,64,128]{2,1,0:T(8,128)S(1)}, u32[]{:S(2)}, u32[]{:S(2)}) collective-permute-start(f32[2,64,128]{2,1,0:T(8,128)S(1)} %get-tuple-element.28), channel_id=1, source_target_pairs={{0,8},{16,24},{32,40},{48,56},{64,72},{80,88},{96,104},{112,120},{... | collective-permute-start | bytes 196616 | tf_op jit(solution)/shard_map/ppermute | solution.py:31
  13.2 1.6 copy-done.1
  14.7 2.1 %reorder.1 = (bf16[4,512,512]{2,1,0:T(8,128)(2,1)S(1)}, bf16[4,512,128]{2,1,0:T(8,128)(2,1)}, f32[4,512,128]{2,1,0:T(8,128)S(1)}, f32[4,512,128]{2,1,0:T(8,128)S(1)}) custom-call(s32[4,64]{1,0:T(4,128)S(1)} %copy-done.5, bf16[4,512,512]{2,1,0:T(8,128)(2,1)S(1)} %copy-done.1, bf16[4,512,128]{2,1,0:T(8,128)(2,1)S(1)} %copy-done.3), custom_call_target="tpu_custom_call" | custom-call | tf_op jit(solution)/shard_map/reorder/pallas_call | solution.py:151
  16.8 0.3 first_step.1
  17.2 0.7 collective-permute-start.2
  17.9 4.6 %collective-permute-start.3 = (f32[64,128]{1,0:T(8,128)S(1)}, f32[64,128]{1,0:T(8,128)S(1)}, u32[]{:S(2)}, u32[]{:S(2)}) collective-permute-start(f32[64,128]{1,0:T(8,128)S(1)} %get-tuple-element.66), channel_id=1, source_target_pairs={{0,8},{16,24},{32,40},{48,56},{64,72},{80,88},{96,104},{112,120},{... | collective-permute-start | bytes 98312 | tf_op jit(solution)/shard_map/ppermute | solution.py:31
  22.5 0.7 fusion.24
  23.2 0.1 slice.96
  23.3 0.5 collective-permute-done.3
  23.8 0.1 fusion.8
  24.0 0.2 fusion.6
  24.1 0.2 broadcast_select_fusion.3
  24.3 0.7 collective-permute-start.4
  25.0 6.4 %collective-permute-start.5 = (f32[64,128]{1,0:T(8,128)S(1)}, f32[64,128]{1,0:T(8,128)S(1)}, u32[]{:S(2)}, u32[]{:S(2)}) collective-permute-start(f32[64,128]{1,0:T(8,128)S(1)} %get-tuple-element.62), channel_id=1, source_target_pairs={{0,8},{16,24},{32,40},{48,56},{64,72},{80,88},{96,104},{112,120},{... | collective-permute-start | bytes 98312 | tf_op jit(solution)/shard_map/ppermute | solution.py:31
  31.4 0.7 fusion.25
  32.1 0.1 slice.103
  32.2 0.5 collective-permute-done.5
  32.7 0.1 fusion.2
  32.9 0.2 fusion.4
  33.0 0.2 broadcast_select_fusion.1
  33.2 0.7 collective-permute-start.6
  33.9 6.4 %collective-permute-start.7 = (f32[64,128]{1,0:T(8,128)S(1)}, f32[64,128]{1,0:T(8,128)S(1)}, u32[]{:S(2)}, u32[]{:S(2)}) collective-permute-start(f32[64,128]{1,0:T(8,128)S(1)} %get-tuple-element.58), channel_id=1, source_target_pairs={{0,8},{16,24},{32,40},{48,56},{64,72},{80,88},{96,104},{112,120},{... | collective-permute-start | bytes 98312 | tf_op jit(solution)/shard_map/ppermute | solution.py:31
  40.3 0.7 fusion.26
  41.1 0.5 collective-permute-done.7
  41.6 1.1 fusion.19
  42.7 0.1 pack.1
  42.8 35.6 %all_to_all.25.rows_ref.own_ref = bf16[4,576,128]{2,1,0:T(8,128)(2,1)S(1)} all-to-all(bf16[4,576,128]{2,1,0:T(8,128)(2,1)S(1)} %pack.1), channel_id=1, replica_groups=mesh['y'=8,'x'=4,'zl'=3,'zh'=4,'core'=2] {'zh'}, dimensions={0} | all-to-all | bytes 1179648 | tf_op jit(solution)/shard_map/all_to_all | solution.py:336
  78.3 12.4 %collective-permute-start.8 = (bf16[4,576,128]{2,1,0:T(8,128)(2,1)S(1)}, bf16[4,576,128]{2,1,0:T(8,128)(2,1)S(1)}, u32[]{:S(2)}, u32[]{:S(2)}) collective-permute-start(bf16[4,576,128]{2,1,0:T(8,128)(2,1)S(1)} %all_to_all.25.rows_ref.own_ref), channel_id=1, source_target_pairs={{0,1},{1,0},{2,3},{3,2},{4,5},{5,4},{6,7},{7,6},{8,9},{9,8},{10,11... | collective-permute-start | bytes 1769480 | tf_op jit(solution)/shard_map/ppermute | solution.py:285
  90.8 0.1 pad_add_fusion.where_ref
  90.9 1.3 right.1.right_ref
  92.2 0.2 collective-permute-done.8.other_ref
  92.4 1.9 gram.1
  94.3 32.3 %all_to_all.26 = bf16[4,8,4,2,32,128]{5,4,3,2,1,0:T(8,128)(2,1)S(1)} all-to-all(bf16[4,8,4,2,32,128]{5,4,3,2,1,0:T(8,128)(2,1)S(1)} %gram.1), channel_id=1, replica_groups=mesh['y'=8,'x'=4,'zl'=3,'zh'=4,'core'=2] {'x'}, dimensions={0} | all-to-all | bytes 4194304 | tf_op jit(solution)/shard_map/all_to_all | solution.py:289
  126.6 0.4 reduce_sum.36
  127.0 23.6 %all_to_all.27 = bf16[8,4,2,32,128]{4,3,2,1,0:T(8,128)(2,1)S(1)} all-to-all(bf16[8,4,2,32,128]{4,3,2,1,0:T(8,128)(2,1)S(1)} %reduce_sum.36), channel_id=1, replica_groups=mesh['y'=8,'x'=4,'zl'=3,'zh'=4,'core'=2] {'y'}, dimensions={0} | all-to-all | bytes 1048576 | tf_op jit(solution)/shard_map/all_to_all | solution.py:289
  150.6 0.1 reduce_sum.37
  150.7 19.9 %all_to_all.28 = bf16[24,32,128]{2,1,0:T(8,128)(2,1)S(1)} all-to-all(bf16[24,32,128]{2,1,0:T(8,128)(2,1)S(1)} %bitcast.58), channel_id=1, replica_groups=mesh['y'=8,'x'=4,'zl'=3,'zh'=4,'core'=2] {'zl','zh','core'}, dimensions={0} | all-to-all | bytes 393216 | tf_op jit(solution)/shard_map/all_to_all | solution.py:344
  170.7 0.9 broadcast_in_dim.39
  171.6 3.9 %all-to-all-start.4 = ((bf16[32,2,32,128]{3,2,1,0:T(8,128)(2,1)}), bf16[32,2,32,128]{3,2,1,0:T(8,128)(2,1)S(1)}, u32[]{:S(2)}, u32[]{:S(2)}) async-start(bf16[32,2,32,128]{3,2,1,0:T(8,128)(2,1)} %broadcast_in_dim.39), calls=%async_computation.4 | async-start | bytes 1048576 | tf_op jit(solution)/shard_map/all_to_all | solution.py:347
  175.6 0.2 convolution_convert_fusion
  175.8 0.8 pad_maximum_fusion
  176.6 16.2 %all-to-all-done.4 = bf16[32,2,32,128]{3,2,1,0:T(8,128)(2,1)S(1)} async-done(((bf16[32,2,32,128]{3,2,1,0:T(8,128)(2,1)}), bf16[32,2,32,128]{3,2,1,0:T(8,128)(2,1)S(1)}, u32[]{:S(2)}, u32[]{:S(2)}) %all-to-all-start.4) | async-done | bytes 524320 | tf_op jit(solution)/shard_map/all_to_all | solution.py:347
  192.8 1.0 assemble.1
  (29 shorter events, 0.4 us)
Async XLA Ops:
  0.7 1.6 copy-start
  2.2 1.0 copy-start.2
  3.3 0.7 copy-start.4
  4.0 9.1 %copy-start.3 = (bf16[4,512,128]{2,1,0:T(8,128)(2,1)S(1)}, bf16[4,512,128]{2,1,0:T(8,128)(2,1)}, u32[]{:S(2)}) copy-start(bf16[4,512,128]{2,1,0:T(8,128)(2,1)} %x_ref) | copy-start | bytes 1572868
  4.0 9.2 %copy-start.5 = (s32[4,64]{1,0:T(4,128)S(1)}, s32[4,64]{1,0:T(4,128)}, u32[]{:S(2)}) copy-start(s32[4,64]{1,0:T(4,128)} %map_ref.3) | copy-start | bytes 3076
  4.3 12.6 %collective-permute-start = (f32[2,64,128]{2,1,0:T(8,128)S(1)}, f32[2,64,128]{2,1,0:T(8,128)S(1)}, u32[]{:S(2)}, u32[]{:S(2)}) collective-permute-start(f32[2,64,128]{2,1,0:T(8,128)S(1)} %get-tuple-element.27), channel_id=1, source_target_pairs={{8,16},{24,32},{40,48},{56,64},{72,80},{88,96},{104,112},{120,128}... | collective-permute-start | bytes 196616 | tf_op jit(solution)/shard_map/ppermute | solution.py:31
  4.9 11.9 %collective-permute-start.1 = (f32[2,64,128]{2,1,0:T(8,128)S(1)}, f32[2,64,128]{2,1,0:T(8,128)S(1)}, u32[]{:S(2)}, u32[]{:S(2)}) collective-permute-start(f32[2,64,128]{2,1,0:T(8,128)S(1)} %get-tuple-element.28), channel_id=1, source_target_pairs={{0,8},{16,24},{32,40},{48,56},{64,72},{80,88},{96,104},{112,120},{... | collective-permute-start | bytes 196616 | tf_op jit(solution)/shard_map/ppermute | solution.py:31
  13.1 1.6 copy-start.1
  17.2 6.1 %collective-permute-start.2 = (f32[64,128]{1,0:T(8,128)S(1)}, f32[64,128]{1,0:T(8,128)S(1)}, u32[]{:S(2)}, u32[]{:S(2)}) collective-permute-start(f32[64,128]{1,0:T(8,128)S(1)} %get-tuple-element.65), channel_id=1, source_target_pairs={{8,16},{24,32},{40,48},{56,64},{72,80},{88,96},{104,112},{120,128}... | collective-permute-start | bytes 98312 | tf_op jit(solution)/shard_map/ppermute | solution.py:31
  17.9 5.9 %collective-permute-start.3 = (f32[64,128]{1,0:T(8,128)S(1)}, f32[64,128]{1,0:T(8,128)S(1)}, u32[]{:S(2)}, u32[]{:S(2)}) collective-permute-start(f32[64,128]{1,0:T(8,128)S(1)} %get-tuple-element.66), channel_id=1, source_target_pairs={{0,8},{16,24},{32,40},{48,56},{64,72},{80,88},{96,104},{112,120},{... | collective-permute-start | bytes 98312 | tf_op jit(solution)/shard_map/ppermute | solution.py:31
  24.3 7.9 %collective-permute-start.4 = (f32[64,128]{1,0:T(8,128)S(1)}, f32[64,128]{1,0:T(8,128)S(1)}, u32[]{:S(2)}, u32[]{:S(2)}) collective-permute-start(f32[64,128]{1,0:T(8,128)S(1)} %get-tuple-element.61), channel_id=1, source_target_pairs={{8,16},{24,32},{40,48},{56,64},{72,80},{88,96},{104,112},{120,128}... | collective-permute-start | bytes 98312 | tf_op jit(solution)/shard_map/ppermute | solution.py:31
  25.0 7.7 %collective-permute-start.5 = (f32[64,128]{1,0:T(8,128)S(1)}, f32[64,128]{1,0:T(8,128)S(1)}, u32[]{:S(2)}, u32[]{:S(2)}) collective-permute-start(f32[64,128]{1,0:T(8,128)S(1)} %get-tuple-element.62), channel_id=1, source_target_pairs={{0,8},{16,24},{32,40},{48,56},{64,72},{80,88},{96,104},{112,120},{... | collective-permute-start | bytes 98312 | tf_op jit(solution)/shard_map/ppermute | solution.py:31
  33.2 7.9 %collective-permute-start.6 = (f32[64,128]{1,0:T(8,128)S(1)}, f32[64,128]{1,0:T(8,128)S(1)}, u32[]{:S(2)}, u32[]{:S(2)}) collective-permute-start(f32[64,128]{1,0:T(8,128)S(1)} %get-tuple-element.57), channel_id=1, source_target_pairs={{8,16},{24,32},{40,48},{56,64},{72,80},{88,96},{104,112},{120,128}... | collective-permute-start | bytes 98312 | tf_op jit(solution)/shard_map/ppermute | solution.py:31
  33.9 7.7 %collective-permute-start.7 = (f32[64,128]{1,0:T(8,128)S(1)}, f32[64,128]{1,0:T(8,128)S(1)}, u32[]{:S(2)}, u32[]{:S(2)}) collective-permute-start(f32[64,128]{1,0:T(8,128)S(1)} %get-tuple-element.58), channel_id=1, source_target_pairs={{0,8},{16,24},{32,40},{48,56},{64,72},{80,88},{96,104},{112,120},{... | collective-permute-start | bytes 98312 | tf_op jit(solution)/shard_map/ppermute | solution.py:31
  78.3 14.1 %collective-permute-start.8 = (bf16[4,576,128]{2,1,0:T(8,128)(2,1)S(1)}, bf16[4,576,128]{2,1,0:T(8,128)(2,1)S(1)}, u32[]{:S(2)}, u32[]{:S(2)}) collective-permute-start(bf16[4,576,128]{2,1,0:T(8,128)(2,1)S(1)} %all_to_all.25.rows_ref.own_ref), channel_id=1, source_target_pairs={{0,1},{1,0},{2,3},{3,2},{4,5},{5,4},{6,7},{7,6},{8,9},{9,8},{10,11... | collective-permute-start | bytes 1769480 | tf_op jit(solution)/shard_map/ppermute | solution.py:285
  127.0 48.5 %copy-start.6 = (bf16[4,512,128]{2,1,0:T(8,128)(2,1)S(1)}, bf16[4,512,128]{2,1,0:T(8,128)(2,1)}, u32[]{:S(2)}) copy-start(bf16[4,512,128]{2,1,0:T(8,128)(2,1)} %get-tuple-element.41) | copy-start | bytes 1572868
  171.6 21.2 %all-to-all-start.4 = ((bf16[32,2,32,128]{3,2,1,0:T(8,128)(2,1)}), bf16[32,2,32,128]{3,2,1,0:T(8,128)(2,1)S(1)}, u32[]{:S(2)}, u32[]{:S(2)}) async-start(bf16[32,2,32,128]{3,2,1,0:T(8,128)(2,1)} %broadcast_in_dim.39), calls=%async_computation.4 | async-start | bytes 1048576 | tf_op jit(solution)/shard_map/all_to_all | solution.py:347

commit v6 on v5

--- a/solution.py
+++ b/solution.py
@@ -86,7 +86,6 @@
         ],
         out_specs=[pl.BlockSpec((2, face, orb), lambda i: (0, 0, 0))] * 2,
         out_shape=[out, out],
-        compiler_params=SMALL,
         name="first_edges",
     )(is_even, face_map, cell_matrices, cell_matrices, states, states)
 
@@ -98,11 +97,11 @@
     is_even = even_ref[0] == 1
     for c in (0, cells - 1, *range(1, cells - 1)):
         if c == 0:
-            below = jnp.where(is_even, first_ref[0], second_ref[0])
+            below = jnp.where(is_even, first_ref[0].astype(f32), second_ref[0].astype(f32))
         else:
             below = product_ref[c - 1, inner:]
         if c == cells - 1:
-            above = jnp.where(is_even, second_ref[0], first_ref[0])
+            above = jnp.where(is_even, second_ref[0].astype(f32), first_ref[0].astype(f32))
         else:
             above = product_ref[c + 1, :face]
         wide_ref[c, :face] = (product_ref[c, :face] + below) / filter_width
@@ -111,7 +110,7 @@
         now_ref[c] = wide_ref[c].astype(bf16)
     head_ref[...] = dot(k_ref[0, :face], now_ref[0])
     tail_ref[...] = dot(k_ref[cells - 1, inner:], now_ref[cells - 1])
-    next_ref[...] = jnp.where(is_even, second_ref[1], first_ref[1])
+    next_ref[...] = jnp.where(is_even, second_ref[1].astype(f32), first_ref[1].astype(f32))
 
 
 def first_step(is_even, first, second, products, matrices):

time: 195 us -> 193 us (0.990)
  local copies, waits for them, and re-layouts: 6.08 us -> 2.78 us
    unnamed x14 -> x8, local copies, waits for them, and re-layouts: 4.91 us -> 1.6 us
where the time goes in v6:
time: 193 us
  blocking collectives  112 us (58%)
  starting transfers between devices  44.6 us (23%)
  waiting for transfers between devices  17.9 us (9%)
  Pallas kernels  8.76 us (5%)
  matrix products  2.99 us (2%)
  other arithmetic  2.96 us (2%)
  local copies, waits for them, and re-layouts  2.78 us (1%)
    all_to_all x2, blocking collectives, swap_sum(): lax.all_to_all(part, axis, split_axis=0, concat_axis=0, tiled=True)  55.9 us
    all_to_all x1, blocking collectives, local(): rows = lax.all_to_all(rows, 'zh', split_axis=0, concat_axis=0, tiled=True)  35.8 us
    ppermute x8, starting transfers between devices, swapped(): swaps.append(lax.ppermute(sent, elem, pairs + [(j, i) for i, j in pairs]))  28.3 us
    all_to_all x1, blocking collectives, local(): lax.all_to_all(column, ('zl', 'zh', 'core'), split_axis=0, concat_axis=0,...  19.9 us
    all_to_all x1, waiting for transfers between devices, local(): lax.all_to_all(pieces, ('y', 'x'), split_axis=0, concat_axis=0, tiled=True)  16.2 us
    ppermute x1, starting transfers between devices, ring(): lax.ppermute(part, axis, [(i, (i + step) % count) for i in range(count)])  12.4 us
    all_to_all x1, starting transfers between devices, local(): lax.all_to_all(pieces, ('y', 'x'), split_axis=0, concat_axis=0, tiled=True)  3.89 us
  transfers between devices with their start and end apart: 10, of which 5 were waited for; matrix products, arithmetic and copies ran while one was open for 2% of the time, Pallas kernels for 2%

profile of v6, /device:TPU:1, one launch (start us, length us, event | category | flops | bytes accessed | tf_op | source)
XLA Modules:
  0.0 192.5 jit_solution(125434651229281516)
XLA Ops:
  0.7 2.1 %first_edges.1 = (f32[2,64,128]{2,1,0:T(8,128)}, f32[2,64,128]{2,1,0:T(8,128)}) custom-call(s32[1]{0:T(128)} %bitcast.even_ref, s32[4,64]{1,0:T(4,128)} %map_ref.3, bf16[4,512,512]{2,1,0:T(8,128)(2,1)} %k_ref, bf16[4,512,512]{2,1,0:T(8,128)(2,1)} %k_ref, bf16[4,512,128]{2,1,0:T(8,128)(2,1)} %x_ref, bf16[4,512,128]{2,1,0:T(8,128)(2,1)} %x_ref), custom_call_target="tpu_custom_call" | custom-call | tf_op jit(solution)/shard_map/first_edges/pallas_call | solution.py:76
  2.7 0.7 collective-permute-start
  3.4 8.2 %collective-permute-start.1 = (f32[2,64,128]{2,1,0:T(8,128)}, f32[2,64,128]{2,1,0:T(8,128)S(1)}, u32[]{:S(2)}, u32[]{:S(2)}) collective-permute-start(f32[2,64,128]{2,1,0:T(8,128)} %get-tuple-element.28), channel_id=1, source_target_pairs={{0,8},{16,24},{32,40},{48,56},{64,72},{80,88},{96,104},{112,120},{... | collective-permute-start | bytes 196616 | tf_op jit(solution)/shard_map/ppermute | solution.py:31
  11.6 0.0 copy-start
  11.6 1.6 copy-done
  13.2 2.1 %reorder.1 = (bf16[4,512,512]{2,1,0:T(8,128)(2,1)S(1)}, bf16[4,512,128]{2,1,0:T(8,128)(2,1)}, f32[4,512,128]{2,1,0:T(8,128)S(1)}, f32[4,512,128]{2,1,0:T(8,128)S(1)}) custom-call(s32[4,64]{1,0:T(4,128)S(1)} %copy-done.2, bf16[4,512,512]{2,1,0:T(8,128)(2,1)S(1)} %copy-done, bf16[4,512,128]{2,1,0:T(8,128)(2,1)S(1)} %copy-done.1), custom_call_target="tpu_custom_call" | custom-call | tf_op jit(solution)/shard_map/reorder/pallas_call | solution.py:150
  15.3 0.3 first_step.1
  15.6 0.7 collective-permute-start.2
  16.3 4.6 %collective-permute-start.3 = (f32[64,128]{1,0:T(8,128)S(1)}, f32[64,128]{1,0:T(8,128)S(1)}, u32[]{:S(2)}, u32[]{:S(2)}) collective-permute-start(f32[64,128]{1,0:T(8,128)S(1)} %get-tuple-element.66), channel_id=1, source_target_pairs={{0,8},{16,24},{32,40},{48,56},{64,72},{80,88},{96,104},{112,120},{... | collective-permute-start | bytes 98312 | tf_op jit(solution)/shard_map/ppermute | solution.py:31
  20.9 0.7 fusion.24
  21.7 0.1 slice.96
  21.8 0.5 collective-permute-done.3
  22.3 0.1 fusion.8
  22.4 0.2 fusion.6
  22.6 0.2 broadcast_select_fusion.3
  22.8 0.7 collective-permute-start.4
  23.4 6.4 %collective-permute-start.5 = (f32[64,128]{1,0:T(8,128)S(1)}, f32[64,128]{1,0:T(8,128)S(1)}, u32[]{:S(2)}, u32[]{:S(2)}) collective-permute-start(f32[64,128]{1,0:T(8,128)S(1)} %get-tuple-element.62), channel_id=1, source_target_pairs={{0,8},{16,24},{32,40},{48,56},{64,72},{80,88},{96,104},{112,120},{... | collective-permute-start | bytes 98312 | tf_op jit(solution)/shard_map/ppermute | solution.py:31
  29.8 0.7 fusion.25
  30.6 0.1 slice.103
  30.7 0.5 collective-permute-done.5
  31.2 0.1 fusion.2
  31.3 0.2 fusion.4
  31.5 0.2 broadcast_select_fusion.1
  31.7 0.7 collective-permute-start.6
  32.3 6.4 %collective-permute-start.7 = (f32[64,128]{1,0:T(8,128)S(1)}, f32[64,128]{1,0:T(8,128)S(1)}, u32[]{:S(2)}, u32[]{:S(2)}) collective-permute-start(f32[64,128]{1,0:T(8,128)S(1)} %get-tuple-element.58), channel_id=1, source_target_pairs={{0,8},{16,24},{32,40},{48,56},{64,72},{80,88},{96,104},{112,120},{... | collective-permute-start | bytes 98312 | tf_op jit(solution)/shard_map/ppermute | solution.py:31
  38.7 0.7 fusion.26
  39.5 0.1 slice.110
  39.6 0.5 collective-permute-done.7
  40.1 1.1 fusion.19
  41.2 0.1 pack.1
  41.2 35.8 %all_to_all.25.rows_ref.own_ref = bf16[4,576,128]{2,1,0:T(8,128)(2,1)S(1)} all-to-all(bf16[4,576,128]{2,1,0:T(8,128)(2,1)S(1)} %pack.1), channel_id=1, replica_groups=mesh['y'=8,'x'=4,'zl'=3,'zh'=4,'core'=2] {'zh'}, dimensions={0} | all-to-all | bytes 1179648 | tf_op jit(solution)/shard_map/all_to_all | solution.py:335
  77.0 12.4 %collective-permute-start.8 = (bf16[4,576,128]{2,1,0:T(8,128)(2,1)S(1)}, bf16[4,576,128]{2,1,0:T(8,128)(2,1)S(1)}, u32[]{:S(2)}, u32[]{:S(2)}) collective-permute-start(bf16[4,576,128]{2,1,0:T(8,128)(2,1)S(1)} %all_to_all.25.rows_ref.own_ref), channel_id=1, source_target_pairs={{0,1},{1,0},{2,3},{3,2},{4,5},{5,4},{6,7},{7,6},{8,9},{9,8},{10,11... | collective-permute-start | bytes 1769480 | tf_op jit(solution)/shard_map/ppermute | solution.py:284
  89.5 0.1 pad_add_fusion.where_ref
  89.5 1.3 right.1.right_ref
  90.8 0.2 collective-permute-done.8.other_ref
  91.1 1.9 gram.1
  93.0 32.3 %all_to_all.26 = bf16[4,8,4,2,32,128]{5,4,3,2,1,0:T(8,128)(2,1)S(1)} all-to-all(bf16[4,8,4,2,32,128]{5,4,3,2,1,0:T(8,128)(2,1)S(1)} %gram.1), channel_id=1, replica_groups=mesh['y'=8,'x'=4,'zl'=3,'zh'=4,'core'=2] {'x'}, dimensions={0} | all-to-all | bytes 4194304 | tf_op jit(solution)/shard_map/all_to_all | solution.py:288
  125.2 0.4 reduce_sum.36
  125.7 0.0 copy-start.3
  125.7 23.6 %all_to_all.27 = bf16[8,4,2,32,128]{4,3,2,1,0:T(8,128)(2,1)S(1)} all-to-all(bf16[8,4,2,32,128]{4,3,2,1,0:T(8,128)(2,1)S(1)} %reduce_sum.36), channel_id=1, replica_groups=mesh['y'=8,'x'=4,'zl'=3,'zh'=4,'core'=2] {'y'}, dimensions={0} | all-to-all | bytes 1048576 | tf_op jit(solution)/shard_map/all_to_all | solution.py:288
  149.3 0.1 reduce_sum.37
  149.4 19.9 %all_to_all.28 = bf16[24,32,128]{2,1,0:T(8,128)(2,1)S(1)} all-to-all(bf16[24,32,128]{2,1,0:T(8,128)(2,1)S(1)} %bitcast.58), channel_id=1, replica_groups=mesh['y'=8,'x'=4,'zl'=3,'zh'=4,'core'=2] {'zl','zh','core'}, dimensions={0} | all-to-all | bytes 393216 | tf_op jit(solution)/shard_map/all_to_all | solution.py:343
  169.4 0.9 broadcast_in_dim.39
  170.3 3.9 %all-to-all-start.4 = ((bf16[32,2,32,128]{3,2,1,0:T(8,128)(2,1)}), bf16[32,2,32,128]{3,2,1,0:T(8,128)(2,1)S(1)}, u32[]{:S(2)}, u32[]{:S(2)}) async-start(bf16[32,2,32,128]{3,2,1,0:T(8,128)(2,1)} %broadcast_in_dim.39), calls=%async_computation.4 | async-start | bytes 1048576 | tf_op jit(solution)/shard_map/all_to_all | solution.py:346
  174.2 0.2 convolution_convert_fusion
  174.5 0.8 pad_maximum_fusion
  175.3 16.2 %all-to-all-done.4 = bf16[32,2,32,128]{3,2,1,0:T(8,128)(2,1)S(1)} async-done(((bf16[32,2,32,128]{3,2,1,0:T(8,128)(2,1)}), bf16[32,2,32,128]{3,2,1,0:T(8,128)(2,1)S(1)}, u32[]{:S(2)}, u32[]{:S(2)}) %all-to-all-start.4) | async-done | bytes 524320 | tf_op jit(solution)/shard_map/all_to_all | solution.py:346
  191.5 1.0 assemble.1
  (23 shorter events, 0.3 us)
Async XLA Ops:
  0.7 10.9 %copy-start.1 = (bf16[4,512,128]{2,1,0:T(8,128)(2,1)S(1)}, bf16[4,512,128]{2,1,0:T(8,128)(2,1)}, u32[]{:S(2)}) copy-start(bf16[4,512,128]{2,1,0:T(8,128)(2,1)} %x_ref) | copy-start | bytes 1572868
  0.7 10.9 %copy-start.2 = (s32[4,64]{1,0:T(4,128)S(1)}, s32[4,64]{1,0:T(4,128)}, u32[]{:S(2)}) copy-start(s32[4,64]{1,0:T(4,128)} %map_ref.3) | copy-start | bytes 3076
  2.7 12.6 %collective-permute-start = (f32[2,64,128]{2,1,0:T(8,128)}, f32[2,64,128]{2,1,0:T(8,128)S(1)}, u32[]{:S(2)}, u32[]{:S(2)}) collective-permute-start(f32[2,64,128]{2,1,0:T(8,128)} %get-tuple-element.27), channel_id=1, source_target_pairs={{8,16},{24,32},{40,48},{56,64},{72,80},{88,96},{104,112},{120,128}... | collective-permute-start | bytes 196616 | tf_op jit(solution)/shard_map/ppermute | solution.py:31
  3.4 11.9 %collective-permute-start.1 = (f32[2,64,128]{2,1,0:T(8,128)}, f32[2,64,128]{2,1,0:T(8,128)S(1)}, u32[]{:S(2)}, u32[]{:S(2)}) collective-permute-start(f32[2,64,128]{2,1,0:T(8,128)} %get-tuple-element.28), channel_id=1, source_target_pairs={{0,8},{16,24},{32,40},{48,56},{64,72},{80,88},{96,104},{112,120},{... | collective-permute-start | bytes 196616 | tf_op jit(solution)/shard_map/ppermute | solution.py:31
  11.6 1.6 copy-start
  15.6 6.1 %collective-permute-start.2 = (f32[64,128]{1,0:T(8,128)S(1)}, f32[64,128]{1,0:T(8,128)S(1)}, u32[]{:S(2)}, u32[]{:S(2)}) collective-permute-start(f32[64,128]{1,0:T(8,128)S(1)} %get-tuple-element.65), channel_id=1, source_target_pairs={{8,16},{24,32},{40,48},{56,64},{72,80},{88,96},{104,112},{120,128}... | collective-permute-start | bytes 98312 | tf_op jit(solution)/shard_map/ppermute | solution.py:31
  16.3 5.9 %collective-permute-start.3 = (f32[64,128]{1,0:T(8,128)S(1)}, f32[64,128]{1,0:T(8,128)S(1)}, u32[]{:S(2)}, u32[]{:S(2)}) collective-permute-start(f32[64,128]{1,0:T(8,128)S(1)} %get-tuple-element.66), channel_id=1, source_target_pairs={{0,8},{16,24},{32,40},{48,56},{64,72},{80,88},{96,104},{112,120},{... | collective-permute-start | bytes 98312 | tf_op jit(solution)/shard_map/ppermute | solution.py:31
  22.8 7.9 %collective-permute-start.4 = (f32[64,128]{1,0:T(8,128)S(1)}, f32[64,128]{1,0:T(8,128)S(1)}, u32[]{:S(2)}, u32[]{:S(2)}) collective-permute-start(f32[64,128]{1,0:T(8,128)S(1)} %get-tuple-element.61), channel_id=1, source_target_pairs={{8,16},{24,32},{40,48},{56,64},{72,80},{88,96},{104,112},{120,128}... | collective-permute-start | bytes 98312 | tf_op jit(solution)/shard_map/ppermute | solution.py:31
  23.4 7.7 %collective-permute-start.5 = (f32[64,128]{1,0:T(8,128)S(1)}, f32[64,128]{1,0:T(8,128)S(1)}, u32[]{:S(2)}, u32[]{:S(2)}) collective-permute-start(f32[64,128]{1,0:T(8,128)S(1)} %get-tuple-element.62), channel_id=1, source_target_pairs={{0,8},{16,24},{32,40},{48,56},{64,72},{80,88},{96,104},{112,120},{... | collective-permute-start | bytes 98312 | tf_op jit(solution)/shard_map/ppermute | solution.py:31
  31.7 7.9 %collective-permute-start.6 = (f32[64,128]{1,0:T(8,128)S(1)}, f32[64,128]{1,0:T(8,128)S(1)}, u32[]{:S(2)}, u32[]{:S(2)}) collective-permute-start(f32[64,128]{1,0:T(8,128)S(1)} %get-tuple-element.57), channel_id=1, source_target_pairs={{8,16},{24,32},{40,48},{56,64},{72,80},{88,96},{104,112},{120,128}... | collective-permute-start | bytes 98312 | tf_op jit(solution)/shard_map/ppermute | solution.py:31
  32.3 7.7 %collective-permute-start.7 = (f32[64,128]{1,0:T(8,128)S(1)}, f32[64,128]{1,0:T(8,128)S(1)}, u32[]{:S(2)}, u32[]{:S(2)}) collective-permute-start(f32[64,128]{1,0:T(8,128)S(1)} %get-tuple-element.58), channel_id=1, source_target_pairs={{0,8},{16,24},{32,40},{48,56},{64,72},{80,88},{96,104},{112,120},{... | collective-permute-start | bytes 98312 | tf_op jit(solution)/shard_map/ppermute | solution.py:31
  77.0 14.1 %collective-permute-start.8 = (bf16[4,576,128]{2,1,0:T(8,128)(2,1)S(1)}, bf16[4,576,128]{2,1,0:T(8,128)(2,1)S(1)}, u32[]{:S(2)}, u32[]{:S(2)}) collective-permute-start(bf16[4,576,128]{2,1,0:T(8,128)(2,1)S(1)} %all_to_all.25.rows_ref.own_ref), channel_id=1, source_target_pairs={{0,1},{1,0},{2,3},{3,2},{4,5},{5,4},{6,7},{7,6},{8,9},{9,8},{10,11... | collective-permute-start | bytes 1769480 | tf_op jit(solution)/shard_map/ppermute | solution.py:284
  125.7 48.5 %copy-start.3 = (bf16[4,512,128]{2,1,0:T(8,128)(2,1)S(1)}, bf16[4,512,128]{2,1,0:T(8,128)(2,1)}, u32[]{:S(2)}) copy-start(bf16[4,512,128]{2,1,0:T(8,128)(2,1)} %get-tuple-element.41) | copy-start | bytes 1572868
  170.3 21.2 %all-to-all-start.4 = ((bf16[32,2,32,128]{3,2,1,0:T(8,128)(2,1)}), bf16[32,2,32,128]{3,2,1,0:T(8,128)(2,1)S(1)}, u32[]{:S(2)}, u32[]{:S(2)}) async-start(bf16[32,2,32,128]{3,2,1,0:T(8,128)(2,1)} %broadcast_in_dim.39), calls=%async_computation.4 | async-start | bytes 1048576 | tf_op jit(solution)/shard_map/all_to_all | solution.py:346
